TPU v7x, 32 devices: a whole 2x2x4 slice. The times are simulated.
32 devices in a mesh: cfg: 1, node: 32 (over z, y, x, core), pair: 1.
Axes of the slice: x: 2, y: 2, z: 4, core: 2. Of those that a mesh axis runs over, the one named last changes fastest.
Arguments:
- node_blocks: float32 [256, 2, 256, 256], P(('cfg', 'node'), None, None, 'pair'), may hold values from -1.5 to 1.5
- node_slot: int32 [256], replicated, may hold values from 0 to 255, as said below
- pair_list: int32 [128, 2], replicated, may hold values from 0 to 255, as said below
- second_list: int32 [128, 2], replicated, may hold values from 0 to 127, as said below
- targets: int32 [128], replicated, may hold values from 0 to 63, as said below
- spin_signs: int32 [128], replicated, may hold values from -1 to 1, as said below
Outputs:
- results: float32 [64, 2, 256, 256], P(('cfg', 'node'), None, None, 'pair')
Inputs may be any that keep to these rules, and one draw needn't show every extreme that they name: `node_slot`: A permutation of the slots. `pair_list`: rows b * 4 to (b + 1) * 4 - 1 form block b. The first node of a pair in block b sits at a slot of b * 8 to (b + 1) * 8 - 1. For every block b and every owner o, at most 1 pair of block b has its second node at slots o * 8 to (o + 1) * 8 - 1; one owner supplies exactly 1 such node to every block. `second_list`: rows b * 4 to (b + 1) * 4 - 1 form block b. The first pair of a product in block b lies in block b of the pairs. For every block b and owner o, at most 1 product of block b has its second pair in block o of the pairs; one owner supplies exactly 1 such pair product to every block. `targets`: products of block b target results b * 2 to (b + 1) * 2 - 1. `spin_signs`: each entry is -1 or 1.
All inputs are finite; a program needn't handle non-finite values.
Results may differ from a plain program's by a relative error of at most 0.000098.
Values sent between devices are 32-bit elements; how exact they have to be, the bound alone decides.
No kernel may reach another device: no remote copies, remote signals or barrier semaphores. Data moves between devices by JAX's collectives and lax.ppermute only.
A program may use at most 128 MiB of HBM per device.

v0:
```python
import functools

import jax
import jax.numpy as jnp
from jax import lax
from jax.experimental import pallas as pl
from jax.experimental.pallas import tpu as pltpu
from jax.sharding import PartitionSpec as P


RES_COL = 2
LANES = 128
CROSS_SHARE = 29 / 64
ANY = pl.BlockSpec(memory_space=pl.ANY)
HBM = pl.BlockSpec(memory_space=pltpu.HBM)
SMEM = pl.BlockSpec(memory_space=pltpu.SMEM)
VMEM = pl.BlockSpec(memory_space=pltpu.VMEM)
PARAMS = pltpu.CompilerParams(vmem_limit_bytes=24 * 1024 * 1024)
LARGE = pltpu.CompilerParams(vmem_limit_bytes=56 * 1024 * 1024)
CHAIN = pltpu.CompilerParams(vmem_limit_bytes=44 * 1024 * 1024)


def cut_kernel(in_ref, out_ref):
    rows = out_ref.shape[3]
    for j in range(out_ref.shape[0]):
        out_ref[j] = in_ref[:, :, j * rows : (j + 1) * rows, :]


def cut_rows(nodes, group, part, width):
    count, _, order, _ = nodes.shape
    rows = order // group
    steps = 4 if group % 4 == 0 else 1
    return pl.pallas_call(
        cut_kernel,
        grid=(steps,),
        in_specs=[pl.BlockSpec((count, 2, order // steps, width), lambda i: (0, 0, i, part))],
        out_specs=pl.BlockSpec((group // steps, count, 2, rows, width), lambda i: (i, 0, 0, 0, 0)),
        out_shape=jax.ShapeDtypeStruct((group, count, 2, rows, width), jnp.float32),
        name="cut_rows",
    )(nodes)


def plan_kernel(room, half_ref, ids_ref, send_ref, source_ref, crowded_ref, place_ref):
    half = half_ref[0]
    count = send_ref.shape[0]
    asked = source_ref.shape[0]

    def clear(i, carry):
        place_ref[i] = -1
        return carry

    def empty(i, carry):
        send_ref[i] = 0
        return carry

    lax.fori_loop(0, 2 * count, clear, 0, unroll=8)
    lax.fori_loop(0, count, empty, 0, unroll=8)

    def visit_other(q, found):
        item = ids_ref[(1 - half) * asked + q]
        here = item - half * count
        fresh = (here >= 0) & (here < count) & (place_ref[item] < 0)

        @pl.when(fresh)
        def _():
            place_ref[item] = 0
            send_ref[found] = here

        return found + fresh.astype(jnp.int32)

    def visit_own(q, found):
        item = ids_ref[half * asked + q]
        here = item - half * count
        inside = (here >= 0) & (here < count)
        known = place_ref[item]
        fresh = jnp.logical_not(inside) & (known < 0)
        there = count + room + item - (1 - half) * count
        place = jnp.where(known < 0, jnp.where(found < room, count + found, there), known)

        @pl.when(fresh)
        def _():
            place_ref[item] = place

        source_ref[q] = jnp.where(inside, here, place)
        return found + fresh.astype(jnp.int32)

    sent = lax.fori_loop(0, asked, visit_other, jnp.int32(0))
    received = lax.fori_loop(0, asked, visit_own, jnp.int32(0))
    crowded_ref[0] = (jnp.maximum(sent, received) > room).astype(jnp.int32)


def make_plan(half, ids, count, room):
    asked = ids.shape[0] // 2
    return pl.pallas_call(
        functools.partial(plan_kernel, room),
        in_specs=[SMEM] * 2,
        out_specs=[SMEM] * 3,
        out_shape=[
            jax.ShapeDtypeStruct((count,), jnp.int32),
            jax.ShapeDtypeStruct((asked,), jnp.int32),
            jax.ShapeDtypeStruct((1,), jnp.int32),
        ],
        scratch_shapes=[pltpu.SMEM((2 * count,), jnp.int32)],
        compiler_params=PARAMS,
        name="make_plan",
    )(half, ids)


def leave_kernel(send_ref, spread_ref, out_ref):
    def copy(i, carry):
        out_ref[i] = spread_ref[send_ref[i]]
        return carry

    lax.fori_loop(0, out_ref.shape[0], copy, 0, unroll=8)


def pick_leaving(send, spread, room):
    return pl.pallas_call(
        leave_kernel,
        in_specs=[SMEM, VMEM],
        out_specs=VMEM,
        out_shape=jax.ShapeDtypeStruct((room,) + spread.shape[1:], jnp.float32),
        compiler_params=PARAMS,
        name="pick_leaving",
    )(send, spread)


def collect_kernel(source_ref, crowded_ref, spread_ref, arrived_ref, extra_ref, out_ref, sem):
    count, room = spread_ref.shape[0], arrived_ref.shape[0]

    def copy(q, carry):
        source = source_ref[q]
        near = jnp.minimum(source, count - 1)
        far = jnp.clip(source - count, 0, room - 1)
        out_ref[q] = jnp.where(source < count, spread_ref[near], arrived_ref[far])
        return carry

    lax.fori_loop(0, out_ref.shape[0], copy, 0, unroll=8)

    @pl.when(crowded_ref[0] > 0)
    def _():
        def fetch(q, carry):
            source = source_ref[q] - (count + room)

            @pl.when(source >= 0)
            def _():
                slow = pltpu.make_async_copy(extra_ref.at[source], out_ref.at[q], sem)
                slow.start()
                slow.wait()

            return carry

        lax.fori_loop(0, out_ref.shape[0], fetch, 0)


def collect(source, crowded, spread, arrived, extra):
    return pl.pallas_call(
        collect_kernel,
        in_specs=[SMEM, SMEM, VMEM, VMEM, ANY],
        out_specs=VMEM,
        out_shape=jax.ShapeDtypeStruct((source.shape[0],) + spread.shape[1:], jnp.float32),
        scratch_shapes=[pltpu.SemaphoreType.DMA],
        compiler_params=PARAMS,
        name="collect",
    )(source, crowded, spread, arrived, extra)


def fetch_items(cuts, ids):
    devices = lax.axis_size("node")
    group = devices // 2
    half = (lax.axis_index("node") // group).astype(jnp.int32).reshape(1)
    halves = [[h * group + i for i in range(group)] for h in range(2)]
    swap = [(i, (i + group) % devices) for i in range(devices)]
    count = group * cuts[0].shape[1]
    room = min(count, max(8, int(count * CROSS_SHARE)))
    send, source, crowded = make_plan(half, ids.reshape(-1), count, room)

    def exchange(x):
        return lax.all_to_all(x, "node", 0, 0, axis_index_groups=halves, tiled=True)

    delivered = []
    for cut in cuts:
        spread = exchange(cut)
        spread = spread.reshape((count,) + spread.shape[2:])
        leaving = pick_leaving(send, spread, room)
        arrived = lax.ppermute(leaving, "node", swap)
        extra = lax.cond(
            crowded[0] > 0,
            lambda x: lax.ppermute(x, "node", swap),
            jnp.zeros_like,
            spread,
        )
        picked = collect(source, crowded, spread, arrived, extra)
        picked = picked.reshape((group, ids.shape[1]) + picked.shape[1:])
        delivered.append(exchange(picked))
    return delivered


def halves_of(x):
    high = x.astype(jnp.bfloat16)
    return high, (x - high.astype(jnp.float32)).astype(jnp.bfloat16)


def stacked(blocks):
    order = blocks[0].shape[0] * blocks[0].shape[2]
    real, imag = (
        jnp.concatenate([b[:, c].reshape(order, b.shape[-1]) for b in blocks], axis=1)
        for c in range(2)
    )
    pairs = zip(halves_of(real), halves_of(imag))
    return [
        jnp.concatenate([jnp.concatenate([r, i], axis=1), jnp.concatenate([-i, r], axis=1)], axis=0)
        for r, i in pairs
    ]


def product(left, blocks):
    left_high, left_low = halves_of(left)
    right_high, right_low = stacked(blocks)
    dot = functools.partial(jnp.dot, preferred_element_type=jnp.float32)
    small = dot(left_high, right_low) + dot(left_low, right_high)
    return dot(left_high, right_high) + small


def wide(ref):
    return jnp.concatenate([ref[0, 0], ref[0, 1]], axis=1)


def triple_spec(array):
    group, _, _, rows, width = array.shape
    return pl.BlockSpec((group, 3, 2, rows, width), lambda k, *scalars: (0, k, 0, 0, 0))


def multiply_kernel(which, index_ref, left_ref, *refs):
    right_refs, out_ref = refs[:-1], refs[-1]
    both = product(wide(left_ref), [ref[:, which] for ref in right_refs])
    width = out_ref.shape[-1]
    out_ref[0, 0] = both[:, :width]
    out_ref[0, 1] = both[:, width:]


def multiply(left_index, lefts, rights, which):
    order = lefts.shape[2]
    number = left_index.shape[0]
    cols = sum(right.shape[-1] for right in rights)
    return pl.pallas_call(
        functools.partial(multiply_kernel, which),
        grid_spec=pltpu.PrefetchScalarGridSpec(
            num_scalar_prefetch=1,
            grid=(number,),
            in_specs=[
                pl.BlockSpec((1, 2, order, order), lambda k, index: (index[k], 0, 0, 0)),
                *[triple_spec(right) for right in rights],
            ],
            out_specs=pl.BlockSpec((1, 2, order, cols), lambda k, index: (k, 0, 0, 0)),
        ),
        out_shape=jax.ShapeDtypeStruct((number, 2, order, cols), jnp.float32),
        compiler_params=CHAIN,
        name="multiply",
    )(left_index, lefts, *rights)


def add_result(step, target, sign, both, out_ref):
    width = out_ref.shape[-1]

    @pl.when(step == 0)
    def _():
        out_ref[...] = jnp.zeros_like(out_ref)

    both = both * sign[step].astype(jnp.float32)
    row = target[step]
    out_ref[row, 0] += both[:, :width]
    out_ref[row, 1] += both[:, width:]


def finish_kernel(target, sign, left_ref, *refs):
    right_refs, out_ref = refs[:-1], refs[-1]
    both = product(wide(left_ref), [ref[:, 2] for ref in right_refs])
    add_result(pl.program_id(0), target, sign, both, out_ref)


def finish(target, sign, lefts, rights):
    order = lefts.shape[2]
    whole = (RES_COL, 2, order, sum(right.shape[-1] for right in rights))
    return pl.pallas_call(
        finish_kernel,
        grid_spec=pltpu.PrefetchScalarGridSpec(
            num_scalar_prefetch=2,
            grid=(lefts.shape[0],),
            in_specs=[
                pl.BlockSpec((1, 2, order, order), lambda k, t, s: (k, 0, 0, 0)),
                *[triple_spec(right) for right in rights],
            ],
            out_specs=pl.BlockSpec(whole, lambda k, t, s: (0, 0, 0, 0)),
        ),
        out_shape=jax.ShapeDtypeStruct(whole, jnp.float32),
        compiler_params=LARGE,
        name="finish",
    )(target, sign, lefts, *rights)


def chain_kernel(slot, target, sign, node_ref, start_ref, *refs):
    right_refs, out_ref = refs[:-1], refs[-1]
    last = product(wide(node_ref), [right_refs[-1][:, 0]])
    width = last.shape[1] // 2
    first = jnp.concatenate(
        [start_ref[0, 0], last[:, :width], start_ref[0, 1], last[:, width:]], axis=1
    )
    longer = product(first, [ref[:, 1] for ref in right_refs])
    both = product(longer, [ref[:, 2] for ref in right_refs])
    add_result(pl.program_id(0), target, sign, both, out_ref)


def chain(slot, target, sign, nodes, start, rights):
    order = nodes.shape[2]
    whole = (RES_COL, 2, order, order)
    early = start.shape[-1]
    return pl.pallas_call(
        chain_kernel,
        grid_spec=pltpu.PrefetchScalarGridSpec(
            num_scalar_prefetch=3,
            grid=(slot.shape[0],),
            in_specs=[
                pl.BlockSpec((1, 2, order, order), lambda k, slot, t, s: (slot[k], 0, 0, 0)),
                pl.BlockSpec((1, 2, order, early), lambda k, slot, t, s: (k, 0, 0, 0)),
                *[triple_spec(right) for right in rights],
            ],
            out_specs=pl.BlockSpec(whole, lambda k, slot, t, s: (0, 0, 0, 0)),
        ),
        out_shape=jax.ShapeDtypeStruct(whole, jnp.float32),
        compiler_params=CHAIN,
        name="chain",
    )(slot, target, sign, nodes, start, *rights)


def all_columns(x):
    if lax.axis_size("pair") == 1:
        return x
    return lax.all_gather(x, "pair", axis=3, tiled=True)


def per_device(node_blocks, node_slot, pair_list, second_list, targets, spin_signs):
    devices = lax.axis_size("node")
    column = lax.axis_index("node")
    group = devices // 2
    node_col, _, _, local_width = node_blocks.shape
    second_col = second_list.shape[0] // devices
    width = min(LANES, local_width)
    cuts = [cut_rows(node_blocks, group, c, width) for c in range(local_width // width)]

    slots = node_slot[pair_list]
    slots = slots[second_list].reshape(devices, second_col, 4)
    rights = fetch_items(cuts, slots[:, :, 1:].reshape(devices, second_col * 3))

    own_slots = lax.dynamic_index_in_dim(slots[:, :, 0], column, 0, keepdims=False)
    own_slots = own_slots - column * node_col
    own_signs = lax.dynamic_slice_in_dim(spin_signs, column * second_col, second_col, 0)
    own_targets = lax.dynamic_slice_in_dim(targets, column * second_col, second_col, 0)
    own_targets = own_targets - column * RES_COL

    if lax.axis_size("pair") == 1 and len(rights) > 1:
        start = multiply(own_slots, node_blocks, rights[:-1], 0)
        return chain(own_slots, own_targets, own_signs, node_blocks, start, rights)
    same = jnp.arange(second_col, dtype=jnp.int32)
    products = multiply(own_slots, all_columns(node_blocks), rights, 0)
    longer = multiply(same, all_columns(products), rights, 1)
    return finish(own_targets, own_signs, all_columns(longer), rights)


def solution(mesh):
    placed = (P(("cfg", "node"), None, None, "pair"), P(), P(), P(), P(), P())

    return jax.shard_map(
        per_device,
        mesh=mesh,
        in_specs=placed,
        out_specs=P(("cfg", "node"), None, None, "pair"),
        check_vma=False,
    )
```

profile of v0, /device:TPU:0, one launch (start us, length us, event | category | flops | bytes accessed | tf_op | source)
XLA Modules:
  0.0 245.3 jit_solution(16782117421168517973)
XLA Ops:
  0.0 3.8 %cut_rows.2 = f32[16,8,2,16,128]{4,3,2,1,0:T(8,128)} custom-call(f32[8,2,256,256]{3,2,1,0:T(8,128)} %node_ref.1), custom_call_target="tpu_custom_call" | custom-call | tf_op jit(solution)/shard_map/cut_rows/pallas_call | solution.py:33
  3.8 6.3 %all-to-all-start = ((f32[16,8,2,16,128]{4,3,2,1,0:T(8,128)}), f32[16,8,2,16,128]{4,3,2,1,0:T(8,128)S(1)}, u32[]{:S(2)}, u32[]{:S(2)}) async-start(f32[16,8,2,16,128]{4,3,2,1,0:T(8,128)} %cut_rows.2), calls=%async_computation | async-start | bytes 4194304 | tf_op jit(solution)/shard_map/all_to_all | solution.py:179
  10.2 3.8 %cut_rows.3 = f32[16,8,2,16,128]{4,3,2,1,0:T(8,128)} custom-call(f32[8,2,256,256]{3,2,1,0:T(8,128)} %node_ref.1), custom_call_target="tpu_custom_call" | custom-call | tf_op jit(solution)/shard_map/cut_rows/pallas_call | solution.py:33
  14.0 25.2 %all-to-all-done = f32[16,8,2,16,128]{4,3,2,1,0:T(8,128)S(1)} async-done(((f32[16,8,2,16,128]{4,3,2,1,0:T(8,128)}), f32[16,8,2,16,128]{4,3,2,1,0:T(8,128)S(1)}, u32[]{:S(2)}, u32[]{:S(2)}) %all-to-all-start) | async-done | bytes 2097184 | tf_op jit(solution)/shard_map/all_to_all | solution.py:179
  39.2 5.0 %all-to-all-start.2 = ((f32[16,8,2,16,128]{4,3,2,1,0:T(8,128)}), f32[16,8,2,16,128]{4,3,2,1,0:T(8,128)}, u32[]{:S(2)}, u32[]{:S(2)}) async-start(f32[16,8,2,16,128]{4,3,2,1,0:T(8,128)} %cut_rows.3), calls=%async_computation.2 | async-start | bytes 4194304 | tf_op jit(solution)/shard_map/all_to_all | solution.py:179
  44.4 0.1 reshape.41
  44.5 1.9 gather_fusion
  46.9 0.7 gather_fusion.1
  47.8 0.2 reshape_reshape.3.ids_ref
  48.1 6.6 %make_plan.1 = (s32[128]{0:T(128)S(1)}, s32[192]{0:T(256)S(1)}, s32[1]{0:T(128)}) custom-call(s32[1]{0:T(128)} %bitcast.half_ref, s32[384]{0:T(512)S(1)} %reshape_reshape.3.ids_ref), custom_call_target="tpu_custom_call" | custom-call | tf_op jit(solution)/shard_map/make_plan/pallas_call | solution.py:94
  54.7 1.7 pick_leaving.2
  56.4 2.7 %collective-permute-start.2 = (f32[58,2,16,128]{3,2,1,0:T(8,128)S(1)}, f32[58,2,16,128]{3,2,1,0:T(8,128)S(1)}, u32[]{:S(2)}, u32[]{:S(2)}) collective-permute-start(f32[58,2,16,128]{3,2,1,0:T(8,128)S(1)} %pick_leaving.2), channel_id=1, source_target_pairs={{0,16},{1,17},{2,18},{3,19},{4,20},{5,21},{6,22},{7,23},{8,24},{9,... | collective-permute-start | bytes 2850824 | tf_op jit(solution)/shard_map/ppermute | solution.py:186
  59.6 1.7 conditional.2
  59.7 1.7 broadcast.9
  61.3 39.8 %collective-permute-done.2.arrived_ref = f32[58,2,16,128]{3,2,1,0:T(8,128)S(1)} collective-permute-done((f32[58,2,16,128]{3,2,1,0:T(8,128)S(1)}, f32[58,2,16,128]{3,2,1,0:T(8,128)S(1)}, u32[]{:S(2)}, u32[]{:S(2)}) %collective-permute-start.2) | collective-permute-done | bytes 950304 | tf_op jit(solution)/shard_map/ppermute | solution.py:186
  101.1 3.2 %collect.2 = f32[192,2,16,128]{3,2,1,0:T(8,128)S(1)} custom-call(s32[192]{0:T(256)S(1)} %get-tuple-element.16.source_ref, s32[1]{0:T(128)} %get-tuple-element.17.crowded_ref, f32[128,2,16,128]{3,2,1,0:T(8,128)} %bitcast.11, f32[58,2,16,128]{3,2,1,0:T(8,128)S(1)} %collective-permute-done.2.arrived_ref, f32[128,2,16,128]{3,2,1,0:T(8,128)} %get-tuple-element.19.extra_ref), custom_call_target="tpu_custom_call" | custom-call | tf_op jit(solution)/shard_map/collect/pallas_call | solution.py:157
  104.3 1.6 copy-done.2
  106.0 4.0 %all-to-all-start.1 = ((f32[16,12,2,16,128]{4,3,2,1,0:T(8,128)}), f32[16,12,2,16,128]{4,3,2,1,0:T(8,128)S(1)}, u32[]{:S(2)}, u32[]{:S(2)}) async-start(f32[16,12,2,16,128]{4,3,2,1,0:T(8,128)} %bitcast.7), calls=%async_computation.1 | async-start | bytes 6291456 | tf_op jit(solution)/shard_map/all_to_all | solution.py:179
  110.0 2.6 %pick_leaving.3 = f32[58,2,16,128]{3,2,1,0:T(8,128)} custom-call(s32[128]{0:T(128)S(1)} %get-tuple-element.18.send_ref, f32[128,2,16,128]{3,2,1,0:T(8,128)} %bitcast.4.spread_ref), custom_call_target="tpu_custom_call" | custom-call | tf_op jit(solution)/shard_map/pick_leaving/pallas_call | solution.py:118
  112.6 3.4 %collective-permute-start.3 = (f32[58,2,16,128]{3,2,1,0:T(8,128)}, f32[58,2,16,128]{3,2,1,0:T(8,128)}, u32[]{:S(2)}, u32[]{:S(2)}) collective-permute-start(f32[58,2,16,128]{3,2,1,0:T(8,128)} %pick_leaving.3), channel_id=1, source_target_pairs={{0,16},{1,17},{2,18},{3,19},{4,20},{5,21},{6,22},{7,23},{8,24},{9,... | collective-permute-start | bytes 2850824 | tf_op jit(solution)/shard_map/ppermute | solution.py:186
  116.0 1.6 conditional.3
  116.0 1.6 broadcast.10
  117.6 57.8 %collective-permute-done.3.arrived_ref = f32[58,2,16,128]{3,2,1,0:T(8,128)} collective-permute-done((f32[58,2,16,128]{3,2,1,0:T(8,128)}, f32[58,2,16,128]{3,2,1,0:T(8,128)}, u32[]{:S(2)}, u32[]{:S(2)}) %collective-permute-start.3) | collective-permute-done | bytes 950304 | tf_op jit(solution)/shard_map/ppermute | solution.py:186
  175.4 3.4 %collect.3 = f32[192,2,16,128]{3,2,1,0:T(8,128)S(1)} custom-call(s32[192]{0:T(256)S(1)} %get-tuple-element.16.source_ref, s32[1]{0:T(128)} %get-tuple-element.17.crowded_ref, f32[128,2,16,128]{3,2,1,0:T(8,128)} %bitcast.4.spread_ref, f32[58,2,16,128]{3,2,1,0:T(8,128)} %collective-permute-done.3.arrived_ref, f32[128,2,16,128]{3,2,1,0:T(8,128)} %get-tuple-element.20.extra_ref), custom_call_target="tpu_custom_call" | custom-call | tf_op jit(solution)/shard_map/collect/pallas_call | solution.py:157
  178.9 1.7 copy-done.3
  180.6 6.8 %all-to-all-start.3 = ((f32[16,12,2,16,128]{4,3,2,1,0:T(8,128)}), f32[16,12,2,16,128]{4,3,2,1,0:T(8,128)}, u32[]{:S(2)}, u32[]{:S(2)}) async-start(f32[16,12,2,16,128]{4,3,2,1,0:T(8,128)} %bitcast.8), calls=%async_computation.3 | async-start | bytes 6291456 | tf_op jit(solution)/shard_map/all_to_all | solution.py:179
  187.7 2.2 copy-done.1
  189.8 2.3 multiply.1.start_ref
  192.2 1.0 copy-done.4
  193.2 39.4 %all-to-all-done.3.refs_1_ = f32[16,12,2,16,128]{4,3,2,1,0:T(8,128)} async-done(((f32[16,12,2,16,128]{4,3,2,1,0:T(8,128)}), f32[16,12,2,16,128]{4,3,2,1,0:T(8,128)}, u32[]{:S(2)}, u32[]{:S(2)}) %all-to-all-start.3) | async-done | bytes 3145760 | tf_op jit(solution)/shard_map/all_to_all | solution.py:179
  232.6 1.2 copy-done.5
  233.8 11.6 %chain.1 = f32[2,2,256,256]{3,2,1,0:T(8,128)} custom-call(s32[4]{0:T(128)S(1)} %subtract_reduce_fusion.index_ref.slot, s32[4]{0:T(128)S(1)} %dynamic-slice_subtract_fusion.target, s32[4]{0:T(128)S(1)} %dynamic_slice.12.sign, f32[8,2,256,256]{3,2,1,0:T(8,128)} %node_ref.1, f32[4,2,256,128]{3,2,1,0:T(8,128)S(1)} %copy-done.5, ...), custom_call_target="tpu_custom_call" | custom-call | tf_op jit(solution)/shard_map/chain/pallas_call | solution.py:318
  (32 shorter events, 1.0 us)
Async XLA Ops:
  0.0 44.5 %copy-start = (s32[256]{0:T(256)S(1)}, s32[256]{0:T(256)}, u32[]{:S(2)}) copy-start(s32[256]{0:T(256)} %param.11) | copy-start | bytes 3076
  3.8 35.4 %all-to-all-start = ((f32[16,8,2,16,128]{4,3,2,1,0:T(8,128)}), f32[16,8,2,16,128]{4,3,2,1,0:T(8,128)S(1)}, u32[]{:S(2)}, u32[]{:S(2)}) async-start(f32[16,8,2,16,128]{4,3,2,1,0:T(8,128)} %cut_rows.2), calls=%async_computation | async-start | bytes 4194304 | tf_op jit(solution)/shard_map/all_to_all | solution.py:179
  14.0 30.2 %copy-start.7 = (s32[128,2]{0,1:T(2,128)S(1)}, s32[128,2]{0,1:T(2,128)}, u32[]{:S(2)}) copy-start(s32[128,2]{0,1:T(2,128)} %param.12) | copy-start | bytes 3076
  39.2 5.0 %copy-start.6 = (f32[16,8,2,16,128]{4,3,2,1,0:T(8,128)}, f32[16,8,2,16,128]{4,3,2,1,0:T(8,128)S(1)}, u32[]{:S(2)}) copy-start(f32[16,8,2,16,128]{4,3,2,1,0:T(8,128)S(1)} %all-to-all-done) | copy-start | bytes 6291460
  39.2 66.7 %all-to-all-start.2 = ((f32[16,8,2,16,128]{4,3,2,1,0:T(8,128)}), f32[16,8,2,16,128]{4,3,2,1,0:T(8,128)}, u32[]{:S(2)}, u32[]{:S(2)}) async-start(f32[16,8,2,16,128]{4,3,2,1,0:T(8,128)} %cut_rows.3), calls=%async_computation.2 | async-start | bytes 4194304 | tf_op jit(solution)/shard_map/all_to_all | solution.py:179
  44.5 2.1 copy-start.8
  56.4 44.7 %collective-permute-start.2 = (f32[58,2,16,128]{3,2,1,0:T(8,128)S(1)}, f32[58,2,16,128]{3,2,1,0:T(8,128)S(1)}, u32[]{:S(2)}, u32[]{:S(2)}) collective-permute-start(f32[58,2,16,128]{3,2,1,0:T(8,128)S(1)} %pick_leaving.2), channel_id=1, source_target_pairs={{0,16},{1,17},{2,18},{3,19},{4,20},{5,21},{6,22},{7,23},{8,24},{9,... | collective-permute-start | bytes 2850824 | tf_op jit(solution)/shard_map/ppermute | solution.py:186
  104.3 1.6 copy-start.2
  106.0 74.6 %all-to-all-start.1 = ((f32[16,12,2,16,128]{4,3,2,1,0:T(8,128)}), f32[16,12,2,16,128]{4,3,2,1,0:T(8,128)S(1)}, u32[]{:S(2)}, u32[]{:S(2)}) async-start(f32[16,12,2,16,128]{4,3,2,1,0:T(8,128)} %bitcast.7), calls=%async_computation.1 | async-start | bytes 6291456 | tf_op jit(solution)/shard_map/all_to_all | solution.py:179
  112.6 62.8 %collective-permute-start.3 = (f32[58,2,16,128]{3,2,1,0:T(8,128)}, f32[58,2,16,128]{3,2,1,0:T(8,128)}, u32[]{:S(2)}, u32[]{:S(2)}) collective-permute-start(f32[58,2,16,128]{3,2,1,0:T(8,128)} %pick_leaving.3), channel_id=1, source_target_pairs={{0,16},{1,17},{2,18},{3,19},{4,20},{5,21},{6,22},{7,23},{8,24},{9,... | collective-permute-start | bytes 2850824 | tf_op jit(solution)/shard_map/ppermute | solution.py:186
  178.9 1.7 copy-start.3
  180.6 6.8 %copy-start.10 = (s32[128]{0:T(128)S(1)}, s32[128]{0:T(128)}, u32[]{:S(2)}) copy-start(s32[128]{0:T(128)} %param.15) | copy-start | bytes 1540
  180.6 7.0 %copy-start.9 = (s32[128]{0:T(128)S(1)}, s32[128]{0:T(128)}, u32[]{:S(2)}) copy-start(s32[128]{0:T(128)} %param.14) | copy-start | bytes 1540
  180.6 52.0 %all-to-all-start.3 = ((f32[16,12,2,16,128]{4,3,2,1,0:T(8,128)}), f32[16,12,2,16,128]{4,3,2,1,0:T(8,128)}, u32[]{:S(2)}, u32[]{:S(2)}) async-start(f32[16,12,2,16,128]{4,3,2,1,0:T(8,128)} %bitcast.8), calls=%async_computation.3 | async-start | bytes 6291456 | tf_op jit(solution)/shard_map/all_to_all | solution.py:179
  187.7 2.2 copy-start.1
  192.2 1.0 copy-start.4
  232.6 1.2 copy-start.5
where the time goes:
time: 247 us; the launch traced here: 245 us
  waiting for transfers between devices  162 us (66%)
  Pallas kernels  39.2 us (16%)
  starting transfers between devices  28.1 us (11%)
  local copies, waits for them, and re-layouts  14.8 us (6%)
    ppermute x2, waiting for transfers between devices, fetch_items(): arrived = lax.ppermute(leaving, 'node', swap)  97.6 us
    all_to_all x4, waiting for transfers between devices, exchange(): return lax.all_to_all(x, 'node', 0, 0, axis_index_groups=halves, tiled=True)  64.6 us
    all_to_all x4, starting transfers between devices, exchange(): return lax.all_to_all(x, 'node', 0, 0, axis_index_groups=halves, tiled=True)  22.1 us
    pallas_call x1, Pallas kernels, chain(): pl.pallas_call(chain_kernel, grid_spec=pltpu.PrefetchScalarGridSpec(num_s...  11.6 us
    unnamed x22, local copies, waits for them, and re-layouts  7.69 us
    pallas_call x2, Pallas kernels, cut_rows(): pl.pallas_call(cut_kernel, grid=(steps,), in_specs=[pl.BlockSpec((count,...  7.67 us
    pallas_call x2, Pallas kernels, collect(): pl.pallas_call(collect_kernel, in_specs=[SMEM, SMEM, VMEM, VMEM, ANY], ou...  6.65 us
    pallas_call x1, Pallas kernels, make_plan(): pl.pallas_call(functools.partial(plan_kernel, room), in_specs=[SMEM] * 2,...  6.59 us
  transfers between devices with their start and end apart: 6, of which 4 were waited for; matrix products, arithmetic and copies ran while one was open for 3% of the time, Pallas kernels for 10%

commit v1 on v0

v1 whole, which is shorter than its diff:
```python
import functools

import jax
import jax.numpy as jnp
from jax import lax
from jax.experimental import pallas as pl
from jax.experimental.pallas import tpu as pltpu
from jax.sharding import PartitionSpec as P


RES_COL = 2
LANES = 128
CROSS_SHARE = 17 / 32
NEAR_SHARE = 13 / 32
PIECES = 2
PLANES = 4
SMEM = pl.BlockSpec(memory_space=pltpu.SMEM)
VMEM = pl.BlockSpec(memory_space=pltpu.VMEM)
PARAMS = pltpu.CompilerParams(vmem_limit_bytes=24 * 1024 * 1024)
CHAIN = pltpu.CompilerParams(vmem_limit_bytes=44 * 1024 * 1024)


def cut_kernel(in_ref, out_ref):
    rows = out_ref.shape[3]
    for j in range(out_ref.shape[0]):
        out_ref[j] = in_ref[:, :, j * rows : (j + 1) * rows, :]


def cut_rows(nodes, group, part, width):
    count, _, order, _ = nodes.shape
    rows = order // group
    steps = 4 if group % 4 == 0 else 1
    return pl.pallas_call(
        cut_kernel,
        grid=(steps,),
        in_specs=[pl.BlockSpec((count, 2, order // steps, width), lambda i: (0, 0, i, part))],
        out_specs=pl.BlockSpec((group // steps, count, 2, rows, width), lambda i: (i, 0, 0, 0, 0)),
        out_shape=jax.ShapeDtypeStruct((group, count, 2, rows, width), jnp.float32),
        name="cut_rows",
    )(nodes)


def plan_kernel(plane_ref, ids_ref, cross_ref, near_ref, far_ref, source_ref, mark_ref, place_ref):
    plane = plane_ref[0]
    asked = source_ref.shape[0]
    cross_room, near_room, far_room = cross_ref.shape[0], near_ref.shape[0], far_ref.shape[0]
    total = mark_ref.shape[0]
    count = total // PLANES
    half = plane // 2
    partner = plane ^ 1

    def clear(i, carry):
        mark_ref[i] = -1
        place_ref[i] = -1
        return carry

    lax.fori_loop(0, total, clear, 0, unroll=8)
    for ref in (cross_ref, near_ref, far_ref):

        def empty(i, carry, ref=ref):
            ref[i] = 0
            return carry

        lax.fori_loop(0, ref.shape[0], empty, 0)

    def enter(fresh, marks, item, found, room, ref, value):
        @pl.when(fresh)
        def _():
            marks[item] = found

        @pl.when(fresh & (found < room))
        def _():
            ref[found] = value

        return found + fresh.astype(jnp.int32)

    def to_other_half(q, found):
        item = ids_ref[(1 - half) * 2 * asked + q]
        fresh = (item // count == plane) & (mark_ref[item] < 0)
        return enter(fresh, mark_ref, item, found, cross_room, cross_ref, item - plane * count)

    lax.fori_loop(0, 2 * asked, to_other_half, jnp.int32(0))

    def from_other_half(q, found):
        item = ids_ref[half * 2 * asked + q]
        fresh = (item // count == (plane ^ 2)) & (place_ref[item] < 0)

        @pl.when(fresh)
        def _():
            place_ref[item] = found

        return found + fresh.astype(jnp.int32)

    lax.fori_loop(0, 2 * asked, from_other_half, jnp.int32(0))

    def clear_marks(i, carry):
        mark_ref[i] = -1
        return carry

    lax.fori_loop(0, total, clear_marks, 0, unroll=8)

    def to_partner(q, founds):
        near, far = founds
        item = ids_ref[partner * asked + q]
        owner = item // count
        fresh = mark_ref[item] < 0
        near = enter(
            fresh & (owner == plane), mark_ref, item, near, near_room, near_ref, item - plane * count
        )
        crossed = jnp.clip(place_ref[item], 0, cross_room - 1)
        far = enter(
            fresh & (owner == (plane ^ 2)), mark_ref, item, far, far_room, far_ref, crossed
        )
        return near, far

    lax.fori_loop(0, asked, to_partner, (jnp.int32(0), jnp.int32(0)))
    lax.fori_loop(0, total, clear_marks, 0, unroll=8)

    def own(q, founds):
        near, far = founds
        item = ids_ref[plane * asked + q]
        owner = item // count
        known = mark_ref[item]
        from_near = owner == partner
        from_far = owner == (plane ^ 3)
        found = jnp.where(from_near, near, far)
        fresh = (known < 0) & (from_near | from_far)

        @pl.when(fresh)
        def _():
            mark_ref[item] = found

        place = jnp.where(known < 0, found, known)
        source = jnp.where(
            owner == plane,
            item - plane * count,
            jnp.where(
                owner == (plane ^ 2),
                count + place_ref[item],
                count + cross_room + place + jnp.where(from_near, 0, near_room),
            ),
        )
        source_ref[q] = source
        step = fresh.astype(jnp.int32)
        return near + jnp.where(from_near, step, 0), far + jnp.where(from_far, step, 0)

    lax.fori_loop(0, asked, own, (jnp.int32(0), jnp.int32(0)))


def make_plan(plane, ids, count, rooms):
    asked = ids.shape[0] // PLANES
    return pl.pallas_call(
        plan_kernel,
        in_specs=[SMEM] * 2,
        out_specs=[SMEM] * 4,
        out_shape=[jax.ShapeDtypeStruct((n,), jnp.int32) for n in (*rooms, asked)],
        scratch_shapes=[pltpu.SMEM((PLANES * count,), jnp.int32)] * 2,
        compiler_params=PARAMS,
        name="make_plan",
    )(plane, ids)


def is_crowded(ids, count, rooms):
    items = jnp.arange(PLANES * count, dtype=jnp.int32)
    wants = (ids.reshape(PLANES, -1, 1) == items).any(axis=1)
    halves = wants.reshape(2, 2, PLANES * count).any(axis=1)
    crowded = jnp.bool_(False)
    for plane in range(PLANES):
        cross = halves[1 - plane // 2, plane * count : (plane + 1) * count]
        crowded |= jnp.sum(cross.astype(jnp.int32)) > rooms[0]
        for step, room in ((1, rooms[1]), (3, rooms[2])):
            other = plane ^ step
            wanted = wants[plane, other * count : (other + 1) * count]
            crowded |= jnp.sum(wanted.astype(jnp.int32)) > room
    return crowded


def leave_kernel(cross_ids, near_ids, spread_ref, *refs):
    cross_refs, near_ref = refs[:-1], refs[-1]
    rows = cross_refs[0].shape[2]

    def copy(i, carry):
        item = spread_ref[cross_ids[i]]
        for r, ref in enumerate(cross_refs):
            ref[i] = item[:, r * rows : (r + 1) * rows]
        return carry

    lax.fori_loop(0, cross_refs[0].shape[0], copy, 0, unroll=4)

    def copy_near(i, carry):
        near_ref[i] = spread_ref[near_ids[i]]
        return carry

    lax.fori_loop(0, near_ref.shape[0], copy_near, 0, unroll=4)


def pick_leaving(cross, near, spread):
    _, _, rows, width = spread.shape
    piece = (cross.shape[0], 2, rows // PIECES, width)
    shapes = [piece] * PIECES + [(near.shape[0],) + spread.shape[1:]]
    return pl.pallas_call(
        leave_kernel,
        in_specs=[SMEM, SMEM, VMEM],
        out_specs=[VMEM] * (PIECES + 1),
        out_shape=[jax.ShapeDtypeStruct(shape, jnp.float32) for shape in shapes],
        compiler_params=PARAMS,
        name="pick_leaving",
    )(cross, near, spread)


def pass_kernel(far_ids, crossed_ref, out_ref):
    def copy(i, carry):
        out_ref[i] = crossed_ref[far_ids[i]]
        return carry

    lax.fori_loop(0, out_ref.shape[0], copy, 0, unroll=4)


def pick_passing(far, crossed):
    return pl.pallas_call(
        pass_kernel,
        in_specs=[SMEM, VMEM],
        out_specs=VMEM,
        out_shape=jax.ShapeDtypeStruct((far.shape[0],) + crossed.shape[1:], jnp.float32),
        compiler_params=PARAMS,
        name="pick_passing",
    )(far, crossed)


def collect_kernel(first_row, source_ref, spread_ref, crossed_ref, near_ref, far_ref, out_ref):
    rows = out_ref.shape[2]
    piece = slice(first_row, first_row + rows)
    bases = [0]
    for ref in (spread_ref, crossed_ref, near_ref):
        bases.append(bases[-1] + ref.shape[0])

    def copy(q, carry):
        source = source_ref[q]

        def index(place, ref):
            return jnp.clip(source - bases[place], 0, ref.shape[0] - 1)

        value = spread_ref[index(0, spread_ref), :, piece, :]
        value = jnp.where(source < bases[1], value, crossed_ref[index(1, crossed_ref)])
        value = jnp.where(source < bases[2], value, near_ref[index(2, near_ref), :, piece, :])
        out_ref[q] = jnp.where(source < bases[3], value, far_ref[index(3, far_ref)])
        return carry

    lax.fori_loop(0, out_ref.shape[0], copy, 0, unroll=4)


def collect(source, spread, crossed, near, far, piece):
    rows = crossed.shape[2]
    return pl.pallas_call(
        functools.partial(collect_kernel, piece * rows),
        in_specs=[SMEM] + [VMEM] * 4,
        out_specs=VMEM,
        out_shape=jax.ShapeDtypeStruct((source.shape[0],) + crossed.shape[1:], jnp.float32),
        compiler_params=PARAMS,
        name="collect",
    )(source, spread, crossed, near, far)


def fetch_items(cuts, ids):
    devices = lax.axis_size("node")
    group = devices // PLANES
    plane = (lax.axis_index("node") // group).astype(jnp.int32)
    planes = [[p * group + i for i in range(group)] for p in range(PLANES)]
    swap = [(i, (i // group ^ 2) * group + i % group) for i in range(devices)]
    mate = [(i, (i // group ^ 1) * group + i % group) for i in range(devices)]
    count = group * cuts[0].shape[1]
    rooms = tuple(
        min(count, max(8, int(count * share))) for share in (CROSS_SHARE, NEAR_SHARE, NEAR_SHARE)
    )
    flat = ids.reshape(-1)
    cross, near, far, source = make_plan(plane.reshape(1), flat, count, rooms)
    crowded = is_crowded(flat, count, rooms)
    own_ids = lax.dynamic_index_in_dim(ids.reshape(PLANES, -1), plane, 0, keepdims=False)

    def exchange(x):
        return lax.all_to_all(x, "node", 0, 0, axis_index_groups=planes, tiled=True)

    def gather_all(spread, crossed, near_by, far_by, piece):
        rows = crossed.shape[2]
        here = spread[:, :, piece * rows : (piece + 1) * rows]
        crossing = lax.ppermute(here, "node", swap)
        both = jnp.concatenate([here, crossing])
        every = jnp.concatenate([both, lax.ppermute(both, "node", mate)])
        order = own_ids // count ^ plane
        index = jnp.array([0, 2, 1, 3])[order] * count + own_ids % count
        return jnp.take(every, index, axis=0)

    delivered = []
    for cut in cuts:
        spread = exchange(cut)
        spread = spread.reshape((count,) + spread.shape[2:])
        *leaving, staying = pick_leaving(cross, near, spread)
        crossed = []
        for r in range(PIECES):
            crossed.append(lax.ppermute(leaving[r], "node", swap))
        near_by = lax.ppermute(staying, "node", mate)
        pieces = []
        for r in range(PIECES):
            passing = pick_passing(far, crossed[r])
            far_by = lax.ppermute(passing, "node", mate)
            picked = lax.cond(
                crowded,
                functools.partial(gather_all, piece=r),
                functools.partial(collect, source, piece=r),
                spread,
                crossed[r],
                near_by,
                far_by,
            )
            picked = picked.reshape((group, ids.shape[1]) + picked.shape[1:])
            pieces.append(exchange(picked))
        delivered.append(pieces)
    return delivered


def halves_of(x):
    high = x.astype(jnp.bfloat16)
    return high, (x - high.astype(jnp.float32)).astype(jnp.bfloat16)


def joined(pieces):
    rows = jnp.concatenate([p[:, None] for p in pieces], axis=1)
    return rows.reshape(-1, rows.shape[-1])


def stacked(blocks):
    real, imag = (
        jnp.concatenate([joined([piece[:, c] for piece in block]) for block in blocks], axis=1)
        for c in range(2)
    )
    pairs = zip(halves_of(real), halves_of(imag))
    return [
        jnp.concatenate([jnp.concatenate([r, i], axis=1), jnp.concatenate([-i, r], axis=1)], axis=0)
        for r, i in pairs
    ]


def product(left, blocks):
    left_high, left_low = halves_of(left)
    right_high, right_low = stacked(blocks)
    dot = functools.partial(jnp.dot, preferred_element_type=jnp.float32)
    small = dot(left_high, right_low) + dot(left_low, right_high)
    return dot(left_high, right_high) + small


def columns_of(rights):
    return sum(right.shape[-1] for right in rights) // PIECES


def wide(ref):
    return jnp.concatenate([ref[0, 0], ref[0, 1]], axis=1)


def triple_spec(array):
    group, _, _, rows, width = array.shape
    return pl.BlockSpec((group, 3, 2, rows, width), lambda k, *scalars: (0, k, 0, 0, 0))


def items(refs, which):
    pieces = [ref[:, which] for ref in refs]
    return [pieces[i : i + PIECES] for i in range(0, len(pieces), PIECES)]


def multiply_kernel(which, index_ref, left_ref, *refs):
    right_refs, out_ref = refs[:-1], refs[-1]
    both = product(wide(left_ref), items(right_refs, which))
    width = out_ref.shape[-1]
    out_ref[0, 0] = both[:, :width]
    out_ref[0, 1] = both[:, width:]


def multiply(left_index, lefts, rights, which):
    order = lefts.shape[2]
    number = left_index.shape[0]
    cols = columns_of(rights)
    return pl.pallas_call(
        functools.partial(multiply_kernel, which),
        grid_spec=pltpu.PrefetchScalarGridSpec(
            num_scalar_prefetch=1,
            grid=(number,),
            in_specs=[
                pl.BlockSpec((1, 2, order, order), lambda k, index: (index[k], 0, 0, 0)),
                *[triple_spec(right) for right in rights],
            ],
            out_specs=pl.BlockSpec((1, 2, order, cols), lambda k, index: (k, 0, 0, 0)),
        ),
        out_shape=jax.ShapeDtypeStruct((number, 2, order, cols), jnp.float32),
        compiler_params=CHAIN,
        name="multiply",
    )(left_index, lefts, *rights)


def add_result(step, target, sign, both, out_ref):
    width = out_ref.shape[-1]

    @pl.when(step == 0)
    def _():
        out_ref[...] = jnp.zeros_like(out_ref)

    both = both * sign[step].astype(jnp.float32)
    row = target[step]
    out_ref[row, 0] += both[:, :width]
    out_ref[row, 1] += both[:, width:]


def finish_kernel(target, sign, left_ref, *refs):
    right_refs, out_ref = refs[:-1], refs[-1]
    both = product(wide(left_ref), items(right_refs, 2))
    add_result(pl.program_id(0), target, sign, both, out_ref)


def finish(target, sign, lefts, rights):
    order = lefts.shape[2]
    whole = (RES_COL, 2, order, columns_of(rights))
    return pl.pallas_call(
        finish_kernel,
        grid_spec=pltpu.PrefetchScalarGridSpec(
            num_scalar_prefetch=2,
            grid=(lefts.shape[0],),
            in_specs=[
                pl.BlockSpec((1, 2, order, order), lambda k, t, s: (k, 0, 0, 0)),
                *[triple_spec(right) for right in rights],
            ],
            out_specs=pl.BlockSpec(whole, lambda k, t, s: (0, 0, 0, 0)),
        ),
        out_shape=jax.ShapeDtypeStruct(whole, jnp.float32),
        compiler_params=CHAIN,
        name="finish",
    )(target, sign, lefts, *rights)


def chain_kernel(slot, target, sign, node_ref, start_ref, *refs):
    right_refs, out_ref = refs[:-1], refs[-1]
    last = product(wide(node_ref), items(right_refs[-PIECES:], 0))
    width = last.shape[1] // 2
    first = jnp.concatenate(
        [start_ref[0, 0], last[:, :width], start_ref[0, 1], last[:, width:]], axis=1
    )
    longer = product(first, items(right_refs, 1))
    both = product(longer, items(right_refs, 2))
    add_result(pl.program_id(0), target, sign, both, out_ref)


def chain(slot, target, sign, nodes, start, rights):
    order = nodes.shape[2]
    whole = (RES_COL, 2, order, order)
    early = start.shape[-1]
    return pl.pallas_call(
        chain_kernel,
        grid_spec=pltpu.PrefetchScalarGridSpec(
            num_scalar_prefetch=3,
            grid=(slot.shape[0],),
            in_specs=[
                pl.BlockSpec((1, 2, order, order), lambda k, slot, t, s: (slot[k], 0, 0, 0)),
                pl.BlockSpec((1, 2, order, early), lambda k, slot, t, s: (k, 0, 0, 0)),
                *[triple_spec(right) for right in rights],
            ],
            out_specs=pl.BlockSpec(whole, lambda k, slot, t, s: (0, 0, 0, 0)),
        ),
        out_shape=jax.ShapeDtypeStruct(whole, jnp.float32),
        compiler_params=CHAIN,
        name="chain",
    )(slot, target, sign, nodes, start, *rights)


def all_columns(x):
    if lax.axis_size("pair") == 1:
        return x
    return lax.all_gather(x, "pair", axis=3, tiled=True)


def per_device(node_blocks, node_slot, pair_list, second_list, targets, spin_signs):
    devices = lax.axis_size("node")
    column = lax.axis_index("node")
    group = devices // PLANES
    node_col, _, _, local_width = node_blocks.shape
    second_col = second_list.shape[0] // devices
    width = min(LANES, local_width)
    cuts = [cut_rows(node_blocks, group, c, width) for c in range(local_width // width)]

    slots = node_slot[pair_list]
    slots = slots[second_list].reshape(devices, second_col, 4)
    rights = fetch_items(cuts, slots[:, :, 1:].reshape(devices, second_col * 3))

    own_slots = lax.dynamic_index_in_dim(slots[:, :, 0], column, 0, keepdims=False)
    own_slots = own_slots - column * node_col
    own_signs = lax.dynamic_slice_in_dim(spin_signs, column * second_col, second_col, 0)
    own_targets = lax.dynamic_slice_in_dim(targets, column * second_col, second_col, 0)
    own_targets = own_targets - column * RES_COL

    parts = len(rights)
    rights = [piece for pieces in rights for piece in pieces]
    if lax.axis_size("pair") == 1 and parts > 1:
        start = multiply(own_slots, node_blocks, rights[:-PIECES], 0)
        return chain(own_slots, own_targets, own_signs, node_blocks, start, rights)
    same = jnp.arange(second_col, dtype=jnp.int32)
    products = multiply(own_slots, all_columns(node_blocks), rights, 0)
    longer = multiply(same, all_columns(products), rights, 1)
    return finish(own_targets, own_signs, all_columns(longer), rights)


def solution(mesh):
    placed = (P(("cfg", "node"), None, None, "pair"), P(), P(), P(), P(), P())

    return jax.shard_map(
        per_device,
        mesh=mesh,
        in_specs=placed,
        out_specs=P(("cfg", "node"), None, None, "pair"),
        check_vma=False,
    )
```

time: 247 us -> 298 us (1.21)
  waiting for transfers between devices: 162 us -> 181 us
  Pallas kernels: 39.2 us -> 54.3 us
  starting transfers between devices: 28.1 us -> 36.2 us
  between operations: 0.83 us -> 7.95 us
    ppermute x2 -> x10, waiting for transfers between devices: 97.6 us -> 143 us  [the longest x4 101 us: fetch_items(): crossed.append(lax.ppermute(leaving[r], 'node', swap))]
    all_to_all x4 -> x6, waiting for transfers between devices: 64.6 us -> 37.3 us  [exchange(): return lax.all_to_all(x, 'node', 0, 0, axis_index_groups=planes, tiled=True)]
    pallas_call x5 -> x11, Pallas kernels: 17.6 us -> 32.7 us  [the longest x4 14.5 us: collect(): pl.pallas_call(functools.partial(collect_kernel, piece * rows), in_specs=...]
    ppermute x2 -> x10, starting transfers between devices: 6.03 us -> 10.8 us  [the longest x4 6.71 us: fetch_items(): crossed.append(lax.ppermute(leaving[r], 'node', swap))]
    all_to_all x4 -> x6, starting transfers between devices: 22.1 us -> 25.4 us  [exchange(): return lax.all_to_all(x, 'node', 0, 0, axis_index_groups=planes, tiled=True)]
    another operation x3 -> x1, local copies, waits for them, and re-layouts: 3.49 us -> 0.21 us  [fetch_items(): flat = ids.reshape(-1)]
    unnamed x22 -> x34, local copies, waits for them, and re-layouts: 7.69 us -> 8.99 us
  transfers between devices with their start and end apart: 6 -> 16, of which waited for: 4 -> 11; matrix products, arithmetic and copies ran while one was open for 3% -> 3% of each run, Pallas kernels for 10% -> 13%
where the time goes in v1:
time: 298 us; the launch traced here: 296 us
  waiting for transfers between devices  181 us (61%)
  Pallas kernels  54.3 us (18%)
  starting transfers between devices  36.2 us (12%)
  local copies, waits for them, and re-layouts  14.7 us (5%)
  between operations  7.95 us (3%)
    ppermute x4, waiting for transfers between devices, fetch_items(): crossed.append(lax.ppermute(leaving[r], 'node', swap))  101 us
    all_to_all x6, waiting for transfers between devices, exchange(): return lax.all_to_all(x, 'node', 0, 0, axis_index_groups=planes, tiled=True)  37.3 us
    ppermute x4, waiting for transfers between devices, fetch_items(): far_by = lax.ppermute(passing, 'node', mate)  37.1 us
    all_to_all x6, starting transfers between devices, exchange(): return lax.all_to_all(x, 'node', 0, 0, axis_index_groups=planes, tiled=True)  25.4 us
    pallas_call x4, Pallas kernels, collect(): pl.pallas_call(functools.partial(collect_kernel, piece * rows), in_specs=...  14.5 us
    pallas_call x1, Pallas kernels, make_plan(): pl.pallas_call(plan_kernel, in_specs=[SMEM] * 2, out_specs=[SMEM] * 4, ou...  12.7 us
    pallas_call x1, Pallas kernels, chain(): pl.pallas_call(chain_kernel, grid_spec=pltpu.PrefetchScalarGridSpec(num_s...  11.5 us
    unnamed x34, local copies, waits for them, and re-layouts  8.99 us
  transfers between devices with their start and end apart: 16, of which 11 were waited for; matrix products, arithmetic and copies ran while one was open for 3% of the time, Pallas kernels for 13%

profile of v1, /device:TPU:0, one launch (start us, length us, event | category | flops | bytes accessed | tf_op | source)
XLA Modules:
  0.0 296.5 jit_solution(16533930882032434888)
XLA Ops:
  0.0 3.8 %cut_rows.3 = f32[8,8,2,32,128]{4,3,2,1,0:T(8,128)} custom-call(f32[8,2,256,256]{3,2,1,0:T(8,128)} %node_ref.1), custom_call_target="tpu_custom_call" | custom-call | tf_op jit(solution)/shard_map/cut_rows/pallas_call | solution.py:33
  3.8 5.2 %all-to-all-start.3 = ((f32[8,8,2,32,128]{4,3,2,1,0:T(8,128)}), f32[8,8,2,32,128]{4,3,2,1,0:T(8,128)S(1)}, u32[]{:S(2)}, u32[]{:S(2)}) async-start(f32[8,8,2,32,128]{4,3,2,1,0:T(8,128)} %cut_rows.3), calls=%async_computation.3 | async-start | bytes 4194304 | tf_op jit(solution)/shard_map/all_to_all | solution.py:281
  9.0 3.8 %cut_rows.2 = f32[8,8,2,32,128]{4,3,2,1,0:T(8,128)} custom-call(f32[8,2,256,256]{3,2,1,0:T(8,128)} %node_ref.1), custom_call_target="tpu_custom_call" | custom-call | tf_op jit(solution)/shard_map/cut_rows/pallas_call | solution.py:33
  12.9 22.8 %all-to-all-done.3 = f32[8,8,2,32,128]{4,3,2,1,0:T(8,128)S(1)} async-done(((f32[8,8,2,32,128]{4,3,2,1,0:T(8,128)}), f32[8,8,2,32,128]{4,3,2,1,0:T(8,128)S(1)}, u32[]{:S(2)}, u32[]{:S(2)}) %all-to-all-start.3) | async-done | bytes 2097184 | tf_op jit(solution)/shard_map/all_to_all | solution.py:281
  35.7 4.3 %all-to-all-start = ((f32[8,8,2,32,128]{4,3,2,1,0:T(8,128)}), f32[8,8,2,32,128]{4,3,2,1,0:T(8,128)}, u32[]{:S(2)}, u32[]{:S(2)}) async-start(f32[8,8,2,32,128]{4,3,2,1,0:T(8,128)} %cut_rows.2), calls=%async_computation | async-start | bytes 4194304 | tf_op jit(solution)/shard_map/all_to_all | solution.py:281
  43.9 12.7 %make_plan.1 = (s32[34]{0:T(128)S(1)}, s32[26]{0:T(128)S(1)}, s32[26]{0:T(128)S(1)}, s32[96]{0:T(128)S(1)}) custom-call(s32[1]{0:T(128)} %bitcast.16.plane_ref, s32[384]{0:T(512)S(1)} %reshape_reshape.4.ids_ref), custom_call_target="tpu_custom_call" | custom-call | tf_op jit(solution)/shard_map/make_plan/pallas_call | solution.py:152
  58.2 2.6 collective-permute-start.16
  63.3 22.8 %collective-permute-done.16.crossed_ref = f32[34,2,16,128]{3,2,1,0:T(8,128)} collective-permute-done((f32[34,2,16,128]{3,2,1,0:T(8,128)S(1)}, f32[34,2,16,128]{3,2,1,0:T(8,128)}, u32[]{:S(2)}, u32[]{:S(2)}) %collective-permute-start.16) | collective-permute-done | bytes 557088 | tf_op jit(solution)/shard_map/ppermute | solution.py:300
  97.3 4.5 %collective-permute-done.17 = f32[26,2,16,128]{3,2,1,0:T(8,128)} collective-permute-done((f32[26,2,16,128]{3,2,1,0:T(8,128)S(1)}, f32[26,2,16,128]{3,2,1,0:T(8,128)}, u32[]{:S(2)}, u32[]{:S(2)}) %collective-permute-start.17) | collective-permute-done | bytes 426016 | tf_op jit(solution)/shard_map/ppermute | solution.py:305
  101.8 3.7 %conditional.7 = (f32[96,2,16,128]{3,2,1,0:T(8,128)}) conditional(s32[]{:T(128)} %convert_element_type.66, (s32[96]{0:T(128)S(1)}, f32[64,2,32,128]{3,2,1,0:T(8,128)S(1)}, f32[34,2,16,128]{3,2,1,0:T(8,128)}, f32[26,2,32,128]{3,2,1,0:T(8,128)}, f32[26,2,16,128]{3,2,1,0:T(8,128)}) %tuple.73, (f32[64,2,32,128]{3,2,1,0:T(8,128)S(1)}, ...), branch_computations={%region_20.22_spmd, %region_21.23_spmd} | conditional | flops 3019232 | bytes 33560396 | solution.py:306
  101.8 3.7 %collect.7 = f32[96,2,16,128]{3,2,1,0:T(8,128)} custom-call(s32[96]{0:T(128)S(1)} %get-tuple-element.117.source_ref, f32[64,2,32,128]{3,2,1,0:T(8,128)S(1)} %get-tuple-element.118.spread_ref, f32[34,2,16,128]{3,2,1,0:T(8,128)} %get-tuple-element.119.crossed_ref, f32[26,2,32,128]{3,2,1,0:T(8,128)} %get-tuple-element.120.near_ref, ...), custom_call_target="tpu_custom_call" | custom-call | tf_op jit(solution)/shard_map/cond/branch_0_fun/collect/pallas_call | solution.py:254
  105.5 3.8 %all-to-all-start.5 = ((f32[8,12,2,16,128]{4,3,2,1,0:T(8,128)}), f32[8,12,2,16,128]{4,3,2,1,0:T(8,128)S(1)}, u32[]{:S(2)}, u32[]{:S(2)}) async-start(f32[8,12,2,16,128]{4,3,2,1,0:T(8,128)} %bitcast.31), calls=%async_computation.5 | async-start | bytes 3145728 | tf_op jit(solution)/shard_map/all_to_all | solution.py:281
  114.2 24.9 %collective-permute-done.11.crossed_ref = f32[34,2,16,128]{3,2,1,0:T(8,128)S(1)} collective-permute-done((f32[34,2,16,128]{3,2,1,0:T(8,128)S(1)}, f32[34,2,16,128]{3,2,1,0:T(8,128)S(1)}, u32[]{:S(2)}, u32[]{:S(2)}) %collective-permute-start.11) | collective-permute-done | bytes 557088 | tf_op jit(solution)/shard_map/ppermute | solution.py:300
  139.9 5.6 %collective-permute-done.9 = f32[26,2,32,128]{3,2,1,0:T(8,128)S(1)} collective-permute-done((f32[26,2,32,128]{3,2,1,0:T(8,128)S(1)}, f32[26,2,32,128]{3,2,1,0:T(8,128)S(1)}, u32[]{:S(2)}, u32[]{:S(2)}) %collective-permute-start.9) | collective-permute-done | bytes 852000 | tf_op jit(solution)/shard_map/ppermute | solution.py:301
  145.5 9.1 %collective-permute-done.12 = f32[26,2,16,128]{3,2,1,0:T(8,128)S(1)} collective-permute-done((f32[26,2,16,128]{3,2,1,0:T(8,128)S(1)}, f32[26,2,16,128]{3,2,1,0:T(8,128)S(1)}, u32[]{:S(2)}, u32[]{:S(2)}) %collective-permute-start.12) | collective-permute-done | bytes 426016 | tf_op jit(solution)/shard_map/ppermute | solution.py:305
  154.5 3.8 %conditional.5 = (f32[96,2,16,128]{3,2,1,0:T(8,128)}) conditional(s32[]{:T(128)} %convert_element_type.66, (s32[96]{0:T(128)S(1)}, f32[64,2,32,128]{3,2,1,0:T(8,128)}, f32[34,2,16,128]{3,2,1,0:T(8,128)S(1)}, f32[26,2,32,128]{3,2,1,0:T(8,128)S(1)}, f32[26,2,16,128]{3,2,1,0:T(8,128)S(1)}) %tuple.32, (f32[64,2,32,128]{3,2,1,0:T(8,128)}, ...), branch_computations={%region_16.18_spmd, %region_17.19_spmd} | conditional | flops 3019232 | bytes 33560396 | solution.py:306
  154.5 3.8 %collect.5 = f32[96,2,16,128]{3,2,1,0:T(8,128)} custom-call(s32[96]{0:T(128)S(1)} %get-tuple-element.99.source_ref, f32[64,2,32,128]{3,2,1,0:T(8,128)} %get-tuple-element.100.spread_ref, f32[34,2,16,128]{3,2,1,0:T(8,128)S(1)} %get-tuple-element.101.crossed_ref, f32[26,2,32,128]{3,2,1,0:T(8,128)S(1)} %get-tuple-element.102.near_ref, ...), custom_call_target="tpu_custom_call" | custom-call | tf_op jit(solution)/shard_map/cond/branch_0_fun/collect/pallas_call | solution.py:254
  159.5 3.8 %all-to-all-start.2 = ((f32[8,12,2,16,128]{4,3,2,1,0:T(8,128)}), f32[8,12,2,16,128]{4,3,2,1,0:T(8,128)S(1)}, u32[]{:S(2)}, u32[]{:S(2)}) async-start(f32[8,12,2,16,128]{4,3,2,1,0:T(8,128)} %bitcast.32), calls=%async_computation.2 | async-start | bytes 3145728 | tf_op jit(solution)/shard_map/all_to_all | solution.py:281
  164.8 26.4 %collective-permute-done.8.crossed_ref = f32[34,2,16,128]{3,2,1,0:T(8,128)S(1)} collective-permute-done((f32[34,2,16,128]{3,2,1,0:T(8,128)S(1)}, f32[34,2,16,128]{3,2,1,0:T(8,128)S(1)}, u32[]{:S(2)}, u32[]{:S(2)}) %collective-permute-start.8) | collective-permute-done | bytes 557088 | tf_op jit(solution)/shard_map/ppermute | solution.py:300
  191.9 11.8 %collective-permute-done.10 = f32[26,2,16,128]{3,2,1,0:T(8,128)S(1)} collective-permute-done((f32[26,2,16,128]{3,2,1,0:T(8,128)S(1)}, f32[26,2,16,128]{3,2,1,0:T(8,128)S(1)}, u32[]{:S(2)}, u32[]{:S(2)}) %collective-permute-start.10) | collective-permute-done | bytes 426016 | tf_op jit(solution)/shard_map/ppermute | solution.py:305
  203.7 3.8 %conditional.4 = (f32[96,2,16,128]{3,2,1,0:T(8,128)S(1)}) conditional(s32[]{:T(128)} %convert_element_type.66, (s32[96]{0:T(128)S(1)}, f32[64,2,32,128]{3,2,1,0:T(8,128)}, f32[34,2,16,128]{3,2,1,0:T(8,128)S(1)}, f32[26,2,32,128]{3,2,1,0:T(8,128)S(1)}, f32[26,2,16,128]{3,2,1,0:T(8,128)S(1)}) %tuple.30, (f32[64,2,32,128]{3,2,1,0:T(8,128)}, ...), branch_computations={%region_14.15_spmd, %region_15.17_spmd} | conditional | flops 3019232 | bytes 33560396 | solution.py:306
  204.6 2.9 collect.4
  208.7 3.8 %all-to-all-start.1 = ((f32[8,12,2,16,128]{4,3,2,1,0:T(8,128)}), f32[8,12,2,16,128]{4,3,2,1,0:T(8,128)S(1)}, u32[]{:S(2)}, u32[]{:S(2)}) async-start(f32[8,12,2,16,128]{4,3,2,1,0:T(8,128)} %bitcast.33), calls=%async_computation.1 | async-start | bytes 3145728 | tf_op jit(solution)/shard_map/all_to_all | solution.py:281
  213.7 26.6 %collective-permute-done.13.crossed_ref = f32[34,2,16,128]{3,2,1,0:T(8,128)S(1)} collective-permute-done((f32[34,2,16,128]{3,2,1,0:T(8,128)}, f32[34,2,16,128]{3,2,1,0:T(8,128)S(1)}, u32[]{:S(2)}, u32[]{:S(2)}) %collective-permute-start.13) | collective-permute-done | bytes 557088 | tf_op jit(solution)/shard_map/ppermute | solution.py:300
  241.0 11.8 %collective-permute-done.15 = f32[26,2,16,128]{3,2,1,0:T(8,128)S(1)} collective-permute-done((f32[26,2,16,128]{3,2,1,0:T(8,128)S(1)}, f32[26,2,16,128]{3,2,1,0:T(8,128)S(1)}, u32[]{:S(2)}, u32[]{:S(2)}) %collective-permute-start.15) | collective-permute-done | bytes 426016 | tf_op jit(solution)/shard_map/ppermute | solution.py:305
  252.8 4.1 %conditional.6 = (f32[96,2,16,128]{3,2,1,0:T(8,128)}) conditional(s32[]{:T(128)} %convert_element_type.66, (s32[96]{0:T(128)S(1)}, f32[64,2,32,128]{3,2,1,0:T(8,128)}, f32[34,2,16,128]{3,2,1,0:T(8,128)S(1)}, f32[26,2,32,128]{3,2,1,0:T(8,128)}, f32[26,2,16,128]{3,2,1,0:T(8,128)S(1)}) %tuple.74, (f32[64,2,32,128]{3,2,1,0:T(8,128)}, ...), branch_computations={%region_18.20_spmd, %region_19.21_spmd} | conditional | flops 3019232 | bytes 33560396 | solution.py:306
  252.8 4.1 %collect.6 = f32[96,2,16,128]{3,2,1,0:T(8,128)} custom-call(s32[96]{0:T(128)S(1)} %get-tuple-element.108.source_ref, f32[64,2,32,128]{3,2,1,0:T(8,128)} %get-tuple-element.109.spread_ref, f32[34,2,16,128]{3,2,1,0:T(8,128)S(1)} %get-tuple-element.110.crossed_ref, f32[26,2,32,128]{3,2,1,0:T(8,128)} %get-tuple-element.111.near_ref, ...), custom_call_target="tpu_custom_call" | custom-call | tf_op jit(solution)/shard_map/cond/branch_0_fun/collect/pallas_call | solution.py:254
  256.9 4.4 %all-to-all-start.4 = ((f32[8,12,2,16,128]{4,3,2,1,0:T(8,128)}), f32[8,12,2,16,128]{4,3,2,1,0:T(8,128)}, u32[]{:S(2)}, u32[]{:S(2)}) async-start(f32[8,12,2,16,128]{4,3,2,1,0:T(8,128)} %bitcast.34), calls=%async_computation.4 | async-start | bytes 3145728 | tf_op jit(solution)/shard_map/all_to_all | solution.py:281
  262.3 2.2 copy-done.2
  264.5 2.4 multiply.1.start_ref
  267.8 14.5 %all-to-all-done.4.refs_2_ = f32[8,12,2,16,128]{4,3,2,1,0:T(8,128)} async-done(((f32[8,12,2,16,128]{4,3,2,1,0:T(8,128)}), f32[8,12,2,16,128]{4,3,2,1,0:T(8,128)}, u32[]{:S(2)}, u32[]{:S(2)}) %all-to-all-start.4) | async-done | bytes 1572896 | tf_op jit(solution)/shard_map/all_to_all | solution.py:281
  285.0 11.5 %chain.1 = f32[2,2,256,256]{3,2,1,0:T(8,128)} custom-call(s32[4]{0:T(128)S(1)} %subtract_reduce_fusion.index_ref.slot, s32[4]{0:T(128)S(1)} %dynamic-slice_subtract_fusion.target, s32[4]{0:T(128)S(1)} %dynamic_slice.16.sign, f32[8,2,256,256]{3,2,1,0:T(8,128)} %node_ref.1, f32[4,2,256,128]{3,2,1,0:T(8,128)S(1)} %copy-done.6, ...), custom_call_target="tpu_custom_call" | custom-call | tf_op jit(solution)/shard_map/chain/pallas_call | solution.py:453
  (79 shorter events, 28.9 us)
Async XLA Ops:
  0.0 40.3 %copy-start = (s32[256]{0:T(256)S(1)}, s32[256]{0:T(256)}, u32[]{:S(2)}) copy-start(s32[256]{0:T(256)} %param.21) | copy-start | bytes 3076
  3.8 31.8 %all-to-all-start.3 = ((f32[8,8,2,32,128]{4,3,2,1,0:T(8,128)}), f32[8,8,2,32,128]{4,3,2,1,0:T(8,128)S(1)}, u32[]{:S(2)}, u32[]{:S(2)}) async-start(f32[8,8,2,32,128]{4,3,2,1,0:T(8,128)} %cut_rows.3), calls=%async_computation.3 | async-start | bytes 4194304 | tf_op jit(solution)/shard_map/all_to_all | solution.py:281
  12.9 27.1 %copy-start.14 = (s32[128,2]{0,1:T(2,128)S(1)}, s32[128,2]{0,1:T(2,128)}, u32[]{:S(2)}) copy-start(s32[128,2]{0,1:T(2,128)} %param.22) | copy-start | bytes 3076
  35.6 66.1 %copy-start.8 = (f32[8,8,2,32,128]{4,3,2,1,0:T(8,128)}, f32[8,8,2,32,128]{4,3,2,1,0:T(8,128)S(1)}, u32[]{:S(2)}) copy-start(f32[8,8,2,32,128]{4,3,2,1,0:T(8,128)S(1)} %all-to-all-done.3) | copy-start | bytes 6291460
  35.7 69.8 %all-to-all-start = ((f32[8,8,2,32,128]{4,3,2,1,0:T(8,128)}), f32[8,8,2,32,128]{4,3,2,1,0:T(8,128)}, u32[]{:S(2)}, u32[]{:S(2)}) async-start(f32[8,8,2,32,128]{4,3,2,1,0:T(8,128)} %cut_rows.2), calls=%async_computation | async-start | bytes 4194304 | tf_op jit(solution)/shard_map/all_to_all | solution.py:281
  40.3 2.1 copy-start.15
  43.4 58.3 %copy-start.13 = (s32[4]{0:T(128)S(1)}, s32[4]{0:T(128)}, u32[]{:S(2)}) copy-start(s32[4]{0:T(128)} %constant.173.clone) | copy-start | bytes 52
  43.5 13.1 %copy-start.12 = (s32[32,4,4]{2,1,0:T(4,128)}, s32[32,4,4]{2,1,0:T(4,128)S(1)}, u32[]{:S(2)}) copy-start(s32[32,4,4]{2,1,0:T(4,128)S(1)} %reshape.49) | copy-start | bytes 6148
  43.7 13.0 %copy-start.11 = (s32[32,4,3]{2,1,0:T(4,128)}, s32[32,4,3]{2,1,0:T(4,128)S(1)}, u32[]{:S(2)}) copy-start(s32[32,4,3]{2,1,0:T(4,128)S(1)} %slice.101) | copy-start | bytes 4612
  58.2 27.9 %collective-permute-start.16 = (f32[34,2,16,128]{3,2,1,0:T(8,128)S(1)}, f32[34,2,16,128]{3,2,1,0:T(8,128)}, u32[]{:S(2)}, u32[]{:S(2)}) collective-permute-start(f32[34,2,16,128]{3,2,1,0:T(8,128)S(1)} %get-tuple-element.145), channel_id=1, source_target_pairs={{0,16},{1,17},{2,18},{3,19},{4,20},{5,21},{6,22},{7,23},{8,24},{9,... | collective-permute-start | bytes 1671176 | tf_op jit(solution)/shard_map/ppermute | solution.py:300
  60.8 36.5 %collective-permute-start.14 = (f32[26,2,32,128]{3,2,1,0:T(8,128)S(1)}, f32[26,2,32,128]{3,2,1,0:T(8,128)}, u32[]{:S(2)}, u32[]{:S(2)}) collective-permute-start(f32[26,2,32,128]{3,2,1,0:T(8,128)S(1)} %get-tuple-element.144), channel_id=1, source_target_pairs={{0,8},{1,9},{2,10},{3,11},{4,12},{5,13},{6,14},{7,15},{8,0},{9,1},... | collective-permute-start | bytes 2555912 | tf_op jit(solution)/shard_map/ppermute | solution.py:301
  87.3 14.5 %collective-permute-start.17 = (f32[26,2,16,128]{3,2,1,0:T(8,128)S(1)}, f32[26,2,16,128]{3,2,1,0:T(8,128)}, u32[]{:S(2)}, u32[]{:S(2)}) collective-permute-start(f32[26,2,16,128]{3,2,1,0:T(8,128)S(1)} %pick_passing.7), channel_id=1, source_target_pairs={{0,8},{1,9},{2,10},{3,11},{4,12},{5,13},{6,14},{7,15},{8,0},{9,1},... | collective-permute-start | bytes 1277960 | tf_op jit(solution)/shard_map/ppermute | solution.py:305
  105.5 52.9 %all-to-all-start.5 = ((f32[8,12,2,16,128]{4,3,2,1,0:T(8,128)}), f32[8,12,2,16,128]{4,3,2,1,0:T(8,128)S(1)}, u32[]{:S(2)}, u32[]{:S(2)}) async-start(f32[8,12,2,16,128]{4,3,2,1,0:T(8,128)} %bitcast.31), calls=%async_computation.5 | async-start | bytes 3145728 | tf_op jit(solution)/shard_map/all_to_all | solution.py:281
  111.1 28.0 %collective-permute-start.11 = (f32[34,2,16,128]{3,2,1,0:T(8,128)S(1)}, f32[34,2,16,128]{3,2,1,0:T(8,128)S(1)}, u32[]{:S(2)}, u32[]{:S(2)}) collective-permute-start(f32[34,2,16,128]{3,2,1,0:T(8,128)S(1)} %get-tuple-element.142), channel_id=1, source_target_pairs={{0,16},{1,17},{2,18},{3,19},{4,20},{5,21},{6,22},{7,23},{8,24},{9,... | collective-permute-start | bytes 1671176 | tf_op jit(solution)/shard_map/ppermute | solution.py:300
  112.5 32.9 %collective-permute-start.9 = (f32[26,2,32,128]{3,2,1,0:T(8,128)S(1)}, f32[26,2,32,128]{3,2,1,0:T(8,128)S(1)}, u32[]{:S(2)}, u32[]{:S(2)}) collective-permute-start(f32[26,2,32,128]{3,2,1,0:T(8,128)S(1)} %get-tuple-element.140), channel_id=1, source_target_pairs={{0,8},{1,9},{2,10},{3,11},{4,12},{5,13},{6,14},{7,15},{8,0},{9,1},... | collective-permute-start | bytes 2555912 | tf_op jit(solution)/shard_map/ppermute | solution.py:301
  139.8 14.7 %collective-permute-start.12 = (f32[26,2,16,128]{3,2,1,0:T(8,128)S(1)}, f32[26,2,16,128]{3,2,1,0:T(8,128)S(1)}, u32[]{:S(2)}, u32[]{:S(2)}) collective-permute-start(f32[26,2,16,128]{3,2,1,0:T(8,128)S(1)} %pick_passing.5), channel_id=1, source_target_pairs={{0,8},{1,9},{2,10},{3,11},{4,12},{5,13},{6,14},{7,15},{8,0},{9,1},... | collective-permute-start | bytes 1277960 | tf_op jit(solution)/shard_map/ppermute | solution.py:305
  158.4 1.2 copy-start.3
  159.5 47.9 %all-to-all-start.2 = ((f32[8,12,2,16,128]{4,3,2,1,0:T(8,128)}), f32[8,12,2,16,128]{4,3,2,1,0:T(8,128)S(1)}, u32[]{:S(2)}, u32[]{:S(2)}) async-start(f32[8,12,2,16,128]{4,3,2,1,0:T(8,128)} %bitcast.32), calls=%async_computation.2 | async-start | bytes 3145728 | tf_op jit(solution)/shard_map/all_to_all | solution.py:281
  163.3 27.8 %collective-permute-start.8 = (f32[34,2,16,128]{3,2,1,0:T(8,128)S(1)}, f32[34,2,16,128]{3,2,1,0:T(8,128)S(1)}, u32[]{:S(2)}, u32[]{:S(2)}) collective-permute-start(f32[34,2,16,128]{3,2,1,0:T(8,128)S(1)} %get-tuple-element.139), channel_id=1, source_target_pairs={{0,16},{1,17},{2,18},{3,19},{4,20},{5,21},{6,22},{7,23},{8,24},{9,... | collective-permute-start | bytes 1671176 | tf_op jit(solution)/shard_map/ppermute | solution.py:300
  191.8 11.9 %collective-permute-start.10 = (f32[26,2,16,128]{3,2,1,0:T(8,128)S(1)}, f32[26,2,16,128]{3,2,1,0:T(8,128)S(1)}, u32[]{:S(2)}, u32[]{:S(2)}) collective-permute-start(f32[26,2,16,128]{3,2,1,0:T(8,128)S(1)} %pick_passing.4), channel_id=1, source_target_pairs={{0,8},{1,9},{2,10},{3,11},{4,12},{5,13},{6,14},{7,15},{8,0},{9,1},... | collective-permute-start | bytes 1277960 | tf_op jit(solution)/shard_map/ppermute | solution.py:305
  207.5 1.2 copy-start.9
  208.7 48.2 %all-to-all-start.1 = ((f32[8,12,2,16,128]{4,3,2,1,0:T(8,128)}), f32[8,12,2,16,128]{4,3,2,1,0:T(8,128)S(1)}, u32[]{:S(2)}, u32[]{:S(2)}) async-start(f32[8,12,2,16,128]{4,3,2,1,0:T(8,128)} %bitcast.33), calls=%async_computation.1 | async-start | bytes 3145728 | tf_op jit(solution)/shard_map/all_to_all | solution.py:281
  212.5 27.9 %collective-permute-start.13 = (f32[34,2,16,128]{3,2,1,0:T(8,128)}, f32[34,2,16,128]{3,2,1,0:T(8,128)S(1)}, u32[]{:S(2)}, u32[]{:S(2)}) collective-permute-start(f32[34,2,16,128]{3,2,1,0:T(8,128)} %copy-done.7), channel_id=1, source_target_pairs={{0,16},{1,17},{2,18},{3,19},{4,20},{5,21},{6,22},{7,23},{8,24},{9,... | collective-permute-start | bytes 1671176 | tf_op jit(solution)/shard_map/ppermute | solution.py:300
  240.9 11.9 %collective-permute-start.15 = (f32[26,2,16,128]{3,2,1,0:T(8,128)S(1)}, f32[26,2,16,128]{3,2,1,0:T(8,128)S(1)}, u32[]{:S(2)}, u32[]{:S(2)}) collective-permute-start(f32[26,2,16,128]{3,2,1,0:T(8,128)S(1)} %pick_passing.6), channel_id=1, source_target_pairs={{0,8},{1,9},{2,10},{3,11},{4,12},{5,13},{6,14},{7,15},{8,0},{9,1},... | collective-permute-start | bytes 1277960 | tf_op jit(solution)/shard_map/ppermute | solution.py:305
  256.9 4.5 %copy-start.17 = (s32[128]{0:T(128)S(1)}, s32[128]{0:T(128)}, u32[]{:S(2)}) copy-start(s32[128]{0:T(128)} %param.25) | copy-start | bytes 1540
  256.9 5.3 %copy-start.16 = (s32[128]{0:T(128)S(1)}, s32[128]{0:T(128)}, u32[]{:S(2)}) copy-start(s32[128]{0:T(128)} %param.24) | copy-start | bytes 1540
  256.9 25.5 %all-to-all-start.4 = ((f32[8,12,2,16,128]{4,3,2,1,0:T(8,128)}), f32[8,12,2,16,128]{4,3,2,1,0:T(8,128)}, u32[]{:S(2)}, u32[]{:S(2)}) async-start(f32[8,12,2,16,128]{4,3,2,1,0:T(8,128)} %bitcast.34), calls=%async_computation.4 | async-start | bytes 3145728 | tf_op jit(solution)/shard_map/all_to_all | solution.py:281
  262.3 2.2 copy-start.2
  266.8 1.0 copy-start.5
  282.3 1.4 copy-start.4
  283.7 1.2 copy-start.6
  285.0 11.5 %copy-start.1 = (s32[256]{0:T(256)S(1)}, s32[256]{0:T(256)}, u32[]{:S(2)}) copy-start(s32[256]{0:T(256)} %param.21) | copy-start | bytes 3076
  (2 other events, 1.7 us)

commit v2 on v1

--- a/solution.py
+++ b/solution.py
@@ -17,6 +17,7 @@
 SMEM = pl.BlockSpec(memory_space=pltpu.SMEM)
 VMEM = pl.BlockSpec(memory_space=pltpu.VMEM)
 PARAMS = pltpu.CompilerParams(vmem_limit_bytes=24 * 1024 * 1024)
+COLLECT = PARAMS
 CHAIN = pltpu.CompilerParams(vmem_limit_bytes=44 * 1024 * 1024)
 
 
@@ -227,36 +228,33 @@
     )(far, crossed)
 
 
-def collect_kernel(first_row, source_ref, spread_ref, crossed_ref, near_ref, far_ref, out_ref):
-    rows = out_ref.shape[2]
-    piece = slice(first_row, first_row + rows)
-    bases = [0]
-    for ref in (spread_ref, crossed_ref, near_ref):
-        bases.append(bases[-1] + ref.shape[0])
-
+def collect_kernel(source_ref, spread_ref, crossed_ref, near_ref, far_ref, out_ref):
     def copy(q, carry):
         source = source_ref[q]
-
-        def index(place, ref):
-            return jnp.clip(source - bases[place], 0, ref.shape[0] - 1)
-
-        value = spread_ref[index(0, spread_ref), :, piece, :]
-        value = jnp.where(source < bases[1], value, crossed_ref[index(1, crossed_ref)])
-        value = jnp.where(source < bases[2], value, near_ref[index(2, near_ref), :, piece, :])
-        out_ref[q] = jnp.where(source < bases[3], value, far_ref[index(3, far_ref)])
+        value, base = None, 0
+        for ref in (spread_ref, crossed_ref, near_ref, far_ref):
+            here = ref[jnp.clip(source - base, 0, ref.shape[0] - 1)]
+            value = here if value is None else jnp.where(source < base, value, here)
+            base += ref.shape[0]
+        out_ref[q] = value
         return carry
 
-    lax.fori_loop(0, out_ref.shape[0], copy, 0, unroll=4)
+    lax.fori_loop(0, out_ref.shape[0], copy, 0, unroll=8)
 
 
 def collect(source, spread, crossed, near, far, piece):
-    rows = crossed.shape[2]
-    return pl.pallas_call(
-        functools.partial(collect_kernel, piece * rows),
-        in_specs=[SMEM] + [VMEM] * 4,
+    _, _, rows, width = crossed.shape
+
+    def rows_of(array):
+        return pl.BlockSpec((array.shape[0], 2, rows, width), lambda i: (0, 0, piece, 0))
+
+    return pl.pallas_call(
+        collect_kernel,
+        grid=(1,),
+        in_specs=[SMEM, rows_of(spread), VMEM, rows_of(near), VMEM],
         out_specs=VMEM,
         out_shape=jax.ShapeDtypeStruct((source.shape[0],) + crossed.shape[1:], jnp.float32),
-        compiler_params=PARAMS,
+        compiler_params=COLLECT,
         name="collect",
     )(source, spread, crossed, near, far)
 

time: 298 us -> 296 us (level)
  no operation moved by 1% of the time
where the time goes in v2:
time: 296 us; the launch traced here: 295 us
  waiting for transfers between devices  181 us (61%)
  Pallas kernels  52.8 us (18%)
  starting transfers between devices  36.2 us (12%)
  local copies, waits for them, and re-layouts  14.7 us (5%)
  between operations  7.95 us (3%)
    ppermute x4, waiting for transfers between devices, fetch_items(): crossed.append(lax.ppermute(leaving[r], 'node', swap))  101 us
    all_to_all x6, waiting for transfers between devices, exchange(): return lax.all_to_all(x, 'node', 0, 0, axis_index_groups=planes, tiled=True)  37.3 us
    ppermute x4, waiting for transfers between devices, fetch_items(): far_by = lax.ppermute(passing, 'node', mate)  37.1 us
    all_to_all x6, starting transfers between devices, exchange(): return lax.all_to_all(x, 'node', 0, 0, axis_index_groups=planes, tiled=True)  25.4 us
    pallas_call x4, Pallas kernels, collect(): pl.pallas_call(collect_kernel, grid=(1,), in_specs=[SMEM, rows_of(spread)...  13 us
    pallas_call x1, Pallas kernels, make_plan(): pl.pallas_call(plan_kernel, in_specs=[SMEM] * 2, out_specs=[SMEM] * 4, ou...  12.7 us
    pallas_call x1, Pallas kernels, chain(): pl.pallas_call(chain_kernel, grid_spec=pltpu.PrefetchScalarGridSpec(num_s...  11.5 us
    unnamed x34, local copies, waits for them, and re-layouts  8.99 us
  transfers between devices with their start and end apart: 16, of which 11 were waited for; matrix products, arithmetic and copies ran while one was open for 3% of the time, Pallas kernels for 13%

profile of v2, /device:TPU:0, one launch (start us, length us, event | category | flops | bytes accessed | tf_op | source)
XLA Modules:
  0.0 295.0 jit_solution(8835971702897460035)
XLA Ops:
  0.0 3.8 %cut_rows.3 = f32[8,8,2,32,128]{4,3,2,1,0:T(8,128)} custom-call(f32[8,2,256,256]{3,2,1,0:T(8,128)} %node_ref.1), custom_call_target="tpu_custom_call" | custom-call | tf_op jit(solution)/shard_map/cut_rows/pallas_call | solution.py:34
  3.8 5.2 %all-to-all-start.3 = ((f32[8,8,2,32,128]{4,3,2,1,0:T(8,128)}), f32[8,8,2,32,128]{4,3,2,1,0:T(8,128)S(1)}, u32[]{:S(2)}, u32[]{:S(2)}) async-start(f32[8,8,2,32,128]{4,3,2,1,0:T(8,128)} %cut_rows.3), calls=%async_computation.3 | async-start | bytes 4194304 | tf_op jit(solution)/shard_map/all_to_all | solution.py:279
  9.0 3.8 %cut_rows.2 = f32[8,8,2,32,128]{4,3,2,1,0:T(8,128)} custom-call(f32[8,2,256,256]{3,2,1,0:T(8,128)} %node_ref.1), custom_call_target="tpu_custom_call" | custom-call | tf_op jit(solution)/shard_map/cut_rows/pallas_call | solution.py:34
  12.9 22.8 %all-to-all-done.3 = f32[8,8,2,32,128]{4,3,2,1,0:T(8,128)S(1)} async-done(((f32[8,8,2,32,128]{4,3,2,1,0:T(8,128)}), f32[8,8,2,32,128]{4,3,2,1,0:T(8,128)S(1)}, u32[]{:S(2)}, u32[]{:S(2)}) %all-to-all-start.3) | async-done | bytes 2097184 | tf_op jit(solution)/shard_map/all_to_all | solution.py:279
  35.7 4.3 %all-to-all-start = ((f32[8,8,2,32,128]{4,3,2,1,0:T(8,128)}), f32[8,8,2,32,128]{4,3,2,1,0:T(8,128)}, u32[]{:S(2)}, u32[]{:S(2)}) async-start(f32[8,8,2,32,128]{4,3,2,1,0:T(8,128)} %cut_rows.2), calls=%async_computation | async-start | bytes 4194304 | tf_op jit(solution)/shard_map/all_to_all | solution.py:279
  43.9 12.7 %make_plan.1 = (s32[34]{0:T(128)S(1)}, s32[26]{0:T(128)S(1)}, s32[26]{0:T(128)S(1)}, s32[96]{0:T(128)S(1)}) custom-call(s32[1]{0:T(128)} %bitcast.16.plane_ref, s32[384]{0:T(512)S(1)} %reshape_reshape.4.ids_ref), custom_call_target="tpu_custom_call" | custom-call | tf_op jit(solution)/shard_map/make_plan/pallas_call | solution.py:153
  58.2 2.6 collective-permute-start.16
  63.3 22.8 %collective-permute-done.16.crossed_ref = f32[34,2,16,128]{3,2,1,0:T(8,128)} collective-permute-done((f32[34,2,16,128]{3,2,1,0:T(8,128)S(1)}, f32[34,2,16,128]{3,2,1,0:T(8,128)}, u32[]{:S(2)}, u32[]{:S(2)}) %collective-permute-start.16) | collective-permute-done | bytes 557088 | tf_op jit(solution)/shard_map/ppermute | solution.py:298
  97.3 4.5 %collective-permute-done.17 = f32[26,2,16,128]{3,2,1,0:T(8,128)} collective-permute-done((f32[26,2,16,128]{3,2,1,0:T(8,128)S(1)}, f32[26,2,16,128]{3,2,1,0:T(8,128)}, u32[]{:S(2)}, u32[]{:S(2)}) %collective-permute-start.17) | collective-permute-done | bytes 426016 | tf_op jit(solution)/shard_map/ppermute | solution.py:303
  101.8 3.6 %conditional.7 = (f32[96,2,16,128]{3,2,1,0:T(8,128)}) conditional(s32[]{:T(128)} %convert_element_type.66, (s32[96]{0:T(128)S(1)}, f32[64,2,32,128]{3,2,1,0:T(8,128)S(1)}, f32[34,2,16,128]{3,2,1,0:T(8,128)}, f32[26,2,32,128]{3,2,1,0:T(8,128)}, f32[26,2,16,128]{3,2,1,0:T(8,128)}) %tuple.73, (f32[64,2,32,128]{3,2,1,0:T(8,128)S(1)}, ...), branch_computations={%region_20.22_spmd, %region_21.23_spmd} | conditional | flops 3019232 | bytes 33560396 | solution.py:304
  101.8 3.6 %collect.7 = f32[96,2,16,128]{3,2,1,0:T(8,128)} custom-call(s32[96]{0:T(128)S(1)} %get-tuple-element.117.source_ref, f32[64,2,32,128]{3,2,1,0:T(8,128)S(1)} %get-tuple-element.118.spread_ref, f32[34,2,16,128]{3,2,1,0:T(8,128)} %get-tuple-element.119.crossed_ref, f32[26,2,32,128]{3,2,1,0:T(8,128)} %get-tuple-element.120.near_ref, ...), custom_call_target="tpu_custom_call" | custom-call | tf_op jit(solution)/shard_map/cond/branch_0_fun/collect/pallas_call | solution.py:251
  105.4 3.8 %all-to-all-start.5 = ((f32[8,12,2,16,128]{4,3,2,1,0:T(8,128)}), f32[8,12,2,16,128]{4,3,2,1,0:T(8,128)S(1)}, u32[]{:S(2)}, u32[]{:S(2)}) async-start(f32[8,12,2,16,128]{4,3,2,1,0:T(8,128)} %bitcast.31), calls=%async_computation.5 | async-start | bytes 3145728 | tf_op jit(solution)/shard_map/all_to_all | solution.py:279
  114.1 24.9 %collective-permute-done.11.crossed_ref = f32[34,2,16,128]{3,2,1,0:T(8,128)S(1)} collective-permute-done((f32[34,2,16,128]{3,2,1,0:T(8,128)S(1)}, f32[34,2,16,128]{3,2,1,0:T(8,128)S(1)}, u32[]{:S(2)}, u32[]{:S(2)}) %collective-permute-start.11) | collective-permute-done | bytes 557088 | tf_op jit(solution)/shard_map/ppermute | solution.py:298
  139.8 5.6 %collective-permute-done.9 = f32[26,2,32,128]{3,2,1,0:T(8,128)S(1)} collective-permute-done((f32[26,2,32,128]{3,2,1,0:T(8,128)S(1)}, f32[26,2,32,128]{3,2,1,0:T(8,128)S(1)}, u32[]{:S(2)}, u32[]{:S(2)}) %collective-permute-start.9) | collective-permute-done | bytes 852000 | tf_op jit(solution)/shard_map/ppermute | solution.py:299
  145.4 9.1 %collective-permute-done.12 = f32[26,2,16,128]{3,2,1,0:T(8,128)S(1)} collective-permute-done((f32[26,2,16,128]{3,2,1,0:T(8,128)S(1)}, f32[26,2,16,128]{3,2,1,0:T(8,128)S(1)}, u32[]{:S(2)}, u32[]{:S(2)}) %collective-permute-start.12) | collective-permute-done | bytes 426016 | tf_op jit(solution)/shard_map/ppermute | solution.py:303
  154.4 3.4 %conditional.5 = (f32[96,2,16,128]{3,2,1,0:T(8,128)}) conditional(s32[]{:T(128)} %convert_element_type.66, (s32[96]{0:T(128)S(1)}, f32[64,2,32,128]{3,2,1,0:T(8,128)}, f32[34,2,16,128]{3,2,1,0:T(8,128)S(1)}, f32[26,2,32,128]{3,2,1,0:T(8,128)S(1)}, f32[26,2,16,128]{3,2,1,0:T(8,128)S(1)}) %tuple.32, (f32[64,2,32,128]{3,2,1,0:T(8,128)}, ...), branch_computations={%region_16.18_spmd, %region_17.19_spmd} | conditional | flops 3019232 | bytes 33560396 | solution.py:304
  154.4 3.4 %collect.5 = f32[96,2,16,128]{3,2,1,0:T(8,128)} custom-call(s32[96]{0:T(128)S(1)} %get-tuple-element.99.source_ref, f32[64,2,32,128]{3,2,1,0:T(8,128)} %get-tuple-element.100.spread_ref, f32[34,2,16,128]{3,2,1,0:T(8,128)S(1)} %get-tuple-element.101.crossed_ref, f32[26,2,32,128]{3,2,1,0:T(8,128)S(1)} %get-tuple-element.102.near_ref, ...), custom_call_target="tpu_custom_call" | custom-call | tf_op jit(solution)/shard_map/cond/branch_0_fun/collect/pallas_call | solution.py:251
  159.0 3.8 %all-to-all-start.2 = ((f32[8,12,2,16,128]{4,3,2,1,0:T(8,128)}), f32[8,12,2,16,128]{4,3,2,1,0:T(8,128)S(1)}, u32[]{:S(2)}, u32[]{:S(2)}) async-start(f32[8,12,2,16,128]{4,3,2,1,0:T(8,128)} %bitcast.32), calls=%async_computation.2 | async-start | bytes 3145728 | tf_op jit(solution)/shard_map/all_to_all | solution.py:279
  164.3 26.4 %collective-permute-done.8.crossed_ref = f32[34,2,16,128]{3,2,1,0:T(8,128)S(1)} collective-permute-done((f32[34,2,16,128]{3,2,1,0:T(8,128)S(1)}, f32[34,2,16,128]{3,2,1,0:T(8,128)S(1)}, u32[]{:S(2)}, u32[]{:S(2)}) %collective-permute-start.8) | collective-permute-done | bytes 557088 | tf_op jit(solution)/shard_map/ppermute | solution.py:298
  191.4 11.8 %collective-permute-done.10 = f32[26,2,16,128]{3,2,1,0:T(8,128)S(1)} collective-permute-done((f32[26,2,16,128]{3,2,1,0:T(8,128)S(1)}, f32[26,2,16,128]{3,2,1,0:T(8,128)S(1)}, u32[]{:S(2)}, u32[]{:S(2)}) %collective-permute-start.10) | collective-permute-done | bytes 426016 | tf_op jit(solution)/shard_map/ppermute | solution.py:303
  203.2 3.3 %conditional.4 = (f32[96,2,16,128]{3,2,1,0:T(8,128)S(1)}) conditional(s32[]{:T(128)} %convert_element_type.66, (s32[96]{0:T(128)S(1)}, f32[64,2,32,128]{3,2,1,0:T(8,128)}, f32[34,2,16,128]{3,2,1,0:T(8,128)S(1)}, f32[26,2,32,128]{3,2,1,0:T(8,128)S(1)}, f32[26,2,16,128]{3,2,1,0:T(8,128)S(1)}) %tuple.30, (f32[64,2,32,128]{3,2,1,0:T(8,128)}, ...), branch_computations={%region_14.15_spmd, %region_15.17_spmd} | conditional | flops 3019232 | bytes 33560396 | solution.py:304
  204.1 2.4 collect.4
  207.7 3.8 %all-to-all-start.1 = ((f32[8,12,2,16,128]{4,3,2,1,0:T(8,128)}), f32[8,12,2,16,128]{4,3,2,1,0:T(8,128)S(1)}, u32[]{:S(2)}, u32[]{:S(2)}) async-start(f32[8,12,2,16,128]{4,3,2,1,0:T(8,128)} %bitcast.33), calls=%async_computation.1 | async-start | bytes 3145728 | tf_op jit(solution)/shard_map/all_to_all | solution.py:279
  212.7 26.6 %collective-permute-done.13.crossed_ref = f32[34,2,16,128]{3,2,1,0:T(8,128)S(1)} collective-permute-done((f32[34,2,16,128]{3,2,1,0:T(8,128)}, f32[34,2,16,128]{3,2,1,0:T(8,128)S(1)}, u32[]{:S(2)}, u32[]{:S(2)}) %collective-permute-start.13) | collective-permute-done | bytes 557088 | tf_op jit(solution)/shard_map/ppermute | solution.py:298
  240.0 11.8 %collective-permute-done.15 = f32[26,2,16,128]{3,2,1,0:T(8,128)S(1)} collective-permute-done((f32[26,2,16,128]{3,2,1,0:T(8,128)S(1)}, f32[26,2,16,128]{3,2,1,0:T(8,128)S(1)}, u32[]{:S(2)}, u32[]{:S(2)}) %collective-permute-start.15) | collective-permute-done | bytes 426016 | tf_op jit(solution)/shard_map/ppermute | solution.py:303
  251.8 3.6 %conditional.6 = (f32[96,2,16,128]{3,2,1,0:T(8,128)}) conditional(s32[]{:T(128)} %convert_element_type.66, (s32[96]{0:T(128)S(1)}, f32[64,2,32,128]{3,2,1,0:T(8,128)}, f32[34,2,16,128]{3,2,1,0:T(8,128)S(1)}, f32[26,2,32,128]{3,2,1,0:T(8,128)}, f32[26,2,16,128]{3,2,1,0:T(8,128)S(1)}) %tuple.74, (f32[64,2,32,128]{3,2,1,0:T(8,128)}, ...), branch_computations={%region_18.20_spmd, %region_19.21_spmd} | conditional | flops 3019232 | bytes 33560396 | solution.py:304
  251.8 3.6 %collect.6 = f32[96,2,16,128]{3,2,1,0:T(8,128)} custom-call(s32[96]{0:T(128)S(1)} %get-tuple-element.108.source_ref, f32[64,2,32,128]{3,2,1,0:T(8,128)} %get-tuple-element.109.spread_ref, f32[34,2,16,128]{3,2,1,0:T(8,128)S(1)} %get-tuple-element.110.crossed_ref, f32[26,2,32,128]{3,2,1,0:T(8,128)} %get-tuple-element.111.near_ref, ...), custom_call_target="tpu_custom_call" | custom-call | tf_op jit(solution)/shard_map/cond/branch_0_fun/collect/pallas_call | solution.py:251
  255.4 4.4 %all-to-all-start.4 = ((f32[8,12,2,16,128]{4,3,2,1,0:T(8,128)}), f32[8,12,2,16,128]{4,3,2,1,0:T(8,128)}, u32[]{:S(2)}, u32[]{:S(2)}) async-start(f32[8,12,2,16,128]{4,3,2,1,0:T(8,128)} %bitcast.34), calls=%async_computation.4 | async-start | bytes 3145728 | tf_op jit(solution)/shard_map/all_to_all | solution.py:279
  260.8 2.2 copy-done.2
  263.0 2.4 multiply.1.start_ref
  266.3 14.5 %all-to-all-done.4.refs_2_ = f32[8,12,2,16,128]{4,3,2,1,0:T(8,128)} async-done(((f32[8,12,2,16,128]{4,3,2,1,0:T(8,128)}), f32[8,12,2,16,128]{4,3,2,1,0:T(8,128)}, u32[]{:S(2)}, u32[]{:S(2)}) %all-to-all-start.4) | async-done | bytes 1572896 | tf_op jit(solution)/shard_map/all_to_all | solution.py:279
  283.5 11.5 %chain.1 = f32[2,2,256,256]{3,2,1,0:T(8,128)} custom-call(s32[4]{0:T(128)S(1)} %subtract_reduce_fusion.index_ref.slot, s32[4]{0:T(128)S(1)} %dynamic-slice_subtract_fusion.target, s32[4]{0:T(128)S(1)} %dynamic_slice.16.sign, f32[8,2,256,256]{3,2,1,0:T(8,128)} %node_ref.1, f32[4,2,256,128]{3,2,1,0:T(8,128)S(1)} %copy-done.6, ...), custom_call_target="tpu_custom_call" | custom-call | tf_op jit(solution)/shard_map/chain/pallas_call | solution.py:451
  (79 shorter events, 28.9 us)
Async XLA Ops:
  0.0 40.3 %copy-start = (s32[256]{0:T(256)S(1)}, s32[256]{0:T(256)}, u32[]{:S(2)}) copy-start(s32[256]{0:T(256)} %param.21) | copy-start | bytes 3076
  3.8 31.8 %all-to-all-start.3 = ((f32[8,8,2,32,128]{4,3,2,1,0:T(8,128)}), f32[8,8,2,32,128]{4,3,2,1,0:T(8,128)S(1)}, u32[]{:S(2)}, u32[]{:S(2)}) async-start(f32[8,8,2,32,128]{4,3,2,1,0:T(8,128)} %cut_rows.3), calls=%async_computation.3 | async-start | bytes 4194304 | tf_op jit(solution)/shard_map/all_to_all | solution.py:279
  12.9 27.1 %copy-start.14 = (s32[128,2]{0,1:T(2,128)S(1)}, s32[128,2]{0,1:T(2,128)}, u32[]{:S(2)}) copy-start(s32[128,2]{0,1:T(2,128)} %param.22) | copy-start | bytes 3076
  35.6 66.1 %copy-start.8 = (f32[8,8,2,32,128]{4,3,2,1,0:T(8,128)}, f32[8,8,2,32,128]{4,3,2,1,0:T(8,128)S(1)}, u32[]{:S(2)}) copy-start(f32[8,8,2,32,128]{4,3,2,1,0:T(8,128)S(1)} %all-to-all-done.3) | copy-start | bytes 6291460
  35.7 69.7 %all-to-all-start = ((f32[8,8,2,32,128]{4,3,2,1,0:T(8,128)}), f32[8,8,2,32,128]{4,3,2,1,0:T(8,128)}, u32[]{:S(2)}, u32[]{:S(2)}) async-start(f32[8,8,2,32,128]{4,3,2,1,0:T(8,128)} %cut_rows.2), calls=%async_computation | async-start | bytes 4194304 | tf_op jit(solution)/shard_map/all_to_all | solution.py:279
  40.3 2.1 copy-start.15
  43.4 58.3 %copy-start.13 = (s32[4]{0:T(128)S(1)}, s32[4]{0:T(128)}, u32[]{:S(2)}) copy-start(s32[4]{0:T(128)} %constant.173.clone) | copy-start | bytes 52
  43.5 13.1 %copy-start.12 = (s32[32,4,4]{2,1,0:T(4,128)}, s32[32,4,4]{2,1,0:T(4,128)S(1)}, u32[]{:S(2)}) copy-start(s32[32,4,4]{2,1,0:T(4,128)S(1)} %reshape.49) | copy-start | bytes 6148
  43.7 13.0 %copy-start.11 = (s32[32,4,3]{2,1,0:T(4,128)}, s32[32,4,3]{2,1,0:T(4,128)S(1)}, u32[]{:S(2)}) copy-start(s32[32,4,3]{2,1,0:T(4,128)S(1)} %slice.101) | copy-start | bytes 4612
  58.2 27.9 %collective-permute-start.16 = (f32[34,2,16,128]{3,2,1,0:T(8,128)S(1)}, f32[34,2,16,128]{3,2,1,0:T(8,128)}, u32[]{:S(2)}, u32[]{:S(2)}) collective-permute-start(f32[34,2,16,128]{3,2,1,0:T(8,128)S(1)} %get-tuple-element.145), channel_id=1, source_target_pairs={{0,16},{1,17},{2,18},{3,19},{4,20},{5,21},{6,22},{7,23},{8,24},{9,... | collective-permute-start | bytes 1671176 | tf_op jit(solution)/shard_map/ppermute | solution.py:298
  60.8 36.5 %collective-permute-start.14 = (f32[26,2,32,128]{3,2,1,0:T(8,128)S(1)}, f32[26,2,32,128]{3,2,1,0:T(8,128)}, u32[]{:S(2)}, u32[]{:S(2)}) collective-permute-start(f32[26,2,32,128]{3,2,1,0:T(8,128)S(1)} %get-tuple-element.144), channel_id=1, source_target_pairs={{0,8},{1,9},{2,10},{3,11},{4,12},{5,13},{6,14},{7,15},{8,0},{9,1},... | collective-permute-start | bytes 2555912 | tf_op jit(solution)/shard_map/ppermute | solution.py:299
  87.3 14.5 %collective-permute-start.17 = (f32[26,2,16,128]{3,2,1,0:T(8,128)S(1)}, f32[26,2,16,128]{3,2,1,0:T(8,128)}, u32[]{:S(2)}, u32[]{:S(2)}) collective-permute-start(f32[26,2,16,128]{3,2,1,0:T(8,128)S(1)} %pick_passing.7), channel_id=1, source_target_pairs={{0,8},{1,9},{2,10},{3,11},{4,12},{5,13},{6,14},{7,15},{8,0},{9,1},... | collective-permute-start | bytes 1277960 | tf_op jit(solution)/shard_map/ppermute | solution.py:303
  105.4 52.5 %all-to-all-start.5 = ((f32[8,12,2,16,128]{4,3,2,1,0:T(8,128)}), f32[8,12,2,16,128]{4,3,2,1,0:T(8,128)S(1)}, u32[]{:S(2)}, u32[]{:S(2)}) async-start(f32[8,12,2,16,128]{4,3,2,1,0:T(8,128)} %bitcast.31), calls=%async_computation.5 | async-start | bytes 3145728 | tf_op jit(solution)/shard_map/all_to_all | solution.py:279
  111.1 28.0 %collective-permute-start.11 = (f32[34,2,16,128]{3,2,1,0:T(8,128)S(1)}, f32[34,2,16,128]{3,2,1,0:T(8,128)S(1)}, u32[]{:S(2)}, u32[]{:S(2)}) collective-permute-start(f32[34,2,16,128]{3,2,1,0:T(8,128)S(1)} %get-tuple-element.142), channel_id=1, source_target_pairs={{0,16},{1,17},{2,18},{3,19},{4,20},{5,21},{6,22},{7,23},{8,24},{9,... | collective-permute-start | bytes 1671176 | tf_op jit(solution)/shard_map/ppermute | solution.py:298
  112.4 32.9 %collective-permute-start.9 = (f32[26,2,32,128]{3,2,1,0:T(8,128)S(1)}, f32[26,2,32,128]{3,2,1,0:T(8,128)S(1)}, u32[]{:S(2)}, u32[]{:S(2)}) collective-permute-start(f32[26,2,32,128]{3,2,1,0:T(8,128)S(1)} %get-tuple-element.140), channel_id=1, source_target_pairs={{0,8},{1,9},{2,10},{3,11},{4,12},{5,13},{6,14},{7,15},{8,0},{9,1},... | collective-permute-start | bytes 2555912 | tf_op jit(solution)/shard_map/ppermute | solution.py:299
  139.7 14.7 %collective-permute-start.12 = (f32[26,2,16,128]{3,2,1,0:T(8,128)S(1)}, f32[26,2,16,128]{3,2,1,0:T(8,128)S(1)}, u32[]{:S(2)}, u32[]{:S(2)}) collective-permute-start(f32[26,2,16,128]{3,2,1,0:T(8,128)S(1)} %pick_passing.5), channel_id=1, source_target_pairs={{0,8},{1,9},{2,10},{3,11},{4,12},{5,13},{6,14},{7,15},{8,0},{9,1},... | collective-permute-start | bytes 1277960 | tf_op jit(solution)/shard_map/ppermute | solution.py:303
  157.9 1.2 copy-start.3
  159.0 47.5 %all-to-all-start.2 = ((f32[8,12,2,16,128]{4,3,2,1,0:T(8,128)}), f32[8,12,2,16,128]{4,3,2,1,0:T(8,128)S(1)}, u32[]{:S(2)}, u32[]{:S(2)}) async-start(f32[8,12,2,16,128]{4,3,2,1,0:T(8,128)} %bitcast.32), calls=%async_computation.2 | async-start | bytes 3145728 | tf_op jit(solution)/shard_map/all_to_all | solution.py:279
  162.9 27.8 %collective-permute-start.8 = (f32[34,2,16,128]{3,2,1,0:T(8,128)S(1)}, f32[34,2,16,128]{3,2,1,0:T(8,128)S(1)}, u32[]{:S(2)}, u32[]{:S(2)}) collective-permute-start(f32[34,2,16,128]{3,2,1,0:T(8,128)S(1)} %get-tuple-element.139), channel_id=1, source_target_pairs={{0,16},{1,17},{2,18},{3,19},{4,20},{5,21},{6,22},{7,23},{8,24},{9,... | collective-permute-start | bytes 1671176 | tf_op jit(solution)/shard_map/ppermute | solution.py:298
  191.3 11.9 %collective-permute-start.10 = (f32[26,2,16,128]{3,2,1,0:T(8,128)S(1)}, f32[26,2,16,128]{3,2,1,0:T(8,128)S(1)}, u32[]{:S(2)}, u32[]{:S(2)}) collective-permute-start(f32[26,2,16,128]{3,2,1,0:T(8,128)S(1)} %pick_passing.4), channel_id=1, source_target_pairs={{0,8},{1,9},{2,10},{3,11},{4,12},{5,13},{6,14},{7,15},{8,0},{9,1},... | collective-permute-start | bytes 1277960 | tf_op jit(solution)/shard_map/ppermute | solution.py:303
  206.5 1.2 copy-start.9
  207.7 47.7 %all-to-all-start.1 = ((f32[8,12,2,16,128]{4,3,2,1,0:T(8,128)}), f32[8,12,2,16,128]{4,3,2,1,0:T(8,128)S(1)}, u32[]{:S(2)}, u32[]{:S(2)}) async-start(f32[8,12,2,16,128]{4,3,2,1,0:T(8,128)} %bitcast.33), calls=%async_computation.1 | async-start | bytes 3145728 | tf_op jit(solution)/shard_map/all_to_all | solution.py:279
  211.5 27.9 %collective-permute-start.13 = (f32[34,2,16,128]{3,2,1,0:T(8,128)}, f32[34,2,16,128]{3,2,1,0:T(8,128)S(1)}, u32[]{:S(2)}, u32[]{:S(2)}) collective-permute-start(f32[34,2,16,128]{3,2,1,0:T(8,128)} %copy-done.7), channel_id=1, source_target_pairs={{0,16},{1,17},{2,18},{3,19},{4,20},{5,21},{6,22},{7,23},{8,24},{9,... | collective-permute-start | bytes 1671176 | tf_op jit(solution)/shard_map/ppermute | solution.py:298
  240.0 11.9 %collective-permute-start.15 = (f32[26,2,16,128]{3,2,1,0:T(8,128)S(1)}, f32[26,2,16,128]{3,2,1,0:T(8,128)S(1)}, u32[]{:S(2)}, u32[]{:S(2)}) collective-permute-start(f32[26,2,16,128]{3,2,1,0:T(8,128)S(1)} %pick_passing.6), channel_id=1, source_target_pairs={{0,8},{1,9},{2,10},{3,11},{4,12},{5,13},{6,14},{7,15},{8,0},{9,1},... | collective-permute-start | bytes 1277960 | tf_op jit(solution)/shard_map/ppermute | solution.py:303
  255.4 4.5 %copy-start.17 = (s32[128]{0:T(128)S(1)}, s32[128]{0:T(128)}, u32[]{:S(2)}) copy-start(s32[128]{0:T(128)} %param.25) | copy-start | bytes 1540
  255.4 5.3 %copy-start.16 = (s32[128]{0:T(128)S(1)}, s32[128]{0:T(128)}, u32[]{:S(2)}) copy-start(s32[128]{0:T(128)} %param.24) | copy-start | bytes 1540
  255.4 25.5 %all-to-all-start.4 = ((f32[8,12,2,16,128]{4,3,2,1,0:T(8,128)}), f32[8,12,2,16,128]{4,3,2,1,0:T(8,128)}, u32[]{:S(2)}, u32[]{:S(2)}) async-start(f32[8,12,2,16,128]{4,3,2,1,0:T(8,128)} %bitcast.34), calls=%async_computation.4 | async-start | bytes 3145728 | tf_op jit(solution)/shard_map/all_to_all | solution.py:279
  260.8 2.2 copy-start.2
  265.4 1.0 copy-start.5
  280.8 1.4 copy-start.4
  282.3 1.2 copy-start.6
  283.5 11.5 %copy-start.1 = (s32[256]{0:T(256)S(1)}, s32[256]{0:T(256)}, u32[]{:S(2)}) copy-start(s32[256]{0:T(256)} %param.21) | copy-start | bytes 3076
  (2 other events, 1.7 us)

commit v3 on v0

--- a/solution.py
+++ b/solution.py
@@ -29,7 +29,7 @@
 def cut_rows(nodes, group, part, width):
     count, _, order, _ = nodes.shape
     rows = order // group
-    steps = 4 if group % 4 == 0 else 1
+    steps = 2 if group % 2 == 0 else 1
     return pl.pallas_call(
         cut_kernel,
         grid=(steps,),
@@ -217,9 +217,11 @@
 def product(left, blocks):
     left_high, left_low = halves_of(left)
     right_high, right_low = stacked(blocks)
-    dot = functools.partial(jnp.dot, preferred_element_type=jnp.float32)
-    small = dot(left_high, right_low) + dot(left_low, right_high)
-    return dot(left_high, right_high) + small
+    return jnp.dot(
+        jnp.concatenate([left_high, left_high, left_low], axis=1),
+        jnp.concatenate([right_high, right_low, right_high], axis=0),
+        preferred_element_type=jnp.float32,
+    )
 
 
 def wide(ref):
@@ -255,7 +257,7 @@
             out_specs=pl.BlockSpec((1, 2, order, cols), lambda k, index: (k, 0, 0, 0)),
         ),
         out_shape=jax.ShapeDtypeStruct((number, 2, order, cols), jnp.float32),
-        compiler_params=CHAIN,
+        compiler_params=LARGE,
         name="multiply",
     )(left_index, lefts, *rights)
 
@@ -299,22 +301,17 @@
     )(target, sign, lefts, *rights)
 
 
-def chain_kernel(slot, target, sign, node_ref, start_ref, *refs):
+def chain_kernel(slot, target, sign, node_ref, *refs):
     right_refs, out_ref = refs[:-1], refs[-1]
-    last = product(wide(node_ref), [right_refs[-1][:, 0]])
-    width = last.shape[1] // 2
-    first = jnp.concatenate(
-        [start_ref[0, 0], last[:, :width], start_ref[0, 1], last[:, width:]], axis=1
-    )
-    longer = product(first, [ref[:, 1] for ref in right_refs])
-    both = product(longer, [ref[:, 2] for ref in right_refs])
-    add_result(pl.program_id(0), target, sign, both, out_ref)
-
-
-def chain(slot, target, sign, nodes, start, rights):
+    left = wide(node_ref)
+    for which in range(3):
+        left = product(left, [ref[:, which] for ref in right_refs])
+    add_result(pl.program_id(0), target, sign, left, out_ref)
+
+
+def chain(slot, target, sign, nodes, rights):
     order = nodes.shape[2]
     whole = (RES_COL, 2, order, order)
-    early = start.shape[-1]
     return pl.pallas_call(
         chain_kernel,
         grid_spec=pltpu.PrefetchScalarGridSpec(
@@ -322,7 +319,6 @@
             grid=(slot.shape[0],),
             in_specs=[
                 pl.BlockSpec((1, 2, order, order), lambda k, slot, t, s: (slot[k], 0, 0, 0)),
-                pl.BlockSpec((1, 2, order, early), lambda k, slot, t, s: (k, 0, 0, 0)),
                 *[triple_spec(right) for right in rights],
             ],
             out_specs=pl.BlockSpec(whole, lambda k, slot, t, s: (0, 0, 0, 0)),
@@ -330,7 +326,7 @@
         out_shape=jax.ShapeDtypeStruct(whole, jnp.float32),
         compiler_params=CHAIN,
         name="chain",
-    )(slot, target, sign, nodes, start, *rights)
+    )(slot, target, sign, nodes, *rights)
 
 
 def all_columns(x):
@@ -358,9 +354,8 @@
     own_targets = lax.dynamic_slice_in_dim(targets, column * second_col, second_col, 0)
     own_targets = own_targets - column * RES_COL
 
-    if lax.axis_size("pair") == 1 and len(rights) > 1:
-        start = multiply(own_slots, node_blocks, rights[:-1], 0)
-        return chain(own_slots, own_targets, own_signs, node_blocks, start, rights)
+    if lax.axis_size("pair") == 1:
+        return chain(own_slots, own_targets, own_signs, node_blocks, rights)
     same = jnp.arange(second_col, dtype=jnp.int32)
     products = multiply(own_slots, all_columns(node_blocks), rights, 0)
     longer = multiply(same, all_columns(products), rights, 1)

time: 247 us -> 242 us (0.980)
  local copies, waits for them, and re-layouts: 14.8 us -> 7.02 us
  waiting for transfers between devices: 162 us -> 169 us
  Pallas kernels: 39.2 us -> 35.8 us
    unnamed x22 -> x12, local copies, waits for them, and re-layouts: 7.69 us -> 0.03 us
    all_to_all x4, waiting for transfers between devices: 64.6 us -> 71.3 us  [exchange(): return lax.all_to_all(x, 'node', 0, 0, axis_index_groups=halves, tiled=True)]
    pallas_call x2, Pallas kernels: 6.65 us -> 10 us  [collect(): pl.pallas_call(collect_kernel, in_specs=[SMEM, SMEM, VMEM, VMEM, ANY], ou...]
where the time goes in v3:
time: 242 us; the launch traced here: 241 us
  waiting for transfers between devices  169 us (70%)
  Pallas kernels  35.8 us (15%)
  starting transfers between devices  28 us (12%)
  local copies, waits for them, and re-layouts  7.02 us (3%)
    ppermute x2, waiting for transfers between devices, fetch_items(): arrived = lax.ppermute(leaving, 'node', swap)  97.7 us
    all_to_all x4, waiting for transfers between devices, exchange(): return lax.all_to_all(x, 'node', 0, 0, axis_index_groups=halves, tiled=True)  71.3 us
    all_to_all x4, starting transfers between devices, exchange(): return lax.all_to_all(x, 'node', 0, 0, axis_index_groups=halves, tiled=True)  22 us
    pallas_call x2, Pallas kernels, collect(): pl.pallas_call(collect_kernel, in_specs=[SMEM, SMEM, VMEM, VMEM, ANY], ou...  10 us
    pallas_call x1, Pallas kernels, chain(): pl.pallas_call(chain_kernel, grid_spec=pltpu.PrefetchScalarGridSpec(num_s...  9.5 us
    pallas_call x1, Pallas kernels, make_plan(): pl.pallas_call(functools.partial(plan_kernel, room), in_specs=[SMEM] * 2,...  6.59 us
    ppermute x2, starting transfers between devices, fetch_items(): arrived = lax.ppermute(leaving, 'node', swap)  6.03 us
    pallas_call x2, Pallas kernels, cut_rows(): pl.pallas_call(cut_kernel, grid=(steps,), in_specs=[pl.BlockSpec((count,...  5.37 us
  transfers between devices with their start and end apart: 6, of which 4 were waited for; matrix products, arithmetic and copies ran while one was open for 3% of the time, Pallas kernels for 10%

profile of v3, /device:TPU:0, one launch (start us, length us, event | category | flops | bytes accessed | tf_op | source)
XLA Modules:
  0.0 240.9 jit_solution(3365337884551105985)
XLA Ops:
  0.0 2.7 %cut_rows.2 = f32[16,8,2,16,128]{4,3,2,1,0:T(8,128)} custom-call(f32[8,2,256,256]{3,2,1,0:T(8,128)} %node_ref.1), custom_call_target="tpu_custom_call" | custom-call | tf_op jit(solution)/shard_map/cut_rows/pallas_call | solution.py:33
  2.7 6.3 %all-to-all-start = ((f32[16,8,2,16,128]{4,3,2,1,0:T(8,128)}), f32[16,8,2,16,128]{4,3,2,1,0:T(8,128)S(1)}, u32[]{:S(2)}, u32[]{:S(2)}) async-start(f32[16,8,2,16,128]{4,3,2,1,0:T(8,128)} %cut_rows.2), calls=%async_computation | async-start | bytes 4194304 | tf_op jit(solution)/shard_map/all_to_all | solution.py:179
  9.0 2.7 %cut_rows.3 = f32[16,8,2,16,128]{4,3,2,1,0:T(8,128)} custom-call(f32[8,2,256,256]{3,2,1,0:T(8,128)} %node_ref.1), custom_call_target="tpu_custom_call" | custom-call | tf_op jit(solution)/shard_map/cut_rows/pallas_call | solution.py:33
  11.7 26.4 %all-to-all-done = f32[16,8,2,16,128]{4,3,2,1,0:T(8,128)S(1)} async-done(((f32[16,8,2,16,128]{4,3,2,1,0:T(8,128)}), f32[16,8,2,16,128]{4,3,2,1,0:T(8,128)S(1)}, u32[]{:S(2)}, u32[]{:S(2)}) %all-to-all-start) | async-done | bytes 2097184 | tf_op jit(solution)/shard_map/all_to_all | solution.py:179
  38.1 5.0 %all-to-all-start.2 = ((f32[16,8,2,16,128]{4,3,2,1,0:T(8,128)}), f32[16,8,2,16,128]{4,3,2,1,0:T(8,128)}, u32[]{:S(2)}, u32[]{:S(2)}) async-start(f32[16,8,2,16,128]{4,3,2,1,0:T(8,128)} %cut_rows.3), calls=%async_computation.2 | async-start | bytes 4194304 | tf_op jit(solution)/shard_map/all_to_all | solution.py:179
  43.1 0.1 copy.11
  43.2 0.1 reshape.49
  43.3 0.1 copy.10
  43.5 0.1 reshape.41
  43.6 1.9 gather_fusion
  45.6 0.1 reshape.40
  45.7 0.7 gather_fusion.1
  46.5 0.1 reshape.32
  46.7 0.2 reshape_reshape.3.ids_ref
  46.9 6.6 %make_plan.1 = (s32[128]{0:T(128)S(1)}, s32[192]{0:T(256)S(1)}, s32[1]{0:T(128)}) custom-call(s32[1]{0:T(128)} %bitcast.half_ref, s32[384]{0:T(512)S(1)} %reshape_reshape.3.ids_ref), custom_call_target="tpu_custom_call" | custom-call | tf_op jit(solution)/shard_map/make_plan/pallas_call | solution.py:94
  53.5 1.7 pick_leaving.2
  55.2 2.7 %collective-permute-start.2 = (f32[58,2,16,128]{3,2,1,0:T(8,128)S(1)}, f32[58,2,16,128]{3,2,1,0:T(8,128)S(1)}, u32[]{:S(2)}, u32[]{:S(2)}) collective-permute-start(f32[58,2,16,128]{3,2,1,0:T(8,128)S(1)} %pick_leaving.2), channel_id=1, source_target_pairs={{0,16},{1,17},{2,18},{3,19},{4,20},{5,21},{6,22},{7,23},{8,24},{9,... | collective-permute-start | bytes 2850824 | tf_op jit(solution)/shard_map/ppermute | solution.py:186
  58.4 1.6 conditional.2
  58.5 1.6 broadcast.9
  60.0 39.9 %collective-permute-done.2.arrived_ref = f32[58,2,16,128]{3,2,1,0:T(8,128)S(1)} collective-permute-done((f32[58,2,16,128]{3,2,1,0:T(8,128)S(1)}, f32[58,2,16,128]{3,2,1,0:T(8,128)S(1)}, u32[]{:S(2)}, u32[]{:S(2)}) %collective-permute-start.2) | collective-permute-done | bytes 950304 | tf_op jit(solution)/shard_map/ppermute | solution.py:186
  99.9 4.9 %collect.2 = f32[192,2,16,128]{3,2,1,0:T(8,128)} custom-call(s32[192]{0:T(256)S(1)} %get-tuple-element.16.source_ref, s32[1]{0:T(128)} %get-tuple-element.17.crowded_ref, f32[128,2,16,128]{3,2,1,0:T(8,128)} %bitcast.9, f32[58,2,16,128]{3,2,1,0:T(8,128)S(1)} %collective-permute-done.2.arrived_ref, f32[128,2,16,128]{3,2,1,0:T(8,128)} %get-tuple-element.19.extra_ref), custom_call_target="tpu_custom_call" | custom-call | tf_op jit(solution)/shard_map/collect/pallas_call | solution.py:157
  104.8 4.0 %all-to-all-start.1 = ((f32[16,12,2,16,128]{4,3,2,1,0:T(8,128)}), f32[16,12,2,16,128]{4,3,2,1,0:T(8,128)S(1)}, u32[]{:S(2)}, u32[]{:S(2)}) async-start(f32[16,12,2,16,128]{4,3,2,1,0:T(8,128)} %bitcast.3), calls=%async_computation.1 | async-start | bytes 6291456 | tf_op jit(solution)/shard_map/all_to_all | solution.py:179
  108.9 2.6 %pick_leaving.3 = f32[58,2,16,128]{3,2,1,0:T(8,128)} custom-call(s32[128]{0:T(128)S(1)} %get-tuple-element.18.send_ref, f32[128,2,16,128]{3,2,1,0:T(8,128)} %bitcast.4.spread_ref), custom_call_target="tpu_custom_call" | custom-call | tf_op jit(solution)/shard_map/pick_leaving/pallas_call | solution.py:118
  111.5 3.4 %collective-permute-start.3 = (f32[58,2,16,128]{3,2,1,0:T(8,128)}, f32[58,2,16,128]{3,2,1,0:T(8,128)}, u32[]{:S(2)}, u32[]{:S(2)}) collective-permute-start(f32[58,2,16,128]{3,2,1,0:T(8,128)} %pick_leaving.3), channel_id=1, source_target_pairs={{0,16},{1,17},{2,18},{3,19},{4,20},{5,21},{6,22},{7,23},{8,24},{9,... | collective-permute-start | bytes 2850824 | tf_op jit(solution)/shard_map/ppermute | solution.py:186
  114.9 1.6 conditional.3
  114.9 1.6 broadcast.10
  116.5 57.8 %collective-permute-done.3.arrived_ref = f32[58,2,16,128]{3,2,1,0:T(8,128)} collective-permute-done((f32[58,2,16,128]{3,2,1,0:T(8,128)}, f32[58,2,16,128]{3,2,1,0:T(8,128)}, u32[]{:S(2)}, u32[]{:S(2)}) %collective-permute-start.3) | collective-permute-done | bytes 950304 | tf_op jit(solution)/shard_map/ppermute | solution.py:186
  174.3 5.1 %collect.3 = f32[192,2,16,128]{3,2,1,0:T(8,128)} custom-call(s32[192]{0:T(256)S(1)} %get-tuple-element.16.source_ref, s32[1]{0:T(128)} %get-tuple-element.17.crowded_ref, f32[128,2,16,128]{3,2,1,0:T(8,128)} %bitcast.4.spread_ref, f32[58,2,16,128]{3,2,1,0:T(8,128)} %collective-permute-done.3.arrived_ref, f32[128,2,16,128]{3,2,1,0:T(8,128)} %get-tuple-element.20.extra_ref), custom_call_target="tpu_custom_call" | custom-call | tf_op jit(solution)/shard_map/collect/pallas_call | solution.py:157
  179.5 6.7 %all-to-all-start.3 = ((f32[16,12,2,16,128]{4,3,2,1,0:T(8,128)}), f32[16,12,2,16,128]{4,3,2,1,0:T(8,128)}, u32[]{:S(2)}, u32[]{:S(2)}) async-start(f32[16,12,2,16,128]{4,3,2,1,0:T(8,128)} %bitcast.5), calls=%async_computation.3 | async-start | bytes 6291456 | tf_op jit(solution)/shard_map/all_to_all | solution.py:179
  186.3 0.1 subtract_reduce_fusion.slot
  186.5 44.9 %all-to-all-done.3.refs_1_ = f32[16,12,2,16,128]{4,3,2,1,0:T(8,128)} async-done(((f32[16,12,2,16,128]{4,3,2,1,0:T(8,128)}), f32[16,12,2,16,128]{4,3,2,1,0:T(8,128)}, u32[]{:S(2)}, u32[]{:S(2)}) %all-to-all-start.3) | async-done | bytes 3145760 | tf_op jit(solution)/shard_map/all_to_all | solution.py:179
  231.4 9.5 %chain.1 = f32[2,2,256,256]{3,2,1,0:T(8,128)} custom-call(s32[4]{0:T(128)S(1)} %subtract_reduce_fusion.slot, s32[4]{0:T(128)S(1)} %dynamic-slice_subtract_fusion.target, s32[4]{0:T(128)S(1)} %dynamic_slice.12.sign, f32[8,2,256,256]{3,2,1,0:T(8,128)} %node_ref.1, f32[16,12,2,16,128]{4,3,2,1,0:T(8,128)S(1)} %all-to-all-done.1.refs_0_, ...), custom_call_target="tpu_custom_call" | custom-call | tf_op jit(solution)/shard_map/chain/pallas_call | solution.py:315
  (21 shorter events, 0.3 us)
Async XLA Ops:
  0.0 43.6 %copy-start = (s32[256]{0:T(256)S(1)}, s32[256]{0:T(256)}, u32[]{:S(2)}) copy-start(s32[256]{0:T(256)} %param.11) | copy-start | bytes 3076
  2.7 35.4 %all-to-all-start = ((f32[16,8,2,16,128]{4,3,2,1,0:T(8,128)}), f32[16,8,2,16,128]{4,3,2,1,0:T(8,128)S(1)}, u32[]{:S(2)}, u32[]{:S(2)}) async-start(f32[16,8,2,16,128]{4,3,2,1,0:T(8,128)} %cut_rows.2), calls=%async_computation | async-start | bytes 4194304 | tf_op jit(solution)/shard_map/all_to_all | solution.py:179
  11.7 31.4 %copy-start.2 = (s32[128,2]{0,1:T(2,128)S(1)}, s32[128,2]{0,1:T(2,128)}, u32[]{:S(2)}) copy-start(s32[128,2]{0,1:T(2,128)} %param.13) | copy-start | bytes 3076
  11.7 31.6 %copy-start.3 = (s32[128,2]{0,1:T(2,128)S(1)}, s32[128,2]{0,1:T(2,128)}, u32[]{:S(2)}) copy-start(s32[128,2]{0,1:T(2,128)} %param.12) | copy-start | bytes 3076
  38.1 5.0 %copy-start.1 = (f32[16,8,2,16,128]{4,3,2,1,0:T(8,128)}, f32[16,8,2,16,128]{4,3,2,1,0:T(8,128)S(1)}, u32[]{:S(2)}) copy-start(f32[16,8,2,16,128]{4,3,2,1,0:T(8,128)S(1)} %all-to-all-done) | copy-start | bytes 6291460
  38.1 66.7 %all-to-all-start.2 = ((f32[16,8,2,16,128]{4,3,2,1,0:T(8,128)}), f32[16,8,2,16,128]{4,3,2,1,0:T(8,128)}, u32[]{:S(2)}, u32[]{:S(2)}) async-start(f32[16,8,2,16,128]{4,3,2,1,0:T(8,128)} %cut_rows.3), calls=%async_computation.2 | async-start | bytes 4194304 | tf_op jit(solution)/shard_map/all_to_all | solution.py:179
  55.2 44.7 %collective-permute-start.2 = (f32[58,2,16,128]{3,2,1,0:T(8,128)S(1)}, f32[58,2,16,128]{3,2,1,0:T(8,128)S(1)}, u32[]{:S(2)}, u32[]{:S(2)}) collective-permute-start(f32[58,2,16,128]{3,2,1,0:T(8,128)S(1)} %pick_leaving.2), channel_id=1, source_target_pairs={{0,16},{1,17},{2,18},{3,19},{4,20},{5,21},{6,22},{7,23},{8,24},{9,... | collective-permute-start | bytes 2850824 | tf_op jit(solution)/shard_map/ppermute | solution.py:186
  104.8 74.6 %all-to-all-start.1 = ((f32[16,12,2,16,128]{4,3,2,1,0:T(8,128)}), f32[16,12,2,16,128]{4,3,2,1,0:T(8,128)S(1)}, u32[]{:S(2)}, u32[]{:S(2)}) async-start(f32[16,12,2,16,128]{4,3,2,1,0:T(8,128)} %bitcast.3), calls=%async_computation.1 | async-start | bytes 6291456 | tf_op jit(solution)/shard_map/all_to_all | solution.py:179
  111.5 62.8 %collective-permute-start.3 = (f32[58,2,16,128]{3,2,1,0:T(8,128)}, f32[58,2,16,128]{3,2,1,0:T(8,128)}, u32[]{:S(2)}, u32[]{:S(2)}) collective-permute-start(f32[58,2,16,128]{3,2,1,0:T(8,128)} %pick_leaving.3), channel_id=1, source_target_pairs={{0,16},{1,17},{2,18},{3,19},{4,20},{5,21},{6,22},{7,23},{8,24},{9,... | collective-permute-start | bytes 2850824 | tf_op jit(solution)/shard_map/ppermute | solution.py:186
  179.5 6.7 %copy-start.5 = (s32[128]{0:T(128)S(1)}, s32[128]{0:T(128)}, u32[]{:S(2)}) copy-start(s32[128]{0:T(128)} %param.15) | copy-start | bytes 1540
  179.5 6.9 %copy-start.4 = (s32[128]{0:T(128)S(1)}, s32[128]{0:T(128)}, u32[]{:S(2)}) copy-start(s32[128]{0:T(128)} %param.14) | copy-start | bytes 1540
  179.5 51.9 %all-to-all-start.3 = ((f32[16,12,2,16,128]{4,3,2,1,0:T(8,128)}), f32[16,12,2,16,128]{4,3,2,1,0:T(8,128)}, u32[]{:S(2)}, u32[]{:S(2)}) async-start(f32[16,12,2,16,128]{4,3,2,1,0:T(8,128)} %bitcast.5), calls=%async_computation.3 | async-start | bytes 6291456 | tf_op jit(solution)/shard_map/all_to_all | solution.py:179

commit v4 on v3

--- a/solution.py
+++ b/solution.py
@@ -125,19 +125,23 @@
     )(send, spread)
 
 
-def collect_kernel(source_ref, crowded_ref, spread_ref, arrived_ref, extra_ref, out_ref, sem):
-    count, room = spread_ref.shape[0], arrived_ref.shape[0]
+def collect_kernel(
+    source_ref, flags_ref, spread_ref, first_ref, second_ref, extra_ref, out_ref, sem
+):
+    count, room = spread_ref.shape[0], first_ref.shape[0]
+    outer = flags_ref[1] > 0
 
     def copy(q, carry):
         source = source_ref[q]
         near = jnp.minimum(source, count - 1)
         far = jnp.clip(source - count, 0, room - 1)
-        out_ref[q] = jnp.where(source < count, spread_ref[near], arrived_ref[far])
+        arrived = jnp.where(outer, second_ref[far], first_ref[far])
+        out_ref[q] = jnp.where(source < count, spread_ref[near], arrived)
         return carry
 
     lax.fori_loop(0, out_ref.shape[0], copy, 0, unroll=8)
 
-    @pl.when(crowded_ref[0] > 0)
+    @pl.when(flags_ref[0] > 0)
     def _():
         def fetch(q, carry):
             source = source_ref[q] - (count + room)
@@ -153,16 +157,16 @@
         lax.fori_loop(0, out_ref.shape[0], fetch, 0)
 
 
-def collect(source, crowded, spread, arrived, extra):
+def collect(source, flags, spread, first, second, extra):
     return pl.pallas_call(
         collect_kernel,
-        in_specs=[SMEM, SMEM, VMEM, VMEM, ANY],
+        in_specs=[SMEM, SMEM, VMEM, VMEM, VMEM, ANY],
         out_specs=VMEM,
         out_shape=jax.ShapeDtypeStruct((source.shape[0],) + spread.shape[1:], jnp.float32),
         scratch_shapes=[pltpu.SemaphoreType.DMA],
         compiler_params=PARAMS,
         name="collect",
-    )(source, crowded, spread, arrived, extra)
+    )(source, flags, spread, first, second, extra)
 
 
 def fetch_items(cuts, ids):
@@ -171,9 +175,15 @@
     half = (lax.axis_index("node") // group).astype(jnp.int32).reshape(1)
     halves = [[h * group + i for i in range(group)] for h in range(2)]
     swap = [(i, (i + group) % devices) for i in range(devices)]
+    outer = [i < group // 2 or i >= devices - group // 2 for i in range(devices)]
+    outer_swap = [pair for pair in swap if outer[pair[0]]]
+    inner_swap = [pair for pair in swap if not outer[pair[0]]]
+    index = lax.axis_index("node")
+    is_outer = (index < group // 2) | (index >= devices - group // 2)
     count = group * cuts[0].shape[1]
     room = min(count, max(8, int(count * CROSS_SHARE)))
     send, source, crowded = make_plan(half, ids.reshape(-1), count, room)
+    flags = jnp.concatenate([crowded, is_outer.astype(jnp.int32).reshape(1)])
 
     def exchange(x):
         return lax.all_to_all(x, "node", 0, 0, axis_index_groups=halves, tiled=True)
@@ -183,14 +193,15 @@
         spread = exchange(cut)
         spread = spread.reshape((count,) + spread.shape[2:])
         leaving = pick_leaving(send, spread, room)
-        arrived = lax.ppermute(leaving, "node", swap)
+        first = lax.ppermute(leaving, "node", outer_swap)
+        second = lax.ppermute(leaving, "node", inner_swap)
         extra = lax.cond(
             crowded[0] > 0,
             lambda x: lax.ppermute(x, "node", swap),
             jnp.zeros_like,
             spread,
         )
-        picked = collect(source, crowded, spread, arrived, extra)
+        picked = collect(source, flags, spread, first, second, extra)
         picked = picked.reshape((group, ids.shape[1]) + picked.shape[1:])
         delivered.append(exchange(picked))
     return delivered

time: 242 us -> 243 us (level)
  starting transfers between devices: 28 us -> 37.6 us
  waiting for transfers between devices: 169 us -> 161 us
    ppermute x2 -> x4, starting transfers between devices: 6.03 us -> 15.6 us  [the longest x2 13 us: fetch_items(): first = lax.ppermute(leaving, 'node', outer_swap)]
    ppermute x2 -> x4, waiting for transfers between devices: 97.7 us -> 89.3 us  [the longest x2 53.2 us: fetch_items(): second = lax.ppermute(leaving, 'node', inner_swap)]
  transfers between devices with their start and end apart: 6 -> 8, of which waited for: 4 -> 5; matrix products, arithmetic and copies ran while one was open for 3% -> 3% of each run, Pallas kernels for 10% -> 9%
where the time goes in v4:
time: 243 us; the launch traced here: 242 us
  waiting for transfers between devices  161 us (66%)
  starting transfers between devices  37.6 us (15%)
  Pallas kernels  35.1 us (14%)
  local copies, waits for them, and re-layouts  7.01 us (3%)
    all_to_all x4, waiting for transfers between devices, exchange(): return lax.all_to_all(x, 'node', 0, 0, axis_index_groups=halves, tiled=True)  71.3 us
    ppermute x2, waiting for transfers between devices, fetch_items(): second = lax.ppermute(leaving, 'node', inner_swap)  53.2 us
    ppermute x2, waiting for transfers between devices, fetch_items(): first = lax.ppermute(leaving, 'node', outer_swap)  36.1 us
    all_to_all x4, starting transfers between devices, exchange(): return lax.all_to_all(x, 'node', 0, 0, axis_index_groups=halves, tiled=True)  22 us
    ppermute x2, starting transfers between devices, fetch_items(): first = lax.ppermute(leaving, 'node', outer_swap)  13 us
    pallas_call x1, Pallas kernels, chain(): pl.pallas_call(chain_kernel, grid_spec=pltpu.PrefetchScalarGridSpec(num_s...  9.48 us
    pallas_call x2, Pallas kernels, collect(): pl.pallas_call(collect_kernel, in_specs=[SMEM, SMEM, VMEM, VMEM, VMEM, AN...  9.25 us
    pallas_call x1, Pallas kernels, make_plan(): pl.pallas_call(functools.partial(plan_kernel, room), in_specs=[SMEM] * 2,...  6.59 us
  transfers between devices with their start and end apart: 8, of which 5 were waited for; matrix products, arithmetic and copies ran while one was open for 3% of the time, Pallas kernels for 9%

profile of v4, /device:TPU:0, one launch (start us, length us, event | category | flops | bytes accessed | tf_op | source)
XLA Modules:
  0.0 241.9 jit_solution(16655942996221305656)
XLA Ops:
  0.0 2.7 %cut_rows.2 = f32[16,8,2,16,128]{4,3,2,1,0:T(8,128)} custom-call(f32[8,2,256,256]{3,2,1,0:T(8,128)} %node_ref.1), custom_call_target="tpu_custom_call" | custom-call | tf_op jit(solution)/shard_map/cut_rows/pallas_call | solution.py:33
  2.7 6.3 %all-to-all-start = ((f32[16,8,2,16,128]{4,3,2,1,0:T(8,128)}), f32[16,8,2,16,128]{4,3,2,1,0:T(8,128)S(1)}, u32[]{:S(2)}, u32[]{:S(2)}) async-start(f32[16,8,2,16,128]{4,3,2,1,0:T(8,128)} %cut_rows.2), calls=%async_computation | async-start | bytes 4194304 | tf_op jit(solution)/shard_map/all_to_all | solution.py:189
  9.0 2.7 %cut_rows.3 = f32[16,8,2,16,128]{4,3,2,1,0:T(8,128)} custom-call(f32[8,2,256,256]{3,2,1,0:T(8,128)} %node_ref.1), custom_call_target="tpu_custom_call" | custom-call | tf_op jit(solution)/shard_map/cut_rows/pallas_call | solution.py:33
  11.7 26.4 %all-to-all-done = f32[16,8,2,16,128]{4,3,2,1,0:T(8,128)S(1)} async-done(((f32[16,8,2,16,128]{4,3,2,1,0:T(8,128)}), f32[16,8,2,16,128]{4,3,2,1,0:T(8,128)S(1)}, u32[]{:S(2)}, u32[]{:S(2)}) %all-to-all-start) | async-done | bytes 2097184 | tf_op jit(solution)/shard_map/all_to_all | solution.py:189
  38.1 5.0 %all-to-all-start.2 = ((f32[16,8,2,16,128]{4,3,2,1,0:T(8,128)}), f32[16,8,2,16,128]{4,3,2,1,0:T(8,128)}, u32[]{:S(2)}, u32[]{:S(2)}) async-start(f32[16,8,2,16,128]{4,3,2,1,0:T(8,128)} %cut_rows.3), calls=%async_computation.2 | async-start | bytes 4194304 | tf_op jit(solution)/shard_map/all_to_all | solution.py:189
  43.2 0.1 reshape.59
  43.5 0.1 reshape.51
  43.6 1.9 gather_fusion
  45.6 0.1 reshape.50
  45.7 0.7 gather_fusion.1
  46.7 0.2 reshape_reshape.3.ids_ref
  46.9 6.6 %make_plan.1 = (s32[128]{0:T(128)S(1)}, s32[192]{0:T(256)S(1)}, s32[1]{0:T(128)}) custom-call(s32[1]{0:T(128)} %bitcast.half_ref, s32[384]{0:T(512)S(1)} %reshape_reshape.3.ids_ref), custom_call_target="tpu_custom_call" | custom-call | tf_op jit(solution)/shard_map/make_plan/pallas_call | solution.py:94
  53.5 1.7 pick_leaving.2
  55.2 1.3 collective-permute-start.3
  56.5 5.6 %collective-permute-start.2 = (f32[58,2,16,128]{3,2,1,0:T(8,128)S(1)}, f32[58,2,16,128]{3,2,1,0:T(8,128)S(1)}, u32[]{:S(2)}, u32[]{:S(2)}) collective-permute-start(f32[58,2,16,128]{3,2,1,0:T(8,128)S(1)} %pick_leaving.2), channel_id=1, source_target_pairs={{0,16},{1,17},{2,18},{3,19},{4,20},{5,21},{6,22},{7,23},{24,8},{25... | collective-permute-start | bytes 2850824 | tf_op jit(solution)/shard_map/ppermute | solution.py:196
  62.7 0.6 pad_add_fusion.flags_ref
  63.3 1.6 conditional.2
  63.3 1.6 broadcast.9
  64.9 36.9 %collective-permute-done.3.second_ref = f32[58,2,16,128]{3,2,1,0:T(8,128)S(1)} collective-permute-done((f32[58,2,16,128]{3,2,1,0:T(8,128)S(1)}, f32[58,2,16,128]{3,2,1,0:T(8,128)S(1)}, u32[]{:S(2)}, u32[]{:S(2)}) %collective-permute-start.3) | collective-permute-done | bytes 950304 | tf_op jit(solution)/shard_map/ppermute | solution.py:197
  101.7 4.4 %collect.2 = f32[192,2,16,128]{3,2,1,0:T(8,128)} custom-call(s32[192]{0:T(256)S(1)} %get-tuple-element.16.source_ref, s32[2]{0:T(128)S(1)} %pad_add_fusion.flags_ref, f32[128,2,16,128]{3,2,1,0:T(8,128)} %bitcast.10, f32[58,2,16,128]{3,2,1,0:T(8,128)S(1)} %collective-permute-done.2.first_ref, f32[58,2,16,128]{3,2,1,0:T(8,128)S(1)} %collective-permute-done.3.second_ref, ...), custom_call_target="tpu_custom_call" | custom-call | tf_op jit(solution)/shard_map/collect/pallas_call | solution.py:161
  106.1 4.0 %all-to-all-start.1 = ((f32[16,12,2,16,128]{4,3,2,1,0:T(8,128)}), f32[16,12,2,16,128]{4,3,2,1,0:T(8,128)S(1)}, u32[]{:S(2)}, u32[]{:S(2)}) async-start(f32[16,12,2,16,128]{4,3,2,1,0:T(8,128)} %bitcast.4), calls=%async_computation.1 | async-start | bytes 6291456 | tf_op jit(solution)/shard_map/all_to_all | solution.py:189
  110.2 2.6 %pick_leaving.3 = f32[58,2,16,128]{3,2,1,0:T(8,128)} custom-call(s32[128]{0:T(128)S(1)} %get-tuple-element.18.send_ref, f32[128,2,16,128]{3,2,1,0:T(8,128)} %bitcast.5.spread_ref), custom_call_target="tpu_custom_call" | custom-call | tf_op jit(solution)/shard_map/pick_leaving/pallas_call | solution.py:118
  112.8 1.3 collective-permute-start.5
  114.1 7.5 %collective-permute-start.4 = (f32[58,2,16,128]{3,2,1,0:T(8,128)}, f32[58,2,16,128]{3,2,1,0:T(8,128)}, u32[]{:S(2)}, u32[]{:S(2)}) collective-permute-start(f32[58,2,16,128]{3,2,1,0:T(8,128)} %pick_leaving.3), channel_id=1, source_target_pairs={{0,16},{1,17},{2,18},{3,19},{4,20},{5,21},{6,22},{7,23},{24,8},{25... | collective-permute-start | bytes 2850824 | tf_op jit(solution)/shard_map/ppermute | solution.py:196
  121.6 1.6 conditional.3
  121.6 1.6 broadcast.10
  123.2 16.3 %collective-permute-done.5.second_ref = f32[58,2,16,128]{3,2,1,0:T(8,128)} collective-permute-done((f32[58,2,16,128]{3,2,1,0:T(8,128)}, f32[58,2,16,128]{3,2,1,0:T(8,128)}, u32[]{:S(2)}, u32[]{:S(2)}) %collective-permute-start.5) | collective-permute-done | bytes 950304 | tf_op jit(solution)/shard_map/ppermute | solution.py:197
  139.5 36.1 %collective-permute-done.4.first_ref = f32[58,2,16,128]{3,2,1,0:T(8,128)} collective-permute-done((f32[58,2,16,128]{3,2,1,0:T(8,128)}, f32[58,2,16,128]{3,2,1,0:T(8,128)}, u32[]{:S(2)}, u32[]{:S(2)}) %collective-permute-start.4) | collective-permute-done | bytes 950304 | tf_op jit(solution)/shard_map/ppermute | solution.py:196
  175.6 4.9 %collect.3 = f32[192,2,16,128]{3,2,1,0:T(8,128)} custom-call(s32[192]{0:T(256)S(1)} %get-tuple-element.16.source_ref, s32[2]{0:T(128)S(1)} %pad_add_fusion.flags_ref, f32[128,2,16,128]{3,2,1,0:T(8,128)} %bitcast.5.spread_ref, f32[58,2,16,128]{3,2,1,0:T(8,128)} %collective-permute-done.4.first_ref, f32[58,2,16,128]{3,2,1,0:T(8,128)} %collective-permute-done.5.second_ref, ...), custom_call_target="tpu_custom_call" | custom-call | tf_op jit(solution)/shard_map/collect/pallas_call | solution.py:161
  180.5 6.7 %all-to-all-start.3 = ((f32[16,12,2,16,128]{4,3,2,1,0:T(8,128)}), f32[16,12,2,16,128]{4,3,2,1,0:T(8,128)}, u32[]{:S(2)}, u32[]{:S(2)}) async-start(f32[16,12,2,16,128]{4,3,2,1,0:T(8,128)} %bitcast.6), calls=%async_computation.3 | async-start | bytes 6291456 | tf_op jit(solution)/shard_map/all_to_all | solution.py:189
  187.5 44.9 %all-to-all-done.3.refs_1_ = f32[16,12,2,16,128]{4,3,2,1,0:T(8,128)} async-done(((f32[16,12,2,16,128]{4,3,2,1,0:T(8,128)}), f32[16,12,2,16,128]{4,3,2,1,0:T(8,128)}, u32[]{:S(2)}, u32[]{:S(2)}) %all-to-all-start.3) | async-done | bytes 3145760 | tf_op jit(solution)/shard_map/all_to_all | solution.py:189
  232.4 9.5 %chain.1 = f32[2,2,256,256]{3,2,1,0:T(8,128)} custom-call(s32[4]{0:T(128)S(1)} %subtract_reduce_fusion.slot, s32[4]{0:T(128)S(1)} %dynamic-slice_subtract_fusion.target, s32[4]{0:T(128)S(1)} %dynamic_slice.12.sign, f32[8,2,256,256]{3,2,1,0:T(8,128)} %node_ref.1, f32[16,12,2,16,128]{4,3,2,1,0:T(8,128)S(1)} %all-to-all-done.1.refs_0_, ...), custom_call_target="tpu_custom_call" | custom-call | tf_op jit(solution)/shard_map/chain/pallas_call | solution.py:326
  (26 shorter events, 0.7 us)
Async XLA Ops:
  0.0 43.6 %copy-start = (s32[256]{0:T(256)S(1)}, s32[256]{0:T(256)}, u32[]{:S(2)}) copy-start(s32[256]{0:T(256)} %param.11) | copy-start | bytes 3076
  2.7 35.4 %all-to-all-start = ((f32[16,8,2,16,128]{4,3,2,1,0:T(8,128)}), f32[16,8,2,16,128]{4,3,2,1,0:T(8,128)S(1)}, u32[]{:S(2)}, u32[]{:S(2)}) async-start(f32[16,8,2,16,128]{4,3,2,1,0:T(8,128)} %cut_rows.2), calls=%async_computation | async-start | bytes 4194304 | tf_op jit(solution)/shard_map/all_to_all | solution.py:189
  11.7 31.3 %copy-start.2 = (s32[128,2]{0,1:T(2,128)S(1)}, s32[128,2]{0,1:T(2,128)}, u32[]{:S(2)}) copy-start(s32[128,2]{0,1:T(2,128)} %param.13) | copy-start | bytes 3076
  11.7 31.6 %copy-start.3 = (s32[128,2]{0,1:T(2,128)S(1)}, s32[128,2]{0,1:T(2,128)}, u32[]{:S(2)}) copy-start(s32[128,2]{0,1:T(2,128)} %param.12) | copy-start | bytes 3076
  38.1 5.0 %copy-start.1 = (f32[16,8,2,16,128]{4,3,2,1,0:T(8,128)}, f32[16,8,2,16,128]{4,3,2,1,0:T(8,128)S(1)}, u32[]{:S(2)}) copy-start(f32[16,8,2,16,128]{4,3,2,1,0:T(8,128)S(1)} %all-to-all-done) | copy-start | bytes 6291460
  38.1 68.1 %all-to-all-start.2 = ((f32[16,8,2,16,128]{4,3,2,1,0:T(8,128)}), f32[16,8,2,16,128]{4,3,2,1,0:T(8,128)}, u32[]{:S(2)}, u32[]{:S(2)}) async-start(f32[16,8,2,16,128]{4,3,2,1,0:T(8,128)} %cut_rows.3), calls=%async_computation.2 | async-start | bytes 4194304 | tf_op jit(solution)/shard_map/all_to_all | solution.py:189
  55.2 46.5 %collective-permute-start.3 = (f32[58,2,16,128]{3,2,1,0:T(8,128)S(1)}, f32[58,2,16,128]{3,2,1,0:T(8,128)S(1)}, u32[]{:S(2)}, u32[]{:S(2)}) collective-permute-start(f32[58,2,16,128]{3,2,1,0:T(8,128)S(1)} %pick_leaving.2), channel_id=1, source_target_pairs={{8,24},{9,25},{10,26},{11,27},{12,28},{13,29},{14,30},{15,31},{16,... | collective-permute-start | bytes 2850824 | tf_op jit(solution)/shard_map/ppermute | solution.py:197
  56.5 45.2 %collective-permute-start.2 = (f32[58,2,16,128]{3,2,1,0:T(8,128)S(1)}, f32[58,2,16,128]{3,2,1,0:T(8,128)S(1)}, u32[]{:S(2)}, u32[]{:S(2)}) collective-permute-start(f32[58,2,16,128]{3,2,1,0:T(8,128)S(1)} %pick_leaving.2), channel_id=1, source_target_pairs={{0,16},{1,17},{2,18},{3,19},{4,20},{5,21},{6,22},{7,23},{24,8},{25... | collective-permute-start | bytes 2850824 | tf_op jit(solution)/shard_map/ppermute | solution.py:196
  106.1 74.4 %all-to-all-start.1 = ((f32[16,12,2,16,128]{4,3,2,1,0:T(8,128)}), f32[16,12,2,16,128]{4,3,2,1,0:T(8,128)S(1)}, u32[]{:S(2)}, u32[]{:S(2)}) async-start(f32[16,12,2,16,128]{4,3,2,1,0:T(8,128)} %bitcast.4), calls=%async_computation.1 | async-start | bytes 6291456 | tf_op jit(solution)/shard_map/all_to_all | solution.py:189
  112.8 26.7 %collective-permute-start.5 = (f32[58,2,16,128]{3,2,1,0:T(8,128)}, f32[58,2,16,128]{3,2,1,0:T(8,128)}, u32[]{:S(2)}, u32[]{:S(2)}) collective-permute-start(f32[58,2,16,128]{3,2,1,0:T(8,128)} %pick_leaving.3), channel_id=1, source_target_pairs={{8,24},{9,25},{10,26},{11,27},{12,28},{13,29},{14,30},{15,31},{16,... | collective-permute-start | bytes 2850824 | tf_op jit(solution)/shard_map/ppermute | solution.py:197
  114.1 61.5 %collective-permute-start.4 = (f32[58,2,16,128]{3,2,1,0:T(8,128)}, f32[58,2,16,128]{3,2,1,0:T(8,128)}, u32[]{:S(2)}, u32[]{:S(2)}) collective-permute-start(f32[58,2,16,128]{3,2,1,0:T(8,128)} %pick_leaving.3), channel_id=1, source_target_pairs={{0,16},{1,17},{2,18},{3,19},{4,20},{5,21},{6,22},{7,23},{24,8},{25... | collective-permute-start | bytes 2850824 | tf_op jit(solution)/shard_map/ppermute | solution.py:196
  180.5 6.7 %copy-start.5 = (s32[128]{0:T(128)S(1)}, s32[128]{0:T(128)}, u32[]{:S(2)}) copy-start(s32[128]{0:T(128)} %param.15) | copy-start | bytes 1540
  180.5 6.9 %copy-start.4 = (s32[128]{0:T(128)S(1)}, s32[128]{0:T(128)}, u32[]{:S(2)}) copy-start(s32[128]{0:T(128)} %param.14) | copy-start | bytes 1540
  180.5 51.9 %all-to-all-start.3 = ((f32[16,12,2,16,128]{4,3,2,1,0:T(8,128)}), f32[16,12,2,16,128]{4,3,2,1,0:T(8,128)}, u32[]{:S(2)}, u32[]{:S(2)}) async-start(f32[16,12,2,16,128]{4,3,2,1,0:T(8,128)} %bitcast.6), calls=%async_computation.3 | async-start | bytes 6291456 | tf_op jit(solution)/shard_map/all_to_all | solution.py:189

commit v5 on v3

--- a/solution.py
+++ b/solution.py
@@ -165,7 +165,56 @@
     )(source, crowded, spread, arrived, extra)
 
 
-def fetch_items(cuts, ids):
+def partner(index, k, group):
+    return index ^ k if group & (group - 1) == 0 else (k - index + group) % group
+
+
+def scatter_kernel(source_ref, flags_ref, spread_ref, arrived_ref, extra_ref, *refs):
+    out_refs, sem = refs[:-1], refs[-1]
+    count, room = spread_ref.shape[0], arrived_ref.shape[0]
+    wanted = out_refs[0].shape[0]
+    for k, out_ref in enumerate(out_refs):
+        base = partner(flags_ref[1], k, len(out_refs)) * wanted
+
+        def copy(q, carry, base=base, out_ref=out_ref):
+            source = source_ref[base + q]
+            near = jnp.minimum(source, count - 1)
+            far = jnp.clip(source - count, 0, room - 1)
+            out_ref[q] = jnp.where(source < count, spread_ref[near], arrived_ref[far])
+            return carry
+
+        lax.fori_loop(0, wanted, copy, 0, unroll=4)
+
+        @pl.when(flags_ref[0] > 0)
+        def _(base=base, out_ref=out_ref):
+            def fetch(q, carry):
+                source = source_ref[base + q] - (count + room)
+
+                @pl.when(source >= 0)
+                def _():
+                    slow = pltpu.make_async_copy(extra_ref.at[source], out_ref.at[q], sem)
+                    slow.start()
+                    slow.wait()
+
+                return carry
+
+            lax.fori_loop(0, wanted, fetch, 0)
+
+
+def scatter(source, flags, spread, arrived, extra, group):
+    shape = (source.shape[0] // group,) + spread.shape[1:]
+    return pl.pallas_call(
+        scatter_kernel,
+        in_specs=[SMEM, SMEM, VMEM, VMEM, ANY],
+        out_specs=[VMEM] * group,
+        out_shape=[jax.ShapeDtypeStruct(shape, jnp.float32)] * group,
+        scratch_shapes=[pltpu.SemaphoreType.DMA],
+        compiler_params=PARAMS,
+        name="scatter",
+    )(source, flags, spread, arrived, extra)
+
+
+def fetch_items(cuts, ids, pairwise):
     devices = lax.axis_size("node")
     group = devices // 2
     half = (lax.axis_index("node") // group).astype(jnp.int32).reshape(1)
@@ -179,7 +228,7 @@
         return lax.all_to_all(x, "node", 0, 0, axis_index_groups=halves, tiled=True)
 
     delivered = []
-    for cut in cuts:
+    for c, cut in enumerate(cuts):
         spread = exchange(cut)
         spread = spread.reshape((count,) + spread.shape[2:])
         leaving = pick_leaving(send, spread, room)
@@ -190,6 +239,20 @@
             jnp.zeros_like,
             spread,
         )
+        if pairwise and c == len(cuts) - 1:
+            member = (lax.axis_index("node") % group).astype(jnp.int32).reshape(1)
+            flags = jnp.concatenate([crowded, member])
+            sent = scatter(source, flags, spread, arrived, extra, group)
+            got = []
+            for k in range(group):
+                pairs = [
+                    (i, i // group * group + partner(i % group, k, group))
+                    for i in range(devices)
+                ]
+                still = all(i == j for i, j in pairs)
+                got.append(sent[k] if still else lax.ppermute(sent[k], "node", pairs))
+            delivered.append(got)
+            continue
         picked = collect(source, crowded, spread, arrived, extra)
         picked = picked.reshape((group, ids.shape[1]) + picked.shape[1:])
         delivered.append(exchange(picked))
@@ -301,32 +364,43 @@
     )(target, sign, lefts, *rights)
 
 
-def chain_kernel(slot, target, sign, node_ref, *refs):
-    right_refs, out_ref = refs[:-1], refs[-1]
+def chain_kernel(parts, member, slot, target, sign, node_ref, *refs):
+    part_refs, got_refs, (out_ref, last_ref) = refs[:parts], refs[parts:-2], refs[-2:]
+    for k, ref in enumerate(got_refs):
+        rows = ref.shape[2]
+        row = pl.multiple_of(partner(member[0], k, len(got_refs)) * rows, rows)
+        for which in range(3):
+            last_ref[which, 0, :, pl.ds(row, rows)] = ref[which]
     left = wide(node_ref)
     for which in range(3):
-        left = product(left, [ref[:, which] for ref in right_refs])
+        blocks = [ref[:, which] for ref in part_refs] + [last_ref[which]]
+        left = product(left, blocks)
     add_result(pl.program_id(0), target, sign, left, out_ref)
 
 
-def chain(slot, target, sign, nodes, rights):
+def chain(member, slot, target, sign, nodes, rights):
     order = nodes.shape[2]
     whole = (RES_COL, 2, order, order)
-    return pl.pallas_call(
-        chain_kernel,
+    *parts, got = rights
+    _, _, rows, width = got[0].shape
+
+    return pl.pallas_call(
+        functools.partial(chain_kernel, len(parts)),
         grid_spec=pltpu.PrefetchScalarGridSpec(
-            num_scalar_prefetch=3,
+            num_scalar_prefetch=4,
             grid=(slot.shape[0],),
             in_specs=[
-                pl.BlockSpec((1, 2, order, order), lambda k, slot, t, s: (slot[k], 0, 0, 0)),
-                *[triple_spec(right) for right in rights],
+                pl.BlockSpec((1, 2, order, order), lambda k, m, slot, t, s: (slot[k], 0, 0, 0)),
+                *[triple_spec(part) for part in parts],
+                *[pl.BlockSpec((3, 2, rows, width), lambda k, *scalars: (k, 0, 0, 0))] * len(got),
             ],
-            out_specs=pl.BlockSpec(whole, lambda k, slot, t, s: (0, 0, 0, 0)),
+            out_specs=pl.BlockSpec(whole, lambda k, *scalars: (0, 0, 0, 0)),
+            scratch_shapes=[pltpu.VMEM((3, 1, 2, order, width), jnp.float32)],
         ),
         out_shape=jax.ShapeDtypeStruct(whole, jnp.float32),
         compiler_params=CHAIN,
         name="chain",
-    )(slot, target, sign, nodes, *rights)
+    )(member, slot, target, sign, nodes, *parts, *got)
 
 
 def all_columns(x):
@@ -346,7 +420,8 @@
 
     slots = node_slot[pair_list]
     slots = slots[second_list].reshape(devices, second_col, 4)
-    rights = fetch_items(cuts, slots[:, :, 1:].reshape(devices, second_col * 3))
+    pairwise = lax.axis_size("pair") == 1
+    rights = fetch_items(cuts, slots[:, :, 1:].reshape(devices, second_col * 3), pairwise)
 
     own_slots = lax.dynamic_index_in_dim(slots[:, :, 0], column, 0, keepdims=False)
     own_slots = own_slots - column * node_col
@@ -354,8 +429,9 @@
     own_targets = lax.dynamic_slice_in_dim(targets, column * second_col, second_col, 0)
     own_targets = own_targets - column * RES_COL
 
-    if lax.axis_size("pair") == 1:
-        return chain(own_slots, own_targets, own_signs, node_blocks, rights)
+    if pairwise:
+        member = (column % group).astype(jnp.int32).reshape(1)
+        return chain(member, own_slots, own_targets, own_signs, node_blocks, rights)
     same = jnp.arange(second_col, dtype=jnp.int32)
     products = multiply(own_slots, all_columns(node_blocks), rights, 0)
     longer = multiply(same, all_columns(products), rights, 1)

time: 242 us -> 251 us (1.037)
  waiting for transfers between devices: 169 us -> 150 us
  local copies, waits for them, and re-layouts: 7.02 us -> 21.5 us
  starting transfers between devices: 28 us -> 40.9 us
    all_to_all x4 -> x3, waiting for transfers between devices: 71.3 us -> 26.4 us  [exchange(): return lax.all_to_all(x, 'node', 0, 0, axis_index_groups=halves, tiled=True)]
    ppermute x0 -> x15, waiting for transfers between devices: none -> 26.2 us  [fetch_items(): got.append(sent[k] if still else lax.ppermute(sent[k], 'node', pairs))]
    ppermute x0 -> x15, starting transfers between devices: none -> 19.5 us  [fetch_items(): got.append(sent[k] if still else lax.ppermute(sent[k], 'node', pairs))]
    unnamed x12 -> x48, local copies, waits for them, and re-layouts: 0.03 us -> 14.5 us
    all_to_all x4 -> x3, starting transfers between devices: 22 us -> 15.3 us  [exchange(): return lax.all_to_all(x, 'node', 0, 0, axis_index_groups=halves, tiled=True)]
    pallas_call x2 -> x1, Pallas kernels: 10 us -> 4.88 us  [collect(): pl.pallas_call(collect_kernel, in_specs=[SMEM, SMEM, VMEM, VMEM, ANY], ou...]
    pallas_call x1 -> x2, Pallas kernels: 9.5 us -> 13.7 us  [the longest x1 9.49 us: chain(): pl.pallas_call(functools.partial(chain_kernel, len(parts)), grid_spec=plt...]
  transfers between devices with their start and end apart: 6 -> 20, of which waited for: 4 -> 11; matrix products, arithmetic and copies ran while one was open for 3% -> 4% of each run, Pallas kernels for 10% -> 9%
where the time goes in v5:
time: 251 us; the launch traced here: 250 us
  waiting for transfers between devices  150 us (60%)
  starting transfers between devices  40.9 us (16%)
  Pallas kernels  34.8 us (14%)
  local copies, waits for them, and re-layouts  21.5 us (9%)
    ppermute x2, waiting for transfers between devices, fetch_items(): arrived = lax.ppermute(leaving, 'node', swap)  97 us
    all_to_all x3, waiting for transfers between devices, exchange(): return lax.all_to_all(x, 'node', 0, 0, axis_index_groups=halves, tiled=True)  26.4 us
    ppermute x15, waiting for transfers between devices, fetch_items(): got.append(sent[k] if still else lax.ppermute(sent[k], 'node', pairs))  26.2 us
    ppermute x15, starting transfers between devices, fetch_items(): got.append(sent[k] if still else lax.ppermute(sent[k], 'node', pairs))  19.5 us
    all_to_all x3, starting transfers between devices, exchange(): return lax.all_to_all(x, 'node', 0, 0, axis_index_groups=halves, tiled=True)  15.3 us
    unnamed x48, local copies, waits for them, and re-layouts  14.5 us
    pallas_call x1, Pallas kernels, chain(): pl.pallas_call(functools.partial(chain_kernel, len(parts)), grid_spec=plt...  9.49 us
    pallas_call x1, Pallas kernels, make_plan(): pl.pallas_call(functools.partial(plan_kernel, room), in_specs=[SMEM] * 2,...  6.59 us
  transfers between devices with their start and end apart: 20, of which 11 were waited for; matrix products, arithmetic and copies ran while one was open for 4% of the time, Pallas kernels for 9%

profile of v5, /device:TPU:0, one launch (start us, length us, event | category | flops | bytes accessed | tf_op | source)
XLA Modules:
  0.0 249.9 jit_solution(13663579266893460006)
XLA Ops:
  0.0 2.7 %cut_rows.2 = f32[16,8,2,16,128]{4,3,2,1,0:T(8,128)} custom-call(f32[8,2,256,256]{3,2,1,0:T(8,128)} %node_ref.1), custom_call_target="tpu_custom_call" | custom-call | tf_op jit(solution)/shard_map/cut_rows/pallas_call | solution.py:33
  2.7 6.3 %all-to-all-start = ((f32[16,8,2,16,128]{4,3,2,1,0:T(8,128)}), f32[16,8,2,16,128]{4,3,2,1,0:T(8,128)S(1)}, u32[]{:S(2)}, u32[]{:S(2)}) async-start(f32[16,8,2,16,128]{4,3,2,1,0:T(8,128)} %cut_rows.2), calls=%async_computation | async-start | bytes 4194304 | tf_op jit(solution)/shard_map/all_to_all | solution.py:228
  9.0 2.7 %cut_rows.3 = f32[16,8,2,16,128]{4,3,2,1,0:T(8,128)} custom-call(f32[8,2,256,256]{3,2,1,0:T(8,128)} %node_ref.1), custom_call_target="tpu_custom_call" | custom-call | tf_op jit(solution)/shard_map/cut_rows/pallas_call | solution.py:33
  11.7 26.4 %all-to-all-done = f32[16,8,2,16,128]{4,3,2,1,0:T(8,128)S(1)} async-done(((f32[16,8,2,16,128]{4,3,2,1,0:T(8,128)}), f32[16,8,2,16,128]{4,3,2,1,0:T(8,128)S(1)}, u32[]{:S(2)}, u32[]{:S(2)}) %all-to-all-start) | async-done | bytes 2097184 | tf_op jit(solution)/shard_map/all_to_all | solution.py:228
  38.1 5.0 %all-to-all-start.2 = ((f32[16,8,2,16,128]{4,3,2,1,0:T(8,128)}), f32[16,8,2,16,128]{4,3,2,1,0:T(8,128)}, u32[]{:S(2)}, u32[]{:S(2)}) async-start(f32[16,8,2,16,128]{4,3,2,1,0:T(8,128)} %cut_rows.3), calls=%async_computation.2 | async-start | bytes 4194304 | tf_op jit(solution)/shard_map/all_to_all | solution.py:228
  43.6 1.9 gather_fusion
  46.9 6.6 %make_plan.1 = (s32[128]{0:T(128)S(1)}, s32[192]{0:T(256)S(1)}, s32[1]{0:T(128)}) custom-call(s32[1]{0:T(128)} %bitcast.1.half_ref, s32[384]{0:T(512)S(1)} %reshape_reshape.3.ids_ref), custom_call_target="tpu_custom_call" | custom-call | tf_op jit(solution)/shard_map/make_plan/pallas_call | solution.py:94
  53.5 1.7 pick_leaving.2
  55.2 2.7 %collective-permute-start.2 = (f32[58,2,16,128]{3,2,1,0:T(8,128)S(1)}, f32[58,2,16,128]{3,2,1,0:T(8,128)S(1)}, u32[]{:S(2)}, u32[]{:S(2)}) collective-permute-start(f32[58,2,16,128]{3,2,1,0:T(8,128)S(1)} %pick_leaving.2), channel_id=1, source_target_pairs={{0,16},{1,17},{2,18},{3,19},{4,20},{5,21},{6,22},{7,23},{8,24},{9,... | collective-permute-start | bytes 2850824 | tf_op jit(solution)/shard_map/ppermute | solution.py:235
  58.5 1.6 conditional.2
  60.1 39.8 %collective-permute-done.2.arrived_ref = f32[58,2,16,128]{3,2,1,0:T(8,128)S(1)} collective-permute-done((f32[58,2,16,128]{3,2,1,0:T(8,128)S(1)}, f32[58,2,16,128]{3,2,1,0:T(8,128)S(1)}, u32[]{:S(2)}, u32[]{:S(2)}) %collective-permute-start.2) | collective-permute-done | bytes 950304 | tf_op jit(solution)/shard_map/ppermute | solution.py:235
  99.9 4.9 %collect.1 = f32[192,2,16,128]{3,2,1,0:T(8,128)} custom-call(s32[192]{0:T(256)S(1)} %get-tuple-element.32.source_ref, s32[1]{0:T(128)} %get-tuple-element.33.crowded_ref, f32[128,2,16,128]{3,2,1,0:T(8,128)} %bitcast.9, f32[58,2,16,128]{3,2,1,0:T(8,128)S(1)} %collective-permute-done.2.arrived_ref, f32[128,2,16,128]{3,2,1,0:T(8,128)} %get-tuple-element.51.extra_ref), custom_call_target="tpu_custom_call" | custom-call | tf_op jit(solution)/shard_map/collect/pallas_call | solution.py:157
  104.8 4.0 %all-to-all-start.1 = ((f32[16,12,2,16,128]{4,3,2,1,0:T(8,128)}), f32[16,12,2,16,128]{4,3,2,1,0:T(8,128)S(1)}, u32[]{:S(2)}, u32[]{:S(2)}) async-start(f32[16,12,2,16,128]{4,3,2,1,0:T(8,128)} %bitcast.4), calls=%async_computation.1 | async-start | bytes 6291456 | tf_op jit(solution)/shard_map/all_to_all | solution.py:228
  108.9 2.6 %pick_leaving.3 = f32[58,2,16,128]{3,2,1,0:T(8,128)} custom-call(s32[128]{0:T(128)S(1)} %get-tuple-element.34.send_ref, f32[128,2,16,128]{3,2,1,0:T(8,128)} %bitcast.5.spread_ref), custom_call_target="tpu_custom_call" | custom-call | tf_op jit(solution)/shard_map/pick_leaving/pallas_call | solution.py:118
  111.5 3.4 %collective-permute-start.3 = (f32[58,2,16,128]{3,2,1,0:T(8,128)}, f32[58,2,16,128]{3,2,1,0:T(8,128)}, u32[]{:S(2)}, u32[]{:S(2)}) collective-permute-start(f32[58,2,16,128]{3,2,1,0:T(8,128)} %pick_leaving.3), channel_id=1, source_target_pairs={{0,16},{1,17},{2,18},{3,19},{4,20},{5,21},{6,22},{7,23},{8,24},{9,... | collective-permute-start | bytes 2850824 | tf_op jit(solution)/shard_map/ppermute | solution.py:235
  115.6 1.6 conditional.3
  117.2 57.1 %collective-permute-done.3.arrived_ref = f32[58,2,16,128]{3,2,1,0:T(8,128)} collective-permute-done((f32[58,2,16,128]{3,2,1,0:T(8,128)}, f32[58,2,16,128]{3,2,1,0:T(8,128)}, u32[]{:S(2)}, u32[]{:S(2)}) %collective-permute-start.3) | collective-permute-done | bytes 950304 | tf_op jit(solution)/shard_map/ppermute | solution.py:235
  174.3 4.2 %scatter.1 = (f32[12,2,16,128]{3,2,1,0:T(8,128)S(1)}, f32[12,2,16,128]{3,2,1,0:T(8,128)S(1)}, f32[12,2,16,128]{3,2,1,0:T(8,128)S(1)}, f32[12,2,16,128]{3,2,1,0:T...) custom-call(s32[192]{0:T(256)S(1)} %get-tuple-element.32.source_ref,, ...), custom_call_target="tpu_custom_call" | custom-call | tf_op jit(solution)/shard_map/scatter/pallas_call | solution.py:206
  178.7 1.8 collective-permute-start.6
  180.4 1.7 collective-permute-start.8
  182.2 4.2 %collective-permute-done.5.refs_3_ = f32[12,2,16,128]{3,2,1,0:T(8,128)S(1)} collective-permute-done((f32[12,2,16,128]{3,2,1,0:T(8,128)S(1)}, f32[12,2,16,128]{3,2,1,0:T(8,128)S(1)}, u32[]{:S(2)}, u32[]{:S(2)}) %collective-permute-start.5) | collective-permute-done | bytes 196640 | tf_op jit(solution)/shard_map/ppermute | solution.py:253
  187.1 2.4 collective-permute-done.6.refs_4_
  190.2 4.4 %collective-permute-start.11 = (f32[12,2,16,128]{3,2,1,0:T(8,128)S(1)}, f32[12,2,16,128]{3,2,1,0:T(8,128)S(1)}, u32[]{:S(2)}, u32[]{:S(2)}) collective-permute-start(f32[12,2,16,128]{3,2,1,0:T(8,128)S(1)} %get-tuple-element.43), channel_id=1, source_target_pairs={{0,8},{1,9},{2,10},{3,11},{4,12},{5,13},{6,14},{7,15},{8,0},{9,1},... | collective-permute-start | bytes 589832 | tf_op jit(solution)/shard_map/ppermute | solution.py:253
  194.6 2.0 collective-permute-done.7.refs_5_
  197.3 2.3 collective-permute-done.8.refs_6_
  200.3 5.2 %collective-permute-start.13 = (f32[12,2,16,128]{3,2,1,0:T(8,128)S(1)}, f32[12,2,16,128]{3,2,1,0:T(8,128)S(1)}, u32[]{:S(2)}, u32[]{:S(2)}) collective-permute-start(f32[12,2,16,128]{3,2,1,0:T(8,128)S(1)} %get-tuple-element.45), channel_id=1, source_target_pairs={{0,10},{1,11},{2,8},{3,9},{4,14},{5,15},{6,12},{7,13},{8,2},{9,3},... | collective-permute-start | bytes 589832 | tf_op jit(solution)/shard_map/ppermute | solution.py:253
  210.7 2.9 %collective-permute-start.17 = (f32[12,2,16,128]{3,2,1,0:T(8,128)}, f32[12,2,16,128]{3,2,1,0:T(8,128)}, u32[]{:S(2)}, u32[]{:S(2)}) collective-permute-start(f32[12,2,16,128]{3,2,1,0:T(8,128)} %get-tuple-element.49), channel_id=1, source_target_pairs={{0,14},{1,15},{2,12},{3,13},{4,10},{5,11},{6,8},{7,9},{8,6},{9,7},... | collective-permute-start | bytes 589832 | tf_op jit(solution)/shard_map/ppermute | solution.py:253
  216.8 2.6 %collective-permute-done.15.refs_13_ = f32[12,2,16,128]{3,2,1,0:T(8,128)} collective-permute-done((f32[12,2,16,128]{3,2,1,0:T(8,128)}, f32[12,2,16,128]{3,2,1,0:T(8,128)}, u32[]{:S(2)}, u32[]{:S(2)}) %collective-permute-start.15) | collective-permute-done | bytes 196640 | tf_op jit(solution)/shard_map/ppermute | solution.py:253
  219.4 4.2 %collective-permute-done.16.refs_14_ = f32[12,2,16,128]{3,2,1,0:T(8,128)} collective-permute-done((f32[12,2,16,128]{3,2,1,0:T(8,128)}, f32[12,2,16,128]{3,2,1,0:T(8,128)}, u32[]{:S(2)}, u32[]{:S(2)}) %collective-permute-start.16) | collective-permute-done | bytes 196640 | tf_op jit(solution)/shard_map/ppermute | solution.py:253
  223.6 4.7 %collective-permute-done.17.refs_15_ = f32[12,2,16,128]{3,2,1,0:T(8,128)} collective-permute-done((f32[12,2,16,128]{3,2,1,0:T(8,128)}, f32[12,2,16,128]{3,2,1,0:T(8,128)}, u32[]{:S(2)}, u32[]{:S(2)}) %collective-permute-start.17) | collective-permute-done | bytes 196640 | tf_op jit(solution)/shard_map/ppermute | solution.py:253
  228.3 3.7 %collective-permute-done.18.refs_16_ = f32[12,2,16,128]{3,2,1,0:T(8,128)} collective-permute-done((f32[12,2,16,128]{3,2,1,0:T(8,128)}, f32[12,2,16,128]{3,2,1,0:T(8,128)}, u32[]{:S(2)}, u32[]{:S(2)}) %collective-permute-start.18) | collective-permute-done | bytes 196640 | tf_op jit(solution)/shard_map/ppermute | solution.py:253
  240.4 9.5 %chain.1 = f32[2,2,256,256]{3,2,1,0:T(8,128)} custom-call(s32[1]{0:T(128)} %bitcast.member, s32[4]{0:T(128)S(1)} %subtract_reduce_fusion.slot, s32[4]{0:T(128)S(1)} %dynamic-slice_subtract_fusion.target, s32[4]{0:T(128)S(1)} %dynamic_slice.12.sign, f32[8,2,256,256]{3,2,1,0:T(8,128)} %node_ref.1, f32[16,12,2,16,128]{4,3,2,1,0:T(8,128)S(1)} %all-to-all-done.1.refs_0_, ...), custom_call_target="tpu_custom_call" | custom-call | tf_op jit(solution)/shard_map/chain/pallas_call | solution.py:387
  (86 shorter events, 25.3 us)
Async XLA Ops:
  0.0 43.6 %copy-start = (s32[256]{0:T(256)S(1)}, s32[256]{0:T(256)}, u32[]{:S(2)}) copy-start(s32[256]{0:T(256)} %param.11) | copy-start | bytes 3076
  2.7 35.4 %all-to-all-start = ((f32[16,8,2,16,128]{4,3,2,1,0:T(8,128)}), f32[16,8,2,16,128]{4,3,2,1,0:T(8,128)S(1)}, u32[]{:S(2)}, u32[]{:S(2)}) async-start(f32[16,8,2,16,128]{4,3,2,1,0:T(8,128)} %cut_rows.2), calls=%async_computation | async-start | bytes 4194304 | tf_op jit(solution)/shard_map/all_to_all | solution.py:228
  11.7 31.4 %copy-start.21 = (s32[128,2]{0,1:T(2,128)S(1)}, s32[128,2]{0,1:T(2,128)}, u32[]{:S(2)}) copy-start(s32[128,2]{0,1:T(2,128)} %param.13) | copy-start | bytes 3076
  11.7 31.7 %copy-start.22 = (s32[128,2]{0,1:T(2,128)S(1)}, s32[128,2]{0,1:T(2,128)}, u32[]{:S(2)}) copy-start(s32[128,2]{0,1:T(2,128)} %param.12) | copy-start | bytes 3076
  38.1 5.0 %copy-start.19 = (f32[16,8,2,16,128]{4,3,2,1,0:T(8,128)}, f32[16,8,2,16,128]{4,3,2,1,0:T(8,128)S(1)}, u32[]{:S(2)}) copy-start(f32[16,8,2,16,128]{4,3,2,1,0:T(8,128)S(1)} %all-to-all-done) | copy-start | bytes 6291460
  38.1 66.8 %all-to-all-start.2 = ((f32[16,8,2,16,128]{4,3,2,1,0:T(8,128)}), f32[16,8,2,16,128]{4,3,2,1,0:T(8,128)}, u32[]{:S(2)}, u32[]{:S(2)}) async-start(f32[16,8,2,16,128]{4,3,2,1,0:T(8,128)} %cut_rows.3), calls=%async_computation.2 | async-start | bytes 4194304 | tf_op jit(solution)/shard_map/all_to_all | solution.py:228
  46.6 6.9 %copy-start.20 = (s32[32,4,4]{2,1,0:T(4,128)}, s32[32,4,4]{2,1,0:T(4,128)S(1)}, u32[]{:S(2)}) copy-start(s32[32,4,4]{2,1,0:T(4,128)S(1)} %reshape.34) | copy-start | bytes 6148
  55.2 44.7 %collective-permute-start.2 = (f32[58,2,16,128]{3,2,1,0:T(8,128)S(1)}, f32[58,2,16,128]{3,2,1,0:T(8,128)S(1)}, u32[]{:S(2)}, u32[]{:S(2)}) collective-permute-start(f32[58,2,16,128]{3,2,1,0:T(8,128)S(1)} %pick_leaving.2), channel_id=1, source_target_pairs={{0,16},{1,17},{2,18},{3,19},{4,20},{5,21},{6,22},{7,23},{8,24},{9,... | collective-permute-start | bytes 2850824 | tf_op jit(solution)/shard_map/ppermute | solution.py:235
  104.8 127.2 %all-to-all-start.1 = ((f32[16,12,2,16,128]{4,3,2,1,0:T(8,128)}), f32[16,12,2,16,128]{4,3,2,1,0:T(8,128)S(1)}, u32[]{:S(2)}, u32[]{:S(2)}) async-start(f32[16,12,2,16,128]{4,3,2,1,0:T(8,128)} %bitcast.4), calls=%async_computation.1 | async-start | bytes 6291456 | tf_op jit(solution)/shard_map/all_to_all | solution.py:228
  111.5 62.8 %collective-permute-start.3 = (f32[58,2,16,128]{3,2,1,0:T(8,128)}, f32[58,2,16,128]{3,2,1,0:T(8,128)}, u32[]{:S(2)}, u32[]{:S(2)}) collective-permute-start(f32[58,2,16,128]{3,2,1,0:T(8,128)} %pick_leaving.3), channel_id=1, source_target_pairs={{0,16},{1,17},{2,18},{3,19},{4,20},{5,21},{6,22},{7,23},{8,24},{9,... | collective-permute-start | bytes 2850824 | tf_op jit(solution)/shard_map/ppermute | solution.py:235
  117.2 98.1 %copy-start.23 = (s32[128]{0:T(128)S(1)}, s32[128]{0:T(128)}, u32[]{:S(2)}) copy-start(s32[128]{0:T(128)} %param.15) | copy-start | bytes 1540
  178.5 3.6 %collective-permute-start.4 = (f32[12,2,16,128]{3,2,1,0:T(8,128)S(1)}, f32[12,2,16,128]{3,2,1,0:T(8,128)S(1)}, u32[]{:S(2)}, u32[]{:S(2)}) collective-permute-start(f32[12,2,16,128]{3,2,1,0:T(8,128)S(1)} %get-tuple-element.36), channel_id=1, source_target_pairs={{0,1},{1,0},{2,3},{3,2},{4,5},{5,4},{6,7},{7,6},{8,9},{9,8},{10,11... | collective-permute-start | bytes 589832 | tf_op jit(solution)/shard_map/ppermute | solution.py:253
  178.6 7.8 %collective-permute-start.5 = (f32[12,2,16,128]{3,2,1,0:T(8,128)S(1)}, f32[12,2,16,128]{3,2,1,0:T(8,128)S(1)}, u32[]{:S(2)}, u32[]{:S(2)}) collective-permute-start(f32[12,2,16,128]{3,2,1,0:T(8,128)S(1)} %get-tuple-element.37), channel_id=1, source_target_pairs={{0,2},{1,3},{2,0},{3,1},{4,6},{5,7},{6,4},{7,5},{8,10},{9,11},{10,... | collective-permute-start | bytes 589832 | tf_op jit(solution)/shard_map/ppermute | solution.py:253
  178.7 10.9 %collective-permute-start.6 = (f32[12,2,16,128]{3,2,1,0:T(8,128)S(1)}, f32[12,2,16,128]{3,2,1,0:T(8,128)S(1)}, u32[]{:S(2)}, u32[]{:S(2)}) collective-permute-start(f32[12,2,16,128]{3,2,1,0:T(8,128)S(1)} %get-tuple-element.38), channel_id=1, source_target_pairs={{0,3},{1,2},{2,1},{3,0},{4,7},{5,6},{6,5},{7,4},{8,11},{9,10},{10,... | collective-permute-start | bytes 589832 | tf_op jit(solution)/shard_map/ppermute | solution.py:253
  180.4 16.2 %collective-permute-start.7 = (f32[12,2,16,128]{3,2,1,0:T(8,128)S(1)}, f32[12,2,16,128]{3,2,1,0:T(8,128)S(1)}, u32[]{:S(2)}, u32[]{:S(2)}) collective-permute-start(f32[12,2,16,128]{3,2,1,0:T(8,128)S(1)} %get-tuple-element.39), channel_id=1, source_target_pairs={{0,4},{1,5},{2,6},{3,7},{4,0},{5,1},{6,2},{7,3},{8,12},{9,13},{10,... | collective-permute-start | bytes 589832 | tf_op jit(solution)/shard_map/ppermute | solution.py:253
  180.4 19.2 %collective-permute-start.8 = (f32[12,2,16,128]{3,2,1,0:T(8,128)S(1)}, f32[12,2,16,128]{3,2,1,0:T(8,128)S(1)}, u32[]{:S(2)}, u32[]{:S(2)}) collective-permute-start(f32[12,2,16,128]{3,2,1,0:T(8,128)S(1)} %get-tuple-element.40), channel_id=1, source_target_pairs={{0,5},{1,4},{2,7},{3,6},{4,1},{5,0},{6,3},{7,2},{8,13},{9,12},{10,... | collective-permute-start | bytes 589832 | tf_op jit(solution)/shard_map/ppermute | solution.py:253
  182.1 23.4 %collective-permute-start.9 = (f32[12,2,16,128]{3,2,1,0:T(8,128)S(1)}, f32[12,2,16,128]{3,2,1,0:T(8,128)S(1)}, u32[]{:S(2)}, u32[]{:S(2)}) collective-permute-start(f32[12,2,16,128]{3,2,1,0:T(8,128)S(1)} %get-tuple-element.41), channel_id=1, source_target_pairs={{0,6},{1,7},{2,4},{3,5},{4,2},{5,3},{6,0},{7,1},{8,14},{9,15},{10,... | collective-permute-start | bytes 589832 | tf_op jit(solution)/shard_map/ppermute | solution.py:253
  187.1 19.2 %collective-permute-start.10 = (f32[12,2,16,128]{3,2,1,0:T(8,128)S(1)}, f32[12,2,16,128]{3,2,1,0:T(8,128)S(1)}, u32[]{:S(2)}, u32[]{:S(2)}) collective-permute-start(f32[12,2,16,128]{3,2,1,0:T(8,128)S(1)} %get-tuple-element.42), channel_id=1, source_target_pairs={{0,7},{1,6},{2,5},{3,4},{4,3},{5,2},{6,1},{7,0},{8,15},{9,14},{10,... | collective-permute-start | bytes 589832 | tf_op jit(solution)/shard_map/ppermute | solution.py:253
  190.2 18.0 %collective-permute-start.11 = (f32[12,2,16,128]{3,2,1,0:T(8,128)S(1)}, f32[12,2,16,128]{3,2,1,0:T(8,128)S(1)}, u32[]{:S(2)}, u32[]{:S(2)}) collective-permute-start(f32[12,2,16,128]{3,2,1,0:T(8,128)S(1)} %get-tuple-element.43), channel_id=1, source_target_pairs={{0,8},{1,9},{2,10},{3,11},{4,12},{5,13},{6,14},{7,15},{8,0},{9,1},... | collective-permute-start | bytes 589832 | tf_op jit(solution)/shard_map/ppermute | solution.py:253
  197.3 12.7 %collective-permute-start.12 = (f32[12,2,16,128]{3,2,1,0:T(8,128)S(1)}, f32[12,2,16,128]{3,2,1,0:T(8,128)S(1)}, u32[]{:S(2)}, u32[]{:S(2)}) collective-permute-start(f32[12,2,16,128]{3,2,1,0:T(8,128)S(1)} %get-tuple-element.44), channel_id=1, source_target_pairs={{0,9},{1,8},{2,11},{3,10},{4,13},{5,12},{6,15},{7,14},{8,1},{9,0},... | collective-permute-start | bytes 589832 | tf_op jit(solution)/shard_map/ppermute | solution.py:253
  200.3 13.3 %collective-permute-start.13 = (f32[12,2,16,128]{3,2,1,0:T(8,128)S(1)}, f32[12,2,16,128]{3,2,1,0:T(8,128)S(1)}, u32[]{:S(2)}, u32[]{:S(2)}) collective-permute-start(f32[12,2,16,128]{3,2,1,0:T(8,128)S(1)} %get-tuple-element.45), channel_id=1, source_target_pairs={{0,10},{1,11},{2,8},{3,9},{4,14},{5,15},{6,12},{7,13},{8,2},{9,3},... | collective-permute-start | bytes 589832 | tf_op jit(solution)/shard_map/ppermute | solution.py:253
  206.3 10.5 %collective-permute-start.14 = (f32[12,2,16,128]{3,2,1,0:T(8,128)}, f32[12,2,16,128]{3,2,1,0:T(8,128)}, u32[]{:S(2)}, u32[]{:S(2)}) collective-permute-start(f32[12,2,16,128]{3,2,1,0:T(8,128)} %get-tuple-element.46), channel_id=1, source_target_pairs={{0,11},{1,10},{2,9},{3,8},{4,15},{5,14},{6,13},{7,12},{8,3},{9,2},... | collective-permute-start | bytes 589832 | tf_op jit(solution)/shard_map/ppermute | solution.py:253
  207.0 12.4 %collective-permute-start.15 = (f32[12,2,16,128]{3,2,1,0:T(8,128)}, f32[12,2,16,128]{3,2,1,0:T(8,128)}, u32[]{:S(2)}, u32[]{:S(2)}) collective-permute-start(f32[12,2,16,128]{3,2,1,0:T(8,128)} %get-tuple-element.47), channel_id=1, source_target_pairs={{0,12},{1,13},{2,14},{3,15},{4,8},{5,9},{6,10},{7,11},{8,4},{9,5},... | collective-permute-start | bytes 589832 | tf_op jit(solution)/shard_map/ppermute | solution.py:253
  208.9 14.7 %collective-permute-start.16 = (f32[12,2,16,128]{3,2,1,0:T(8,128)}, f32[12,2,16,128]{3,2,1,0:T(8,128)}, u32[]{:S(2)}, u32[]{:S(2)}) collective-permute-start(f32[12,2,16,128]{3,2,1,0:T(8,128)} %get-tuple-element.48), channel_id=1, source_target_pairs={{0,13},{1,12},{2,15},{3,14},{4,9},{5,8},{6,11},{7,10},{8,5},{9,4},... | collective-permute-start | bytes 589832 | tf_op jit(solution)/shard_map/ppermute | solution.py:253
  210.7 17.5 %collective-permute-start.17 = (f32[12,2,16,128]{3,2,1,0:T(8,128)}, f32[12,2,16,128]{3,2,1,0:T(8,128)}, u32[]{:S(2)}, u32[]{:S(2)}) collective-permute-start(f32[12,2,16,128]{3,2,1,0:T(8,128)} %get-tuple-element.49), channel_id=1, source_target_pairs={{0,14},{1,15},{2,12},{3,13},{4,10},{5,11},{6,8},{7,9},{8,6},{9,7},... | collective-permute-start | bytes 589832 | tf_op jit(solution)/shard_map/ppermute | solution.py:253
  214.3 17.7 %collective-permute-start.18 = (f32[12,2,16,128]{3,2,1,0:T(8,128)}, f32[12,2,16,128]{3,2,1,0:T(8,128)}, u32[]{:S(2)}, u32[]{:S(2)}) collective-permute-start(f32[12,2,16,128]{3,2,1,0:T(8,128)} %get-tuple-element.50), channel_id=1, source_target_pairs={{0,15},{1,14},{2,13},{3,12},{4,11},{5,10},{6,9},{7,8},{8,7},{9,6},... | collective-permute-start | bytes 589832 | tf_op jit(solution)/shard_map/ppermute | solution.py:253
  232.0 0.9 copy-start.2
  232.9 0.9 copy-start.4
  233.9 0.9 copy-start.6
  234.8 0.9 copy-start.8
  235.7 0.9 copy-start.10
  239.4 0.9 copy-start.18
  (12 other events, 9.0 us)

commit v6 on v5

--- a/solution.py
+++ b/solution.py
@@ -38,6 +38,55 @@
         out_shape=jax.ShapeDtypeStruct((group, count, 2, rows, width), jnp.float32),
         name="cut_rows",
     )(nodes)
+
+
+def partner(index, k, group):
+    return index ^ k if group & (group - 1) == 0 else (k - index + group) % group
+
+
+def split_kernel(member, in_ref, *out_refs):
+    rows = out_refs[0].shape[2]
+    for k, out_ref in enumerate(out_refs):
+        row = pl.multiple_of(partner(member[0], k, len(out_refs)) * rows, rows)
+        out_ref[...] = in_ref[:, :, pl.ds(row, rows), :]
+
+
+def split_rows(member, nodes, group, part, width):
+    count, _, order, _ = nodes.shape
+    shape = (count, 2, order // group, width)
+    return pl.pallas_call(
+        split_kernel,
+        grid_spec=pltpu.PrefetchScalarGridSpec(
+            num_scalar_prefetch=1,
+            grid=(1,),
+            in_specs=[pl.BlockSpec((count, 2, order, width), lambda i, member: (0, 0, 0, part))],
+            out_specs=[pl.BlockSpec(shape, lambda i, member: (0, 0, 0, 0))] * group,
+        ),
+        out_shape=[jax.ShapeDtypeStruct(shape, jnp.float32)] * group,
+        name="split_rows",
+    )(member, nodes)
+
+
+def load_spread(member, refs, spread_ref, sems):
+    copies = []
+    for k, ref in enumerate(refs):
+        number = ref.shape[0]
+        first = partner(member, k, len(refs)) * number if len(refs) > 1 else 0
+        copies.append(
+            pltpu.make_async_copy(ref, spread_ref.at[pl.ds(first, number)], sems.at[k])
+        )
+    for copy in copies:
+        copy.start()
+    for copy in copies:
+        copy.wait()
+
+
+def spread_scratch(spread):
+    count = sum(array.shape[0] for array in spread)
+    return [
+        pltpu.VMEM((count,) + spread[0].shape[1:], jnp.float32),
+        pltpu.SemaphoreType.DMA((len(spread),)),
+    ]
 
 
 def plan_kernel(room, half_ref, ids_ref, send_ref, source_ref, crowded_ref, place_ref):
@@ -106,7 +155,10 @@
     )(half, ids)
 
 
-def leave_kernel(send_ref, spread_ref, out_ref):
+def leave_kernel(send_ref, member_ref, *refs):
+    *parts, out_ref, spread_ref, sems = refs
+    load_spread(member_ref[0], parts, spread_ref, sems)
+
     def copy(i, carry):
         out_ref[i] = spread_ref[send_ref[i]]
         return carry
@@ -114,15 +166,16 @@
     lax.fori_loop(0, out_ref.shape[0], copy, 0, unroll=8)
 
 
-def pick_leaving(send, spread, room):
+def pick_leaving(send, member, spread, room):
     return pl.pallas_call(
         leave_kernel,
-        in_specs=[SMEM, VMEM],
+        in_specs=[SMEM, SMEM] + [ANY] * len(spread),
         out_specs=VMEM,
-        out_shape=jax.ShapeDtypeStruct((room,) + spread.shape[1:], jnp.float32),
+        out_shape=jax.ShapeDtypeStruct((room,) + spread[0].shape[1:], jnp.float32),
+        scratch_shapes=spread_scratch(spread),
         compiler_params=PARAMS,
         name="pick_leaving",
-    )(send, spread)
+    )(send, member, *spread)
 
 
 def collect_kernel(source_ref, crowded_ref, spread_ref, arrived_ref, extra_ref, out_ref, sem):
@@ -165,12 +218,9 @@
     )(source, crowded, spread, arrived, extra)
 
 
-def partner(index, k, group):
-    return index ^ k if group & (group - 1) == 0 else (k - index + group) % group
-
-
-def scatter_kernel(source_ref, flags_ref, spread_ref, arrived_ref, extra_ref, *refs):
-    out_refs, sem = refs[:-1], refs[-1]
+def scatter_kernel(parts, source_ref, flags_ref, arrived_ref, extra_ref, *refs):
+    out_refs, (spread_ref, sems, sem) = refs[parts:-3], refs[-3:]
+    load_spread(flags_ref[1], refs[:parts], spread_ref, sems)
     count, room = spread_ref.shape[0], arrived_ref.shape[0]
     wanted = out_refs[0].shape[0]
     for k, out_ref in enumerate(out_refs):
@@ -202,58 +252,75 @@
 
 
 def scatter(source, flags, spread, arrived, extra, group):
-    shape = (source.shape[0] // group,) + spread.shape[1:]
-    return pl.pallas_call(
-        scatter_kernel,
-        in_specs=[SMEM, SMEM, VMEM, VMEM, ANY],
+    shape = (source.shape[0] // group,) + spread[0].shape[1:]
+    return pl.pallas_call(
+        functools.partial(scatter_kernel, len(spread)),
+        in_specs=[SMEM, SMEM, VMEM, ANY] + [ANY] * len(spread),
         out_specs=[VMEM] * group,
         out_shape=[jax.ShapeDtypeStruct(shape, jnp.float32)] * group,
-        scratch_shapes=[pltpu.SemaphoreType.DMA],
+        scratch_shapes=[*spread_scratch(spread), pltpu.SemaphoreType.DMA],
         compiler_params=PARAMS,
         name="scatter",
-    )(source, flags, spread, arrived, extra)
-
-
-def fetch_items(cuts, ids, pairwise):
+    )(source, flags, arrived, extra, *spread)
+
+
+def fetch_items(nodes, ids, pairwise):
     devices = lax.axis_size("node")
     group = devices // 2
-    half = (lax.axis_index("node") // group).astype(jnp.int32).reshape(1)
+    index = lax.axis_index("node")
+    half = (index // group).astype(jnp.int32).reshape(1)
+    member = (index % group).astype(jnp.int32).reshape(1)
     halves = [[h * group + i for i in range(group)] for h in range(2)]
     swap = [(i, (i + group) % devices) for i in range(devices)]
-    count = group * cuts[0].shape[1]
+    count = group * nodes.shape[0]
+    width = min(LANES, nodes.shape[3])
+    parts = nodes.shape[3] // width
     room = min(count, max(8, int(count * CROSS_SHARE)))
     send, source, crowded = make_plan(half, ids.reshape(-1), count, room)
 
     def exchange(x):
         return lax.all_to_all(x, "node", 0, 0, axis_index_groups=halves, tiled=True)
 
+    def trade(arrays):
+        got = []
+        for k, array in enumerate(arrays):
+            pairs = [
+                (i, i // group * group + partner(i % group, k, group)) for i in range(devices)
+            ]
+            still = all(i == j for i, j in pairs)
+            got.append(array if still else lax.ppermute(array, "node", pairs))
+        return got
+
+    def cross_all(spread):
+        if len(spread) == 1:
+            return lax.ppermute(spread[0], "node", swap)
+        members = jnp.arange(group, dtype=jnp.int32)
+        order = jnp.argsort(jnp.stack([partner(member[0], k, group) for k in range(group)]))
+        every = jnp.take(jnp.stack(spread), order[members], axis=0)
+        return lax.ppermute(every.reshape((count,) + every.shape[2:]), "node", swap)
+
     delivered = []
-    for c, cut in enumerate(cuts):
-        spread = exchange(cut)
-        spread = spread.reshape((count,) + spread.shape[2:])
-        leaving = pick_leaving(send, spread, room)
+    for c in range(parts):
+        if pairwise and c > 0:
+            spread = trade(split_rows(member, nodes, group, c, width))
+        else:
+            cut = cut_rows(nodes, group, c, width)
+            spread = exchange(cut)
+            spread = [spread.reshape((count,) + spread.shape[2:])]
+        leaving = pick_leaving(send, member, spread, room)
         arrived = lax.ppermute(leaving, "node", swap)
-        extra = lax.cond(
-            crowded[0] > 0,
-            lambda x: lax.ppermute(x, "node", swap),
-            jnp.zeros_like,
-            spread,
-        )
-        if pairwise and c == len(cuts) - 1:
-            member = (lax.axis_index("node") % group).astype(jnp.int32).reshape(1)
+        piece = (count,) + leaving.shape[1:]
+        extra = lax.cond(crowded[0] > 0, cross_all, lambda _: jnp.zeros(piece, jnp.float32), spread)
+        if pairwise and c == parts - 1:
             flags = jnp.concatenate([crowded, member])
             sent = scatter(source, flags, spread, arrived, extra, group)
-            got = []
-            for k in range(group):
-                pairs = [
-                    (i, i // group * group + partner(i % group, k, group))
-                    for i in range(devices)
-                ]
-                still = all(i == j for i, j in pairs)
-                got.append(sent[k] if still else lax.ppermute(sent[k], "node", pairs))
-            delivered.append(got)
+            delivered.append(trade(sent))
             continue
-        picked = collect(source, crowded, spread, arrived, extra)
+        if len(spread) > 1:
+            order = [partner(member[0], k, group) for k in range(group)]
+            spread = [jnp.take(jnp.stack(spread), jnp.argsort(jnp.stack(order)), axis=0)]
+            spread = [spread[0].reshape((count,) + spread[0].shape[2:])]
+        picked = collect(source, crowded, spread[0], arrived, extra)
         picked = picked.reshape((group, ids.shape[1]) + picked.shape[1:])
         delivered.append(exchange(picked))
     return delivered
@@ -413,15 +480,13 @@
     devices = lax.axis_size("node")
     column = lax.axis_index("node")
     group = devices // 2
-    node_col, _, _, local_width = node_blocks.shape
+    node_col = node_blocks.shape[0]
     second_col = second_list.shape[0] // devices
-    width = min(LANES, local_width)
-    cuts = [cut_rows(node_blocks, group, c, width) for c in range(local_width // width)]
 
     slots = node_slot[pair_list]
     slots = slots[second_list].reshape(devices, second_col, 4)
     pairwise = lax.axis_size("pair") == 1
-    rights = fetch_items(cuts, slots[:, :, 1:].reshape(devices, second_col * 3), pairwise)
+    rights = fetch_items(node_blocks, slots[:, :, 1:].reshape(devices, second_col * 3), pairwise)
 
     own_slots = lax.dynamic_index_in_dim(slots[:, :, 0], column, 0, keepdims=False)
     own_slots = own_slots - column * node_col

time: 251 us -> 297 us (1.18)
  waiting for transfers between devices: 150 us -> 177 us
  starting transfers between devices: 40.9 us -> 53.9 us
  Pallas kernels: 34.8 us -> 37.9 us
    ppermute x15 -> x30, waiting for transfers between devices: 26.2 us -> 81.2 us  [trade(): got.append(array if still else lax.ppermute(array, 'node', pairs))]
    ppermute x2, waiting for transfers between devices: 97 us -> 78.2 us  [fetch_items(): arrived = lax.ppermute(leaving, 'node', swap)]
    ppermute x15 -> x30, starting transfers between devices: 19.5 us -> 36.7 us  [trade(): got.append(array if still else lax.ppermute(array, 'node', pairs))]
    all_to_all x3 -> x2, waiting for transfers between devices: 26.4 us -> 18 us  [exchange(): return lax.all_to_all(x, 'node', 0, 0, axis_index_groups=halves, tiled=True)]
    pallas_call x3 -> x4, Pallas kernels: 8.52 us -> 14.2 us  [the longest x2 5.79 us: pick_leaving(): pl.pallas_call(leave_kernel, in_specs=[SMEM, SMEM] + [ANY] * len(spread),...]
    all_to_all x3 -> x2, starting transfers between devices: 15.3 us -> 11.4 us  [exchange(): return lax.all_to_all(x, 'node', 0, 0, axis_index_groups=halves, tiled=True)]
    unnamed x48 -> x50, local copies, waits for them, and re-layouts: 14.5 us -> 16.4 us
  transfers between devices with their start and end apart: 20 -> 34, of which waited for: 11 -> 19; matrix products, arithmetic and copies ran while one was open for 4% -> 3% of each run, Pallas kernels for 9% -> 6%
where the time goes in v6:
time: 297 us; the launch traced here: 296 us
  waiting for transfers between devices  177 us (60%)
  starting transfers between devices  53.9 us (18%)
  Pallas kernels  37.9 us (13%)
  local copies, waits for them, and re-layouts  23.5 us (8%)
    ppermute x30, waiting for transfers between devices, trade(): got.append(array if still else lax.ppermute(array, 'node', pairs))  81.2 us
    ppermute x2, waiting for transfers between devices, fetch_items(): arrived = lax.ppermute(leaving, 'node', swap)  78.2 us
    ppermute x30, starting transfers between devices, trade(): got.append(array if still else lax.ppermute(array, 'node', pairs))  36.7 us
    all_to_all x2, waiting for transfers between devices, exchange(): return lax.all_to_all(x, 'node', 0, 0, axis_index_groups=halves, tiled=True)  18 us
    unnamed x50, local copies, waits for them, and re-layouts  16.4 us
    all_to_all x2, starting transfers between devices, exchange(): return lax.all_to_all(x, 'node', 0, 0, axis_index_groups=halves, tiled=True)  11.4 us
    pallas_call x1, Pallas kernels, chain(): pl.pallas_call(functools.partial(chain_kernel, len(parts)), grid_spec=plt...  9.5 us
    pallas_call x1, Pallas kernels, make_plan(): pl.pallas_call(functools.partial(plan_kernel, room), in_specs=[SMEM] * 2,...  6.59 us
  transfers between devices with their start and end apart: 34, of which 19 were waited for; matrix products, arithmetic and copies ran while one was open for 3% of the time, Pallas kernels for 6%

profile of v6, /device:TPU:0, one launch (start us, length us, event | category | flops | bytes accessed | tf_op | source)
XLA Modules:
  0.0 295.9 jit_solution(6437914023320349699)
XLA Ops:
  0.0 2.7 cut_rows.1
  2.7 6.4 %all-to-all-start = ((f32[16,8,2,16,128]{4,3,2,1,0:T(8,128)}), f32[16,8,2,16,128]{4,3,2,1,0:T(8,128)S(1)}, u32[]{:S(2)}, u32[]{:S(2)}) async-start(f32[16,8,2,16,128]{4,3,2,1,0:T(8,128)} %cut_rows.1), calls=%async_computation | async-start | bytes 4194304 | tf_op jit(solution)/shard_map/all_to_all | solution.py:282
  9.8 1.9 gather_fusion.2
  13.7 6.6 %make_plan.1 = (s32[128]{0:T(128)S(1)}, s32[192]{0:T(256)S(1)}, s32[1]{0:T(128)}) custom-call(s32[1]{0:T(128)} %bitcast.36.half_ref, s32[384]{0:T(512)S(1)} %reshape_reshape.3.ids_ref), custom_call_target="tpu_custom_call" | custom-call | tf_op jit(solution)/shard_map/make_plan/pallas_call | solution.py:143
  20.3 18.0 %all-to-all-done = f32[16,8,2,16,128]{4,3,2,1,0:T(8,128)S(1)} async-done(((f32[16,8,2,16,128]{4,3,2,1,0:T(8,128)}), f32[16,8,2,16,128]{4,3,2,1,0:T(8,128)S(1)}, u32[]{:S(2)}, u32[]{:S(2)}) %all-to-all-start) | async-done | bytes 2097184 | tf_op jit(solution)/shard_map/all_to_all | solution.py:282
  39.5 2.2 pick_leaving.2
  41.8 2.7 collective-permute-start.2
  46.8 38.8 %collective-permute-done.2.arrived_ref = f32[58,2,16,128]{3,2,1,0:T(8,128)S(1)} collective-permute-done((f32[58,2,16,128]{3,2,1,0:T(8,128)S(1)}, f32[58,2,16,128]{3,2,1,0:T(8,128)S(1)}, u32[]{:S(2)}, u32[]{:S(2)}) %collective-permute-start.2) | collective-permute-done | bytes 950304 | tf_op jit(solution)/shard_map/ppermute | solution.py:311
  85.6 4.9 %collect.1 = f32[192,2,16,128]{3,2,1,0:T(8,128)} custom-call(s32[192]{0:T(256)S(1)} %get-tuple-element.99.source_ref, s32[1]{0:T(128)} %get-tuple-element.100.crowded_ref, f32[128,2,16,128]{3,2,1,0:T(8,128)} %bitcast.62, f32[58,2,16,128]{3,2,1,0:T(8,128)S(1)} %collective-permute-done.2.arrived_ref, f32[128,2,16,128]{3,2,1,0:T(8,128)} %get-tuple-element.134.extra_ref), custom_call_target="tpu_custom_call" | custom-call | tf_op jit(solution)/shard_map/collect/pallas_call | solution.py:210
  90.6 5.0 %all-to-all-start.1 = ((f32[16,12,2,16,128]{4,3,2,1,0:T(8,128)}), f32[16,12,2,16,128]{4,3,2,1,0:T(8,128)S(1)}, u32[]{:S(2)}, u32[]{:S(2)}) async-start(f32[16,12,2,16,128]{4,3,2,1,0:T(8,128)} %bitcast.39), calls=%async_computation.1 | async-start | bytes 6291456 | tf_op jit(solution)/shard_map/all_to_all | solution.py:282
  95.6 3.0 %split_rows.1 = (f32[8,2,16,128]{3,2,1,0:T(8,128)S(1)}, f32[8,2,16,128]{3,2,1,0:T(8,128)}, f32[8,2,16,128]{3,2,1,0:T(8,128)}, f32[8,2,16,128]{3,2,1,0:T(8,128)},...) custom-call(s32[1]{0:T(128)} %bitcast.35.member_ref.member, ...), custom_call_target="tpu_custom_call" | custom-call | tf_op jit(solution)/shard_map/split_rows/pallas_call | solution.py:57
  102.5 2.5 collective-permute-start.8
  105.0 38.4 %collective-permute-done.4.refs_2_ = f32[8,2,16,128]{3,2,1,0:T(8,128)S(1)} collective-permute-done((f32[8,2,16,128]{3,2,1,0:T(8,128)}, f32[8,2,16,128]{3,2,1,0:T(8,128)S(1)}, u32[]{:S(2)}, u32[]{:S(2)}) %collective-permute-start.4) | collective-permute-done | bytes 131104 | tf_op jit(solution)/shard_map/ppermute | solution.py:291
  149.6 3.8 %collective-permute-start.14 = (f32[8,2,16,128]{3,2,1,0:T(8,128)}, f32[8,2,16,128]{3,2,1,0:T(8,128)}, u32[]{:S(2)}, u32[]{:S(2)}) collective-permute-start(f32[8,2,16,128]{3,2,1,0:T(8,128)} %get-tuple-element.114), channel_id=1, source_target_pairs={{0,12},{1,13},{2,14},{3,15},{4,8},{5,9},{6,10},{7,11},{8,4},{9,5},... | collective-permute-start | bytes 393224 | tf_op jit(solution)/shard_map/ppermute | solution.py:291
  159.5 2.8 collective-permute-done.14.refs_12_
  162.3 2.9 collective-permute-done.15.refs_13_
  165.3 3.0 %collective-permute-done.16.refs_14_ = f32[8,2,16,128]{3,2,1,0:T(8,128)} collective-permute-done((f32[8,2,16,128]{3,2,1,0:T(8,128)}, f32[8,2,16,128]{3,2,1,0:T(8,128)}, u32[]{:S(2)}, u32[]{:S(2)}) %collective-permute-start.16) | collective-permute-done | bytes 131104 | tf_op jit(solution)/shard_map/ppermute | solution.py:291
  168.3 3.0 %collective-permute-done.17.refs_15_ = f32[8,2,16,128]{3,2,1,0:T(8,128)} collective-permute-done((f32[8,2,16,128]{3,2,1,0:T(8,128)}, f32[8,2,16,128]{3,2,1,0:T(8,128)}, u32[]{:S(2)}, u32[]{:S(2)}) %collective-permute-start.17) | collective-permute-done | bytes 131104 | tf_op jit(solution)/shard_map/ppermute | solution.py:291
  171.3 3.6 %pick_leaving.3 = f32[58,2,16,128]{3,2,1,0:T(8,128)} custom-call(s32[128]{0:T(128)S(1)} %get-tuple-element.101.send_ref, s32[1]{0:T(128)} %bitcast.35.member_ref.member, f32[8,2,16,128]{3,2,1,0:T(8,128)S(1)} %get-tuple-element.102.refs_0_, f32[8,2,16,128]{3,2,1,0:T(8,128)} %collective-permute-done.3.refs_1_, ...), custom_call_target="tpu_custom_call" | custom-call | tf_op jit(solution)/shard_map/pick_leaving/pallas_call | solution.py:170
  174.8 3.0 %collective-permute-start.18 = (f32[58,2,16,128]{3,2,1,0:T(8,128)}, f32[58,2,16,128]{3,2,1,0:T(8,128)}, u32[]{:S(2)}, u32[]{:S(2)}) collective-permute-start(f32[58,2,16,128]{3,2,1,0:T(8,128)} %pick_leaving.3), channel_id=1, source_target_pairs={{0,16},{1,17},{2,18},{3,19},{4,20},{5,21},{6,22},{7,23},{8,24},{9,... | collective-permute-start | bytes 2850824 | tf_op jit(solution)/shard_map/ppermute | solution.py:311
  180.3 39.4 %collective-permute-done.18.arrived_ref = f32[58,2,16,128]{3,2,1,0:T(8,128)} collective-permute-done((f32[58,2,16,128]{3,2,1,0:T(8,128)}, f32[58,2,16,128]{3,2,1,0:T(8,128)}, u32[]{:S(2)}, u32[]{:S(2)}) %collective-permute-start.18) | collective-permute-done | bytes 950304 | tf_op jit(solution)/shard_map/ppermute | solution.py:311
  219.7 5.4 %scatter.1 = (f32[12,2,16,128]{3,2,1,0:T(8,128)S(1)}, f32[12,2,16,128]{3,2,1,0:T(8,128)S(1)}, f32[12,2,16,128]{3,2,1,0:T(8,128)S(1)}, f32[12,2,16,128]{3,2,1,0:T...) custom-call(s32[192]{0:T(256)S(1)} %get-tuple-element.99.source_ref,, ...), custom_call_target="tpu_custom_call" | custom-call | tf_op jit(solution)/shard_map/scatter/pallas_call | solution.py:256
  227.0 1.9 collective-permute-start.22
  228.9 2.9 collective-permute-start.24
  240.0 5.9 %collective-permute-done.23.refs_6_ = f32[12,2,16,128]{3,2,1,0:T(8,128)S(1)} collective-permute-done((f32[12,2,16,128]{3,2,1,0:T(8,128)S(1)}, f32[12,2,16,128]{3,2,1,0:T(8,128)S(1)}, u32[]{:S(2)}, u32[]{:S(2)}) %collective-permute-start.23) | collective-permute-done | bytes 196640 | tf_op jit(solution)/shard_map/ppermute | solution.py:291
  251.2 1.9 collective-permute-start.30
  254.7 2.5 collective-permute-start.32
  261.0 4.6 %collective-permute-done.30.refs_13_ = f32[12,2,16,128]{3,2,1,0:T(8,128)} collective-permute-done((f32[12,2,16,128]{3,2,1,0:T(8,128)}, f32[12,2,16,128]{3,2,1,0:T(8,128)}, u32[]{:S(2)}, u32[]{:S(2)}) %collective-permute-start.30) | collective-permute-done | bytes 196640 | tf_op jit(solution)/shard_map/ppermute | solution.py:291
  265.7 4.0 %collective-permute-done.31.refs_14_ = f32[12,2,16,128]{3,2,1,0:T(8,128)} collective-permute-done((f32[12,2,16,128]{3,2,1,0:T(8,128)}, f32[12,2,16,128]{3,2,1,0:T(8,128)}, u32[]{:S(2)}, u32[]{:S(2)}) %collective-permute-start.31) | collective-permute-done | bytes 196640 | tf_op jit(solution)/shard_map/ppermute | solution.py:291
  269.6 4.2 %collective-permute-done.32.refs_15_ = f32[12,2,16,128]{3,2,1,0:T(8,128)} collective-permute-done((f32[12,2,16,128]{3,2,1,0:T(8,128)}, f32[12,2,16,128]{3,2,1,0:T(8,128)}, u32[]{:S(2)}, u32[]{:S(2)}) %collective-permute-start.32) | collective-permute-done | bytes 196640 | tf_op jit(solution)/shard_map/ppermute | solution.py:291
  273.9 4.1 %collective-permute-done.33.refs_16_ = f32[12,2,16,128]{3,2,1,0:T(8,128)} collective-permute-done((f32[12,2,16,128]{3,2,1,0:T(8,128)}, f32[12,2,16,128]{3,2,1,0:T(8,128)}, u32[]{:S(2)}, u32[]{:S(2)}) %collective-permute-start.33) | collective-permute-done | bytes 196640 | tf_op jit(solution)/shard_map/ppermute | solution.py:291
  286.4 9.5 %chain.1 = f32[2,2,256,256]{3,2,1,0:T(8,128)} custom-call(s32[1]{0:T(128)} %bitcast.35.member_ref.member, s32[4]{0:T(128)S(1)} %subtract_reduce_fusion.slot, s32[4]{0:T(128)S(1)} %dynamic-slice_subtract_fusion.target, s32[4]{0:T(128)S(1)} %dynamic_slice.12.sign, f32[8,2,256,256]{3,2,1,0:T(8,128)} %node_ref.1, ...), custom_call_target="tpu_custom_call" | custom-call | tf_op jit(solution)/shard_map/chain/pallas_call | solution.py:454
  (116 shorter events, 56.5 us)
Async XLA Ops:
  2.7 35.5 %all-to-all-start = ((f32[16,8,2,16,128]{4,3,2,1,0:T(8,128)}), f32[16,8,2,16,128]{4,3,2,1,0:T(8,128)S(1)}, u32[]{:S(2)}, u32[]{:S(2)}) async-start(f32[16,8,2,16,128]{4,3,2,1,0:T(8,128)} %cut_rows.1), calls=%async_computation | async-start | bytes 4194304 | tf_op jit(solution)/shard_map/all_to_all | solution.py:282
  41.8 43.8 %collective-permute-start.2 = (f32[58,2,16,128]{3,2,1,0:T(8,128)S(1)}, f32[58,2,16,128]{3,2,1,0:T(8,128)S(1)}, u32[]{:S(2)}, u32[]{:S(2)}) collective-permute-start(f32[58,2,16,128]{3,2,1,0:T(8,128)S(1)} %pick_leaving.2), channel_id=1, source_target_pairs={{0,16},{1,17},{2,18},{3,19},{4,20},{5,21},{6,22},{7,23},{8,24},{9,... | collective-permute-start | bytes 2850824 | tf_op jit(solution)/shard_map/ppermute | solution.py:311
  90.6 187.5 %all-to-all-start.1 = ((f32[16,12,2,16,128]{4,3,2,1,0:T(8,128)}), f32[16,12,2,16,128]{4,3,2,1,0:T(8,128)S(1)}, u32[]{:S(2)}, u32[]{:S(2)}) async-start(f32[16,12,2,16,128]{4,3,2,1,0:T(8,128)} %bitcast.39), calls=%async_computation.1 | async-start | bytes 6291456 | tf_op jit(solution)/shard_map/all_to_all | solution.py:282
  99.0 44.5 %collective-permute-start.4 = (f32[8,2,16,128]{3,2,1,0:T(8,128)}, f32[8,2,16,128]{3,2,1,0:T(8,128)S(1)}, u32[]{:S(2)}, u32[]{:S(2)}) collective-permute-start(f32[8,2,16,128]{3,2,1,0:T(8,128)} %get-tuple-element.104), channel_id=1, source_target_pairs={{0,2},{1,3},{2,0},{3,1},{4,6},{5,7},{6,4},{7,5},{8,10},{9,11},{10,... | collective-permute-start | bytes 393224 | tf_op jit(solution)/shard_map/ppermute | solution.py:291
  100.6 44.6 %collective-permute-start.5 = (f32[8,2,16,128]{3,2,1,0:T(8,128)}, f32[8,2,16,128]{3,2,1,0:T(8,128)}, u32[]{:S(2)}, u32[]{:S(2)}) collective-permute-start(f32[8,2,16,128]{3,2,1,0:T(8,128)} %get-tuple-element.105), channel_id=1, source_target_pairs={{0,3},{1,2},{2,1},{3,0},{4,7},{5,6},{6,5},{7,4},{8,11},{9,10},{10,... | collective-permute-start | bytes 393224 | tf_op jit(solution)/shard_map/ppermute | solution.py:291
  100.6 46.3 %collective-permute-start.6 = (f32[8,2,16,128]{3,2,1,0:T(8,128)}, f32[8,2,16,128]{3,2,1,0:T(8,128)}, u32[]{:S(2)}, u32[]{:S(2)}) collective-permute-start(f32[8,2,16,128]{3,2,1,0:T(8,128)} %get-tuple-element.106), channel_id=1, source_target_pairs={{0,4},{1,5},{2,6},{3,7},{4,0},{5,1},{6,2},{7,3},{8,12},{9,13},{10,... | collective-permute-start | bytes 393224 | tf_op jit(solution)/shard_map/ppermute | solution.py:291
  102.4 45.5 %collective-permute-start.7 = (f32[8,2,16,128]{3,2,1,0:T(8,128)}, f32[8,2,16,128]{3,2,1,0:T(8,128)}, u32[]{:S(2)}, u32[]{:S(2)}) collective-permute-start(f32[8,2,16,128]{3,2,1,0:T(8,128)} %get-tuple-element.107), channel_id=1, source_target_pairs={{0,5},{1,4},{2,7},{3,6},{4,1},{5,0},{6,3},{7,2},{8,13},{9,12},{10,... | collective-permute-start | bytes 393224 | tf_op jit(solution)/shard_map/ppermute | solution.py:291
  102.5 45.4 %collective-permute-start.8 = (f32[8,2,16,128]{3,2,1,0:T(8,128)}, f32[8,2,16,128]{3,2,1,0:T(8,128)}, u32[]{:S(2)}, u32[]{:S(2)}) collective-permute-start(f32[8,2,16,128]{3,2,1,0:T(8,128)} %get-tuple-element.108), channel_id=1, source_target_pairs={{0,6},{1,7},{2,4},{3,5},{4,2},{5,3},{6,0},{7,1},{8,14},{9,15},{10,... | collective-permute-start | bytes 393224 | tf_op jit(solution)/shard_map/ppermute | solution.py:291
  143.4 6.2 %collective-permute-start.9 = (f32[8,2,16,128]{3,2,1,0:T(8,128)}, f32[8,2,16,128]{3,2,1,0:T(8,128)}, u32[]{:S(2)}, u32[]{:S(2)}) collective-permute-start(f32[8,2,16,128]{3,2,1,0:T(8,128)} %get-tuple-element.109), channel_id=1, source_target_pairs={{0,7},{1,6},{2,5},{3,4},{4,3},{5,2},{6,1},{7,0},{8,15},{9,14},{10,... | collective-permute-start | bytes 393224 | tf_op jit(solution)/shard_map/ppermute | solution.py:291
  145.2 8.2 %collective-permute-start.10 = (f32[8,2,16,128]{3,2,1,0:T(8,128)}, f32[8,2,16,128]{3,2,1,0:T(8,128)}, u32[]{:S(2)}, u32[]{:S(2)}) collective-permute-start(f32[8,2,16,128]{3,2,1,0:T(8,128)} %get-tuple-element.110), channel_id=1, source_target_pairs={{0,8},{1,9},{2,10},{3,11},{4,12},{5,13},{6,14},{7,15},{8,0},{9,1},... | collective-permute-start | bytes 393224 | tf_op jit(solution)/shard_map/ppermute | solution.py:291
  146.9 8.1 %collective-permute-start.11 = (f32[8,2,16,128]{3,2,1,0:T(8,128)}, f32[8,2,16,128]{3,2,1,0:T(8,128)}, u32[]{:S(2)}, u32[]{:S(2)}) collective-permute-start(f32[8,2,16,128]{3,2,1,0:T(8,128)} %get-tuple-element.111), channel_id=1, source_target_pairs={{0,9},{1,8},{2,11},{3,10},{4,13},{5,12},{6,15},{7,14},{8,1},{9,0},... | collective-permute-start | bytes 393224 | tf_op jit(solution)/shard_map/ppermute | solution.py:291
  147.8 9.7 %collective-permute-start.12 = (f32[8,2,16,128]{3,2,1,0:T(8,128)}, f32[8,2,16,128]{3,2,1,0:T(8,128)}, u32[]{:S(2)}, u32[]{:S(2)}) collective-permute-start(f32[8,2,16,128]{3,2,1,0:T(8,128)} %get-tuple-element.112), channel_id=1, source_target_pairs={{0,10},{1,11},{2,8},{3,9},{4,14},{5,15},{6,12},{7,13},{8,2},{9,3},... | collective-permute-start | bytes 393224 | tf_op jit(solution)/shard_map/ppermute | solution.py:291
  147.8 11.7 %collective-permute-start.13 = (f32[8,2,16,128]{3,2,1,0:T(8,128)}, f32[8,2,16,128]{3,2,1,0:T(8,128)}, u32[]{:S(2)}, u32[]{:S(2)}) collective-permute-start(f32[8,2,16,128]{3,2,1,0:T(8,128)} %get-tuple-element.113), channel_id=1, source_target_pairs={{0,11},{1,10},{2,9},{3,8},{4,15},{5,14},{6,13},{7,12},{8,3},{9,2},... | collective-permute-start | bytes 393224 | tf_op jit(solution)/shard_map/ppermute | solution.py:291
  149.6 12.7 %collective-permute-start.14 = (f32[8,2,16,128]{3,2,1,0:T(8,128)}, f32[8,2,16,128]{3,2,1,0:T(8,128)}, u32[]{:S(2)}, u32[]{:S(2)}) collective-permute-start(f32[8,2,16,128]{3,2,1,0:T(8,128)} %get-tuple-element.114), channel_id=1, source_target_pairs={{0,12},{1,13},{2,14},{3,15},{4,8},{5,9},{6,10},{7,11},{8,4},{9,5},... | collective-permute-start | bytes 393224 | tf_op jit(solution)/shard_map/ppermute | solution.py:291
  153.4 11.9 %collective-permute-start.15 = (f32[8,2,16,128]{3,2,1,0:T(8,128)}, f32[8,2,16,128]{3,2,1,0:T(8,128)}, u32[]{:S(2)}, u32[]{:S(2)}) collective-permute-start(f32[8,2,16,128]{3,2,1,0:T(8,128)} %get-tuple-element.115), channel_id=1, source_target_pairs={{0,13},{1,12},{2,15},{3,14},{4,9},{5,8},{6,11},{7,10},{8,5},{9,4},... | collective-permute-start | bytes 393224 | tf_op jit(solution)/shard_map/ppermute | solution.py:291
  155.0 13.3 %collective-permute-start.16 = (f32[8,2,16,128]{3,2,1,0:T(8,128)}, f32[8,2,16,128]{3,2,1,0:T(8,128)}, u32[]{:S(2)}, u32[]{:S(2)}) collective-permute-start(f32[8,2,16,128]{3,2,1,0:T(8,128)} %get-tuple-element.116), channel_id=1, source_target_pairs={{0,14},{1,15},{2,12},{3,13},{4,10},{5,11},{6,8},{7,9},{8,6},{9,7},... | collective-permute-start | bytes 393224 | tf_op jit(solution)/shard_map/ppermute | solution.py:291
  157.6 13.7 %collective-permute-start.17 = (f32[8,2,16,128]{3,2,1,0:T(8,128)}, f32[8,2,16,128]{3,2,1,0:T(8,128)}, u32[]{:S(2)}, u32[]{:S(2)}) collective-permute-start(f32[8,2,16,128]{3,2,1,0:T(8,128)} %get-tuple-element.117), channel_id=1, source_target_pairs={{0,15},{1,14},{2,13},{3,12},{4,11},{5,10},{6,9},{7,8},{8,7},{9,6},... | collective-permute-start | bytes 393224 | tf_op jit(solution)/shard_map/ppermute | solution.py:291
  174.8 44.9 %collective-permute-start.18 = (f32[58,2,16,128]{3,2,1,0:T(8,128)}, f32[58,2,16,128]{3,2,1,0:T(8,128)}, u32[]{:S(2)}, u32[]{:S(2)}) collective-permute-start(f32[58,2,16,128]{3,2,1,0:T(8,128)} %pick_leaving.3), channel_id=1, source_target_pairs={{0,16},{1,17},{2,18},{3,19},{4,20},{5,21},{6,22},{7,23},{8,24},{9,... | collective-permute-start | bytes 2850824 | tf_op jit(solution)/shard_map/ppermute | solution.py:311
  225.2 7.8 %collective-permute-start.20 = (f32[12,2,16,128]{3,2,1,0:T(8,128)S(1)}, f32[12,2,16,128]{3,2,1,0:T(8,128)S(1)}, u32[]{:S(2)}, u32[]{:S(2)}) collective-permute-start(f32[12,2,16,128]{3,2,1,0:T(8,128)S(1)} %get-tuple-element.120), channel_id=1, source_target_pairs={{0,2},{1,3},{2,0},{3,1},{4,6},{5,7},{6,4},{7,5},{8,10},{9,11},{10,... | collective-permute-start | bytes 589832 | tf_op jit(solution)/shard_map/ppermute | solution.py:291
  225.7 10.4 %collective-permute-start.21 = (f32[12,2,16,128]{3,2,1,0:T(8,128)S(1)}, f32[12,2,16,128]{3,2,1,0:T(8,128)S(1)}, u32[]{:S(2)}, u32[]{:S(2)}) collective-permute-start(f32[12,2,16,128]{3,2,1,0:T(8,128)S(1)} %get-tuple-element.121), channel_id=1, source_target_pairs={{0,3},{1,2},{2,1},{3,0},{4,7},{5,6},{6,5},{7,4},{8,11},{9,10},{10,... | collective-permute-start | bytes 589832 | tf_op jit(solution)/shard_map/ppermute | solution.py:291
  227.0 10.5 %collective-permute-start.22 = (f32[12,2,16,128]{3,2,1,0:T(8,128)S(1)}, f32[12,2,16,128]{3,2,1,0:T(8,128)S(1)}, u32[]{:S(2)}, u32[]{:S(2)}) collective-permute-start(f32[12,2,16,128]{3,2,1,0:T(8,128)S(1)} %get-tuple-element.122), channel_id=1, source_target_pairs={{0,4},{1,5},{2,6},{3,7},{4,0},{5,1},{6,2},{7,3},{8,12},{9,13},{10,... | collective-permute-start | bytes 589832 | tf_op jit(solution)/shard_map/ppermute | solution.py:291
  228.9 17.1 %collective-permute-start.23 = (f32[12,2,16,128]{3,2,1,0:T(8,128)S(1)}, f32[12,2,16,128]{3,2,1,0:T(8,128)S(1)}, u32[]{:S(2)}, u32[]{:S(2)}) collective-permute-start(f32[12,2,16,128]{3,2,1,0:T(8,128)S(1)} %get-tuple-element.123), channel_id=1, source_target_pairs={{0,5},{1,4},{2,7},{3,6},{4,1},{5,0},{6,3},{7,2},{8,13},{9,12},{10,... | collective-permute-start | bytes 589832 | tf_op jit(solution)/shard_map/ppermute | solution.py:291
  228.9 19.4 %collective-permute-start.24 = (f32[12,2,16,128]{3,2,1,0:T(8,128)S(1)}, f32[12,2,16,128]{3,2,1,0:T(8,128)S(1)}, u32[]{:S(2)}, u32[]{:S(2)}) collective-permute-start(f32[12,2,16,128]{3,2,1,0:T(8,128)S(1)} %get-tuple-element.124), channel_id=1, source_target_pairs={{0,6},{1,7},{2,4},{3,5},{4,2},{5,3},{6,0},{7,1},{8,14},{9,15},{10,... | collective-permute-start | bytes 589832 | tf_op jit(solution)/shard_map/ppermute | solution.py:291
  233.7 16.9 %collective-permute-start.25 = (f32[12,2,16,128]{3,2,1,0:T(8,128)S(1)}, f32[12,2,16,128]{3,2,1,0:T(8,128)S(1)}, u32[]{:S(2)}, u32[]{:S(2)}) collective-permute-start(f32[12,2,16,128]{3,2,1,0:T(8,128)S(1)} %get-tuple-element.125), channel_id=1, source_target_pairs={{0,7},{1,6},{2,5},{3,4},{4,3},{5,2},{6,1},{7,0},{8,15},{9,14},{10,... | collective-permute-start | bytes 589832 | tf_op jit(solution)/shard_map/ppermute | solution.py:291
  236.8 16.3 %collective-permute-start.26 = (f32[12,2,16,128]{3,2,1,0:T(8,128)S(1)}, f32[12,2,16,128]{3,2,1,0:T(8,128)S(1)}, u32[]{:S(2)}, u32[]{:S(2)}) collective-permute-start(f32[12,2,16,128]{3,2,1,0:T(8,128)S(1)} %get-tuple-element.126), channel_id=1, source_target_pairs={{0,8},{1,9},{2,10},{3,11},{4,12},{5,13},{6,14},{7,15},{8,0},{9,1},... | collective-permute-start | bytes 589832 | tf_op jit(solution)/shard_map/ppermute | solution.py:291
  238.2 15.8 %collective-permute-start.27 = (f32[12,2,16,128]{3,2,1,0:T(8,128)S(1)}, f32[12,2,16,128]{3,2,1,0:T(8,128)S(1)}, u32[]{:S(2)}, u32[]{:S(2)}) collective-permute-start(f32[12,2,16,128]{3,2,1,0:T(8,128)S(1)} %get-tuple-element.127), channel_id=1, source_target_pairs={{0,9},{1,8},{2,11},{3,10},{4,13},{5,12},{6,15},{7,14},{8,1},{9,0},... | collective-permute-start | bytes 589832 | tf_op jit(solution)/shard_map/ppermute | solution.py:291
  246.7 10.5 %collective-permute-start.28 = (f32[12,2,16,128]{3,2,1,0:T(8,128)S(1)}, f32[12,2,16,128]{3,2,1,0:T(8,128)S(1)}, u32[]{:S(2)}, u32[]{:S(2)}) collective-permute-start(f32[12,2,16,128]{3,2,1,0:T(8,128)S(1)} %get-tuple-element.128), channel_id=1, source_target_pairs={{0,10},{1,11},{2,8},{3,9},{4,14},{5,15},{6,12},{7,13},{8,2},{9,3},... | collective-permute-start | bytes 589832 | tf_op jit(solution)/shard_map/ppermute | solution.py:291
  249.0 12.1 %collective-permute-start.29 = (f32[12,2,16,128]{3,2,1,0:T(8,128)}, f32[12,2,16,128]{3,2,1,0:T(8,128)}, u32[]{:S(2)}, u32[]{:S(2)}) collective-permute-start(f32[12,2,16,128]{3,2,1,0:T(8,128)} %get-tuple-element.129), channel_id=1, source_target_pairs={{0,11},{1,10},{2,9},{3,8},{4,15},{5,14},{6,13},{7,12},{8,3},{9,2},... | collective-permute-start | bytes 589832 | tf_op jit(solution)/shard_map/ppermute | solution.py:291
  251.2 14.5 %collective-permute-start.30 = (f32[12,2,16,128]{3,2,1,0:T(8,128)}, f32[12,2,16,128]{3,2,1,0:T(8,128)}, u32[]{:S(2)}, u32[]{:S(2)}) collective-permute-start(f32[12,2,16,128]{3,2,1,0:T(8,128)} %get-tuple-element.130), channel_id=1, source_target_pairs={{0,12},{1,13},{2,14},{3,15},{4,8},{5,9},{6,10},{7,11},{8,4},{9,5},... | collective-permute-start | bytes 589832 | tf_op jit(solution)/shard_map/ppermute | solution.py:291
  253.8 15.9 %collective-permute-start.31 = (f32[12,2,16,128]{3,2,1,0:T(8,128)}, f32[12,2,16,128]{3,2,1,0:T(8,128)}, u32[]{:S(2)}, u32[]{:S(2)}) collective-permute-start(f32[12,2,16,128]{3,2,1,0:T(8,128)} %get-tuple-element.131), channel_id=1, source_target_pairs={{0,13},{1,12},{2,15},{3,14},{4,9},{5,8},{6,11},{7,10},{8,5},{9,4},... | collective-permute-start | bytes 589832 | tf_op jit(solution)/shard_map/ppermute | solution.py:291
  254.7 19.2 %collective-permute-start.32 = (f32[12,2,16,128]{3,2,1,0:T(8,128)}, f32[12,2,16,128]{3,2,1,0:T(8,128)}, u32[]{:S(2)}, u32[]{:S(2)}) collective-permute-start(f32[12,2,16,128]{3,2,1,0:T(8,128)} %get-tuple-element.132), channel_id=1, source_target_pairs={{0,14},{1,15},{2,12},{3,13},{4,10},{5,11},{6,8},{7,9},{8,6},{9,7},... | collective-permute-start | bytes 589832 | tf_op jit(solution)/shard_map/ppermute | solution.py:291
  257.9 20.2 %collective-permute-start.33 = (f32[12,2,16,128]{3,2,1,0:T(8,128)}, f32[12,2,16,128]{3,2,1,0:T(8,128)}, u32[]{:S(2)}, u32[]{:S(2)}) collective-permute-start(f32[12,2,16,128]{3,2,1,0:T(8,128)} %get-tuple-element.133), channel_id=1, source_target_pairs={{0,15},{1,14},{2,13},{3,12},{4,11},{5,10},{6,9},{7,8},{8,7},{9,6},... | collective-permute-start | bytes 589832 | tf_op jit(solution)/shard_map/ppermute | solution.py:291
  (27 other events, 161.4 us)

commit v7 on v6

--- a/solution.py
+++ b/solution.py
@@ -67,26 +67,15 @@
     )(member, nodes)
 
 
-def load_spread(member, refs, spread_ref, sems):
-    copies = []
+def load_spread(member, refs, spread_ref):
     for k, ref in enumerate(refs):
         number = ref.shape[0]
-        first = partner(member, k, len(refs)) * number if len(refs) > 1 else 0
-        copies.append(
-            pltpu.make_async_copy(ref, spread_ref.at[pl.ds(first, number)], sems.at[k])
-        )
-    for copy in copies:
-        copy.start()
-    for copy in copies:
-        copy.wait()
+        spread_ref[pl.ds(partner(member, k, len(refs)) * number, number)] = ref[...]
 
 
 def spread_scratch(spread):
     count = sum(array.shape[0] for array in spread)
-    return [
-        pltpu.VMEM((count,) + spread[0].shape[1:], jnp.float32),
-        pltpu.SemaphoreType.DMA((len(spread),)),
-    ]
+    return [pltpu.VMEM((count,) + spread[0].shape[1:], jnp.float32)] if len(spread) > 1 else []
 
 
 def plan_kernel(room, half_ref, ids_ref, send_ref, source_ref, crowded_ref, place_ref):
@@ -156,8 +145,11 @@
 
 
 def leave_kernel(send_ref, member_ref, *refs):
-    *parts, out_ref, spread_ref, sems = refs
-    load_spread(member_ref[0], parts, spread_ref, sems)
+    if len(refs) == 2:
+        spread_ref, out_ref = refs
+    else:
+        *parts, out_ref, spread_ref = refs
+        load_spread(member_ref[0], parts, spread_ref)
 
     def copy(i, carry):
         out_ref[i] = spread_ref[send_ref[i]]
@@ -169,7 +161,7 @@
 def pick_leaving(send, member, spread, room):
     return pl.pallas_call(
         leave_kernel,
-        in_specs=[SMEM, SMEM] + [ANY] * len(spread),
+        in_specs=[SMEM, SMEM] + [VMEM] * len(spread),
         out_specs=VMEM,
         out_shape=jax.ShapeDtypeStruct((room,) + spread[0].shape[1:], jnp.float32),
         scratch_shapes=spread_scratch(spread),
@@ -219,8 +211,11 @@
 
 
 def scatter_kernel(parts, source_ref, flags_ref, arrived_ref, extra_ref, *refs):
-    out_refs, (spread_ref, sems, sem) = refs[parts:-3], refs[-3:]
-    load_spread(flags_ref[1], refs[:parts], spread_ref, sems)
+    if parts == 1:
+        spread_ref, *out_refs, sem = refs
+    else:
+        out_refs, (spread_ref, sem) = refs[parts:-2], refs[-2:]
+        load_spread(flags_ref[1], refs[:parts], spread_ref)
     count, room = spread_ref.shape[0], arrived_ref.shape[0]
     wanted = out_refs[0].shape[0]
     for k, out_ref in enumerate(out_refs):
@@ -255,7 +250,7 @@
     shape = (source.shape[0] // group,) + spread[0].shape[1:]
     return pl.pallas_call(
         functools.partial(scatter_kernel, len(spread)),
-        in_specs=[SMEM, SMEM, VMEM, ANY] + [ANY] * len(spread),
+        in_specs=[SMEM, SMEM, VMEM, ANY] + [VMEM] * len(spread),
         out_specs=[VMEM] * group,
         out_shape=[jax.ShapeDtypeStruct(shape, jnp.float32)] * group,
         scratch_shapes=[*spread_scratch(spread), pltpu.SemaphoreType.DMA],

time: 297 us -> 294 us (0.990)
  no operation moved by 1% of the time
where the time goes in v7:
time: 294 us; the launch traced here: 293 us
  waiting for transfers between devices  177 us (60%)
  starting transfers between devices  53.8 us (18%)
  Pallas kernels  35.5 us (12%)
  local copies, waits for them, and re-layouts  23.5 us (8%)
    ppermute x30, waiting for transfers between devices, trade(): got.append(array if still else lax.ppermute(array, 'node', pairs))  81.2 us
    ppermute x2, waiting for transfers between devices, fetch_items(): arrived = lax.ppermute(leaving, 'node', swap)  78.2 us
    ppermute x30, starting transfers between devices, trade(): got.append(array if still else lax.ppermute(array, 'node', pairs))  36.7 us
    all_to_all x2, waiting for transfers between devices, exchange(): return lax.all_to_all(x, 'node', 0, 0, axis_index_groups=halves, tiled=True)  18 us
    unnamed x50, local copies, waits for them, and re-layouts  16.4 us
    all_to_all x2, starting transfers between devices, exchange(): return lax.all_to_all(x, 'node', 0, 0, axis_index_groups=halves, tiled=True)  11.4 us
    pallas_call x1, Pallas kernels, chain(): pl.pallas_call(functools.partial(chain_kernel, len(parts)), grid_spec=plt...  9.5 us
    pallas_call x1, Pallas kernels, make_plan(): pl.pallas_call(functools.partial(plan_kernel, room), in_specs=[SMEM] * 2,...  6.59 us
  transfers between devices with their start and end apart: 34, of which 19 were waited for; matrix products, arithmetic and copies ran while one was open for 3% of the time, Pallas kernels for 6%

profile of v7, /device:TPU:0, one launch (start us, length us, event | category | flops | bytes accessed | tf_op | source)
XLA Modules:
  0.0 293.4 jit_solution(1455692849760773476)
XLA Ops:
  0.0 2.7 cut_rows.1
  2.7 6.4 %all-to-all-start = ((f32[16,8,2,16,128]{4,3,2,1,0:T(8,128)}), f32[16,8,2,16,128]{4,3,2,1,0:T(8,128)S(1)}, u32[]{:S(2)}, u32[]{:S(2)}) async-start(f32[16,8,2,16,128]{4,3,2,1,0:T(8,128)} %cut_rows.1), calls=%async_computation | async-start | bytes 4194304 | tf_op jit(solution)/shard_map/all_to_all | solution.py:277
  9.8 1.9 gather_fusion.2
  13.7 6.6 %make_plan.1 = (s32[128]{0:T(128)S(1)}, s32[192]{0:T(256)S(1)}, s32[1]{0:T(128)}) custom-call(s32[1]{0:T(128)} %bitcast.36.half_ref, s32[384]{0:T(512)S(1)} %reshape_reshape.3.ids_ref), custom_call_target="tpu_custom_call" | custom-call | tf_op jit(solution)/shard_map/make_plan/pallas_call | solution.py:132
  20.3 18.0 %all-to-all-done = f32[16,8,2,16,128]{4,3,2,1,0:T(8,128)S(1)} async-done(((f32[16,8,2,16,128]{4,3,2,1,0:T(8,128)}), f32[16,8,2,16,128]{4,3,2,1,0:T(8,128)S(1)}, u32[]{:S(2)}, u32[]{:S(2)}) %all-to-all-start) | async-done | bytes 2097184 | tf_op jit(solution)/shard_map/all_to_all | solution.py:277
  41.3 2.7 collective-permute-start.2
  46.3 38.8 %collective-permute-done.2.arrived_ref = f32[58,2,16,128]{3,2,1,0:T(8,128)S(1)} collective-permute-done((f32[58,2,16,128]{3,2,1,0:T(8,128)S(1)}, f32[58,2,16,128]{3,2,1,0:T(8,128)S(1)}, u32[]{:S(2)}, u32[]{:S(2)}) %collective-permute-start.2) | collective-permute-done | bytes 950304 | tf_op jit(solution)/shard_map/ppermute | solution.py:306
  85.1 4.9 %collect.1 = f32[192,2,16,128]{3,2,1,0:T(8,128)} custom-call(s32[192]{0:T(256)S(1)} %get-tuple-element.99.source_ref, s32[1]{0:T(128)} %get-tuple-element.100.crowded_ref, f32[128,2,16,128]{3,2,1,0:T(8,128)} %bitcast.62, f32[58,2,16,128]{3,2,1,0:T(8,128)S(1)} %collective-permute-done.2.arrived_ref, f32[128,2,16,128]{3,2,1,0:T(8,128)} %get-tuple-element.134.extra_ref), custom_call_target="tpu_custom_call" | custom-call | tf_op jit(solution)/shard_map/collect/pallas_call | solution.py:202
  90.0 5.0 %all-to-all-start.1 = ((f32[16,12,2,16,128]{4,3,2,1,0:T(8,128)}), f32[16,12,2,16,128]{4,3,2,1,0:T(8,128)S(1)}, u32[]{:S(2)}, u32[]{:S(2)}) async-start(f32[16,12,2,16,128]{4,3,2,1,0:T(8,128)} %bitcast.39), calls=%async_computation.1 | async-start | bytes 6291456 | tf_op jit(solution)/shard_map/all_to_all | solution.py:277
  95.0 3.0 %split_rows.1 = (f32[8,2,16,128]{3,2,1,0:T(8,128)S(1)}, f32[8,2,16,128]{3,2,1,0:T(8,128)}, f32[8,2,16,128]{3,2,1,0:T(8,128)}, f32[8,2,16,128]{3,2,1,0:T(8,128)},...) custom-call(s32[1]{0:T(128)} %bitcast.35.member_ref.member, ...), custom_call_target="tpu_custom_call" | custom-call | tf_op jit(solution)/shard_map/split_rows/pallas_call | solution.py:57
  102.0 2.5 collective-permute-start.8
  104.5 38.4 %collective-permute-done.4.refs_2_ = f32[8,2,16,128]{3,2,1,0:T(8,128)S(1)} collective-permute-done((f32[8,2,16,128]{3,2,1,0:T(8,128)}, f32[8,2,16,128]{3,2,1,0:T(8,128)S(1)}, u32[]{:S(2)}, u32[]{:S(2)}) %collective-permute-start.4) | collective-permute-done | bytes 131104 | tf_op jit(solution)/shard_map/ppermute | solution.py:286
  149.1 3.8 %collective-permute-start.14 = (f32[8,2,16,128]{3,2,1,0:T(8,128)}, f32[8,2,16,128]{3,2,1,0:T(8,128)}, u32[]{:S(2)}, u32[]{:S(2)}) collective-permute-start(f32[8,2,16,128]{3,2,1,0:T(8,128)} %get-tuple-element.114), channel_id=1, source_target_pairs={{0,12},{1,13},{2,14},{3,15},{4,8},{5,9},{6,10},{7,11},{8,4},{9,5},... | collective-permute-start | bytes 393224 | tf_op jit(solution)/shard_map/ppermute | solution.py:286
  157.2 1.8 collective-permute-done.13.refs_11_
  159.0 2.8 collective-permute-done.14.refs_12_
  161.8 2.9 %collective-permute-done.15.refs_13_ = f32[8,2,16,128]{3,2,1,0:T(8,128)} collective-permute-done((f32[8,2,16,128]{3,2,1,0:T(8,128)}, f32[8,2,16,128]{3,2,1,0:T(8,128)}, u32[]{:S(2)}, u32[]{:S(2)}) %collective-permute-start.15) | collective-permute-done | bytes 131104 | tf_op jit(solution)/shard_map/ppermute | solution.py:286
  164.7 3.0 %collective-permute-done.16.refs_14_ = f32[8,2,16,128]{3,2,1,0:T(8,128)} collective-permute-done((f32[8,2,16,128]{3,2,1,0:T(8,128)}, f32[8,2,16,128]{3,2,1,0:T(8,128)}, u32[]{:S(2)}, u32[]{:S(2)}) %collective-permute-start.16) | collective-permute-done | bytes 131104 | tf_op jit(solution)/shard_map/ppermute | solution.py:286
  167.7 3.0 %collective-permute-done.17.refs_15_ = f32[8,2,16,128]{3,2,1,0:T(8,128)} collective-permute-done((f32[8,2,16,128]{3,2,1,0:T(8,128)}, f32[8,2,16,128]{3,2,1,0:T(8,128)}, u32[]{:S(2)}, u32[]{:S(2)}) %collective-permute-start.17) | collective-permute-done | bytes 131104 | tf_op jit(solution)/shard_map/ppermute | solution.py:286
  170.7 2.7 pick_leaving.3
  173.5 3.0 %collective-permute-start.18 = (f32[58,2,16,128]{3,2,1,0:T(8,128)}, f32[58,2,16,128]{3,2,1,0:T(8,128)}, u32[]{:S(2)}, u32[]{:S(2)}) collective-permute-start(f32[58,2,16,128]{3,2,1,0:T(8,128)} %pick_leaving.3), channel_id=1, source_target_pairs={{0,16},{1,17},{2,18},{3,19},{4,20},{5,21},{6,22},{7,23},{8,24},{9,... | collective-permute-start | bytes 2850824 | tf_op jit(solution)/shard_map/ppermute | solution.py:306
  178.9 39.4 %collective-permute-done.18.arrived_ref = f32[58,2,16,128]{3,2,1,0:T(8,128)} collective-permute-done((f32[58,2,16,128]{3,2,1,0:T(8,128)}, f32[58,2,16,128]{3,2,1,0:T(8,128)}, u32[]{:S(2)}, u32[]{:S(2)}) %collective-permute-start.18) | collective-permute-done | bytes 950304 | tf_op jit(solution)/shard_map/ppermute | solution.py:306
  218.2 4.3 %scatter.1 = (f32[12,2,16,128]{3,2,1,0:T(8,128)S(1)}, f32[12,2,16,128]{3,2,1,0:T(8,128)S(1)}, f32[12,2,16,128]{3,2,1,0:T(8,128)S(1)}, f32[12,2,16,128]{3,2,1,0:T...) custom-call(s32[192]{0:T(256)S(1)} %get-tuple-element.99.source_ref,, ...), custom_call_target="tpu_custom_call" | custom-call | tf_op jit(solution)/shard_map/scatter/pallas_call | solution.py:251
  224.5 1.9 collective-permute-start.22
  226.4 2.9 collective-permute-start.24
  237.6 5.9 %collective-permute-done.23.refs_6_ = f32[12,2,16,128]{3,2,1,0:T(8,128)S(1)} collective-permute-done((f32[12,2,16,128]{3,2,1,0:T(8,128)S(1)}, f32[12,2,16,128]{3,2,1,0:T(8,128)S(1)}, u32[]{:S(2)}, u32[]{:S(2)}) %collective-permute-start.23) | collective-permute-done | bytes 196640 | tf_op jit(solution)/shard_map/ppermute | solution.py:286
  248.7 1.9 collective-permute-start.30
  252.2 2.5 collective-permute-start.32
  258.5 4.6 %collective-permute-done.30.refs_13_ = f32[12,2,16,128]{3,2,1,0:T(8,128)} collective-permute-done((f32[12,2,16,128]{3,2,1,0:T(8,128)}, f32[12,2,16,128]{3,2,1,0:T(8,128)}, u32[]{:S(2)}, u32[]{:S(2)}) %collective-permute-start.30) | collective-permute-done | bytes 196640 | tf_op jit(solution)/shard_map/ppermute | solution.py:286
  263.2 4.0 %collective-permute-done.31.refs_14_ = f32[12,2,16,128]{3,2,1,0:T(8,128)} collective-permute-done((f32[12,2,16,128]{3,2,1,0:T(8,128)}, f32[12,2,16,128]{3,2,1,0:T(8,128)}, u32[]{:S(2)}, u32[]{:S(2)}) %collective-permute-start.31) | collective-permute-done | bytes 196640 | tf_op jit(solution)/shard_map/ppermute | solution.py:286
  267.2 4.2 %collective-permute-done.32.refs_15_ = f32[12,2,16,128]{3,2,1,0:T(8,128)} collective-permute-done((f32[12,2,16,128]{3,2,1,0:T(8,128)}, f32[12,2,16,128]{3,2,1,0:T(8,128)}, u32[]{:S(2)}, u32[]{:S(2)}) %collective-permute-start.32) | collective-permute-done | bytes 196640 | tf_op jit(solution)/shard_map/ppermute | solution.py:286
  271.4 4.1 %collective-permute-done.33.refs_16_ = f32[12,2,16,128]{3,2,1,0:T(8,128)} collective-permute-done((f32[12,2,16,128]{3,2,1,0:T(8,128)}, f32[12,2,16,128]{3,2,1,0:T(8,128)}, u32[]{:S(2)}, u32[]{:S(2)}) %collective-permute-start.33) | collective-permute-done | bytes 196640 | tf_op jit(solution)/shard_map/ppermute | solution.py:286
  283.9 9.5 %chain.1 = f32[2,2,256,256]{3,2,1,0:T(8,128)} custom-call(s32[1]{0:T(128)} %bitcast.35.member_ref.member, s32[4]{0:T(128)S(1)} %subtract_reduce_fusion.slot, s32[4]{0:T(128)S(1)} %dynamic-slice_subtract_fusion.target, s32[4]{0:T(128)S(1)} %dynamic_slice.12.sign, f32[8,2,256,256]{3,2,1,0:T(8,128)} %node_ref.1, ...), custom_call_target="tpu_custom_call" | custom-call | tf_op jit(solution)/shard_map/chain/pallas_call | solution.py:449
  (116 shorter events, 56.4 us)
Async XLA Ops:
  2.7 35.5 %all-to-all-start = ((f32[16,8,2,16,128]{4,3,2,1,0:T(8,128)}), f32[16,8,2,16,128]{4,3,2,1,0:T(8,128)S(1)}, u32[]{:S(2)}, u32[]{:S(2)}) async-start(f32[16,8,2,16,128]{4,3,2,1,0:T(8,128)} %cut_rows.1), calls=%async_computation | async-start | bytes 4194304 | tf_op jit(solution)/shard_map/all_to_all | solution.py:277
  41.3 43.8 %collective-permute-start.2 = (f32[58,2,16,128]{3,2,1,0:T(8,128)S(1)}, f32[58,2,16,128]{3,2,1,0:T(8,128)S(1)}, u32[]{:S(2)}, u32[]{:S(2)}) collective-permute-start(f32[58,2,16,128]{3,2,1,0:T(8,128)S(1)} %pick_leaving.2), channel_id=1, source_target_pairs={{0,16},{1,17},{2,18},{3,19},{4,20},{5,21},{6,22},{7,23},{8,24},{9,... | collective-permute-start | bytes 2850824 | tf_op jit(solution)/shard_map/ppermute | solution.py:306
  90.0 185.5 %all-to-all-start.1 = ((f32[16,12,2,16,128]{4,3,2,1,0:T(8,128)}), f32[16,12,2,16,128]{4,3,2,1,0:T(8,128)S(1)}, u32[]{:S(2)}, u32[]{:S(2)}) async-start(f32[16,12,2,16,128]{4,3,2,1,0:T(8,128)} %bitcast.39), calls=%async_computation.1 | async-start | bytes 6291456 | tf_op jit(solution)/shard_map/all_to_all | solution.py:277
  98.5 44.5 %collective-permute-start.4 = (f32[8,2,16,128]{3,2,1,0:T(8,128)}, f32[8,2,16,128]{3,2,1,0:T(8,128)S(1)}, u32[]{:S(2)}, u32[]{:S(2)}) collective-permute-start(f32[8,2,16,128]{3,2,1,0:T(8,128)} %get-tuple-element.104), channel_id=1, source_target_pairs={{0,2},{1,3},{2,0},{3,1},{4,6},{5,7},{6,4},{7,5},{8,10},{9,11},{10,... | collective-permute-start | bytes 393224 | tf_op jit(solution)/shard_map/ppermute | solution.py:286
  100.1 44.6 %collective-permute-start.5 = (f32[8,2,16,128]{3,2,1,0:T(8,128)}, f32[8,2,16,128]{3,2,1,0:T(8,128)}, u32[]{:S(2)}, u32[]{:S(2)}) collective-permute-start(f32[8,2,16,128]{3,2,1,0:T(8,128)} %get-tuple-element.105), channel_id=1, source_target_pairs={{0,3},{1,2},{2,1},{3,0},{4,7},{5,6},{6,5},{7,4},{8,11},{9,10},{10,... | collective-permute-start | bytes 393224 | tf_op jit(solution)/shard_map/ppermute | solution.py:286
  100.1 46.3 %collective-permute-start.6 = (f32[8,2,16,128]{3,2,1,0:T(8,128)}, f32[8,2,16,128]{3,2,1,0:T(8,128)}, u32[]{:S(2)}, u32[]{:S(2)}) collective-permute-start(f32[8,2,16,128]{3,2,1,0:T(8,128)} %get-tuple-element.106), channel_id=1, source_target_pairs={{0,4},{1,5},{2,6},{3,7},{4,0},{5,1},{6,2},{7,3},{8,12},{9,13},{10,... | collective-permute-start | bytes 393224 | tf_op jit(solution)/shard_map/ppermute | solution.py:286
  101.8 45.5 %collective-permute-start.7 = (f32[8,2,16,128]{3,2,1,0:T(8,128)}, f32[8,2,16,128]{3,2,1,0:T(8,128)}, u32[]{:S(2)}, u32[]{:S(2)}) collective-permute-start(f32[8,2,16,128]{3,2,1,0:T(8,128)} %get-tuple-element.107), channel_id=1, source_target_pairs={{0,5},{1,4},{2,7},{3,6},{4,1},{5,0},{6,3},{7,2},{8,13},{9,12},{10,... | collective-permute-start | bytes 393224 | tf_op jit(solution)/shard_map/ppermute | solution.py:286
  102.0 45.4 %collective-permute-start.8 = (f32[8,2,16,128]{3,2,1,0:T(8,128)}, f32[8,2,16,128]{3,2,1,0:T(8,128)}, u32[]{:S(2)}, u32[]{:S(2)}) collective-permute-start(f32[8,2,16,128]{3,2,1,0:T(8,128)} %get-tuple-element.108), channel_id=1, source_target_pairs={{0,6},{1,7},{2,4},{3,5},{4,2},{5,3},{6,0},{7,1},{8,14},{9,15},{10,... | collective-permute-start | bytes 393224 | tf_op jit(solution)/shard_map/ppermute | solution.py:286
  142.9 6.2 %collective-permute-start.9 = (f32[8,2,16,128]{3,2,1,0:T(8,128)}, f32[8,2,16,128]{3,2,1,0:T(8,128)}, u32[]{:S(2)}, u32[]{:S(2)}) collective-permute-start(f32[8,2,16,128]{3,2,1,0:T(8,128)} %get-tuple-element.109), channel_id=1, source_target_pairs={{0,7},{1,6},{2,5},{3,4},{4,3},{5,2},{6,1},{7,0},{8,15},{9,14},{10,... | collective-permute-start | bytes 393224 | tf_op jit(solution)/shard_map/ppermute | solution.py:286
  144.7 8.2 %collective-permute-start.10 = (f32[8,2,16,128]{3,2,1,0:T(8,128)}, f32[8,2,16,128]{3,2,1,0:T(8,128)}, u32[]{:S(2)}, u32[]{:S(2)}) collective-permute-start(f32[8,2,16,128]{3,2,1,0:T(8,128)} %get-tuple-element.110), channel_id=1, source_target_pairs={{0,8},{1,9},{2,10},{3,11},{4,12},{5,13},{6,14},{7,15},{8,0},{9,1},... | collective-permute-start | bytes 393224 | tf_op jit(solution)/shard_map/ppermute | solution.py:286
  146.4 8.1 %collective-permute-start.11 = (f32[8,2,16,128]{3,2,1,0:T(8,128)}, f32[8,2,16,128]{3,2,1,0:T(8,128)}, u32[]{:S(2)}, u32[]{:S(2)}) collective-permute-start(f32[8,2,16,128]{3,2,1,0:T(8,128)} %get-tuple-element.111), channel_id=1, source_target_pairs={{0,9},{1,8},{2,11},{3,10},{4,13},{5,12},{6,15},{7,14},{8,1},{9,0},... | collective-permute-start | bytes 393224 | tf_op jit(solution)/shard_map/ppermute | solution.py:286
  147.3 9.7 %collective-permute-start.12 = (f32[8,2,16,128]{3,2,1,0:T(8,128)}, f32[8,2,16,128]{3,2,1,0:T(8,128)}, u32[]{:S(2)}, u32[]{:S(2)}) collective-permute-start(f32[8,2,16,128]{3,2,1,0:T(8,128)} %get-tuple-element.112), channel_id=1, source_target_pairs={{0,10},{1,11},{2,8},{3,9},{4,14},{5,15},{6,12},{7,13},{8,2},{9,3},... | collective-permute-start | bytes 393224 | tf_op jit(solution)/shard_map/ppermute | solution.py:286
  147.3 11.7 %collective-permute-start.13 = (f32[8,2,16,128]{3,2,1,0:T(8,128)}, f32[8,2,16,128]{3,2,1,0:T(8,128)}, u32[]{:S(2)}, u32[]{:S(2)}) collective-permute-start(f32[8,2,16,128]{3,2,1,0:T(8,128)} %get-tuple-element.113), channel_id=1, source_target_pairs={{0,11},{1,10},{2,9},{3,8},{4,15},{5,14},{6,13},{7,12},{8,3},{9,2},... | collective-permute-start | bytes 393224 | tf_op jit(solution)/shard_map/ppermute | solution.py:286
  149.1 12.7 %collective-permute-start.14 = (f32[8,2,16,128]{3,2,1,0:T(8,128)}, f32[8,2,16,128]{3,2,1,0:T(8,128)}, u32[]{:S(2)}, u32[]{:S(2)}) collective-permute-start(f32[8,2,16,128]{3,2,1,0:T(8,128)} %get-tuple-element.114), channel_id=1, source_target_pairs={{0,12},{1,13},{2,14},{3,15},{4,8},{5,9},{6,10},{7,11},{8,4},{9,5},... | collective-permute-start | bytes 393224 | tf_op jit(solution)/shard_map/ppermute | solution.py:286
  152.9 11.9 %collective-permute-start.15 = (f32[8,2,16,128]{3,2,1,0:T(8,128)}, f32[8,2,16,128]{3,2,1,0:T(8,128)}, u32[]{:S(2)}, u32[]{:S(2)}) collective-permute-start(f32[8,2,16,128]{3,2,1,0:T(8,128)} %get-tuple-element.115), channel_id=1, source_target_pairs={{0,13},{1,12},{2,15},{3,14},{4,9},{5,8},{6,11},{7,10},{8,5},{9,4},... | collective-permute-start | bytes 393224 | tf_op jit(solution)/shard_map/ppermute | solution.py:286
  154.5 13.3 %collective-permute-start.16 = (f32[8,2,16,128]{3,2,1,0:T(8,128)}, f32[8,2,16,128]{3,2,1,0:T(8,128)}, u32[]{:S(2)}, u32[]{:S(2)}) collective-permute-start(f32[8,2,16,128]{3,2,1,0:T(8,128)} %get-tuple-element.116), channel_id=1, source_target_pairs={{0,14},{1,15},{2,12},{3,13},{4,10},{5,11},{6,8},{7,9},{8,6},{9,7},... | collective-permute-start | bytes 393224 | tf_op jit(solution)/shard_map/ppermute | solution.py:286
  157.1 13.7 %collective-permute-start.17 = (f32[8,2,16,128]{3,2,1,0:T(8,128)}, f32[8,2,16,128]{3,2,1,0:T(8,128)}, u32[]{:S(2)}, u32[]{:S(2)}) collective-permute-start(f32[8,2,16,128]{3,2,1,0:T(8,128)} %get-tuple-element.117), channel_id=1, source_target_pairs={{0,15},{1,14},{2,13},{3,12},{4,11},{5,10},{6,9},{7,8},{8,7},{9,6},... | collective-permute-start | bytes 393224 | tf_op jit(solution)/shard_map/ppermute | solution.py:286
  173.5 44.8 %collective-permute-start.18 = (f32[58,2,16,128]{3,2,1,0:T(8,128)}, f32[58,2,16,128]{3,2,1,0:T(8,128)}, u32[]{:S(2)}, u32[]{:S(2)}) collective-permute-start(f32[58,2,16,128]{3,2,1,0:T(8,128)} %pick_leaving.3), channel_id=1, source_target_pairs={{0,16},{1,17},{2,18},{3,19},{4,20},{5,21},{6,22},{7,23},{8,24},{9,... | collective-permute-start | bytes 2850824 | tf_op jit(solution)/shard_map/ppermute | solution.py:306
  222.7 7.8 %collective-permute-start.20 = (f32[12,2,16,128]{3,2,1,0:T(8,128)S(1)}, f32[12,2,16,128]{3,2,1,0:T(8,128)S(1)}, u32[]{:S(2)}, u32[]{:S(2)}) collective-permute-start(f32[12,2,16,128]{3,2,1,0:T(8,128)S(1)} %get-tuple-element.120), channel_id=1, source_target_pairs={{0,2},{1,3},{2,0},{3,1},{4,6},{5,7},{6,4},{7,5},{8,10},{9,11},{10,... | collective-permute-start | bytes 589832 | tf_op jit(solution)/shard_map/ppermute | solution.py:286
  223.2 10.4 %collective-permute-start.21 = (f32[12,2,16,128]{3,2,1,0:T(8,128)S(1)}, f32[12,2,16,128]{3,2,1,0:T(8,128)S(1)}, u32[]{:S(2)}, u32[]{:S(2)}) collective-permute-start(f32[12,2,16,128]{3,2,1,0:T(8,128)S(1)} %get-tuple-element.121), channel_id=1, source_target_pairs={{0,3},{1,2},{2,1},{3,0},{4,7},{5,6},{6,5},{7,4},{8,11},{9,10},{10,... | collective-permute-start | bytes 589832 | tf_op jit(solution)/shard_map/ppermute | solution.py:286
  224.5 10.5 %collective-permute-start.22 = (f32[12,2,16,128]{3,2,1,0:T(8,128)S(1)}, f32[12,2,16,128]{3,2,1,0:T(8,128)S(1)}, u32[]{:S(2)}, u32[]{:S(2)}) collective-permute-start(f32[12,2,16,128]{3,2,1,0:T(8,128)S(1)} %get-tuple-element.122), channel_id=1, source_target_pairs={{0,4},{1,5},{2,6},{3,7},{4,0},{5,1},{6,2},{7,3},{8,12},{9,13},{10,... | collective-permute-start | bytes 589832 | tf_op jit(solution)/shard_map/ppermute | solution.py:286
  226.4 17.1 %collective-permute-start.23 = (f32[12,2,16,128]{3,2,1,0:T(8,128)S(1)}, f32[12,2,16,128]{3,2,1,0:T(8,128)S(1)}, u32[]{:S(2)}, u32[]{:S(2)}) collective-permute-start(f32[12,2,16,128]{3,2,1,0:T(8,128)S(1)} %get-tuple-element.123), channel_id=1, source_target_pairs={{0,5},{1,4},{2,7},{3,6},{4,1},{5,0},{6,3},{7,2},{8,13},{9,12},{10,... | collective-permute-start | bytes 589832 | tf_op jit(solution)/shard_map/ppermute | solution.py:286
  226.4 19.4 %collective-permute-start.24 = (f32[12,2,16,128]{3,2,1,0:T(8,128)S(1)}, f32[12,2,16,128]{3,2,1,0:T(8,128)S(1)}, u32[]{:S(2)}, u32[]{:S(2)}) collective-permute-start(f32[12,2,16,128]{3,2,1,0:T(8,128)S(1)} %get-tuple-element.124), channel_id=1, source_target_pairs={{0,6},{1,7},{2,4},{3,5},{4,2},{5,3},{6,0},{7,1},{8,14},{9,15},{10,... | collective-permute-start | bytes 589832 | tf_op jit(solution)/shard_map/ppermute | solution.py:286
  231.2 16.9 %collective-permute-start.25 = (f32[12,2,16,128]{3,2,1,0:T(8,128)S(1)}, f32[12,2,16,128]{3,2,1,0:T(8,128)S(1)}, u32[]{:S(2)}, u32[]{:S(2)}) collective-permute-start(f32[12,2,16,128]{3,2,1,0:T(8,128)S(1)} %get-tuple-element.125), channel_id=1, source_target_pairs={{0,7},{1,6},{2,5},{3,4},{4,3},{5,2},{6,1},{7,0},{8,15},{9,14},{10,... | collective-permute-start | bytes 589832 | tf_op jit(solution)/shard_map/ppermute | solution.py:286
  234.3 16.3 %collective-permute-start.26 = (f32[12,2,16,128]{3,2,1,0:T(8,128)S(1)}, f32[12,2,16,128]{3,2,1,0:T(8,128)S(1)}, u32[]{:S(2)}, u32[]{:S(2)}) collective-permute-start(f32[12,2,16,128]{3,2,1,0:T(8,128)S(1)} %get-tuple-element.126), channel_id=1, source_target_pairs={{0,8},{1,9},{2,10},{3,11},{4,12},{5,13},{6,14},{7,15},{8,0},{9,1},... | collective-permute-start | bytes 589832 | tf_op jit(solution)/shard_map/ppermute | solution.py:286
  235.7 15.8 %collective-permute-start.27 = (f32[12,2,16,128]{3,2,1,0:T(8,128)S(1)}, f32[12,2,16,128]{3,2,1,0:T(8,128)S(1)}, u32[]{:S(2)}, u32[]{:S(2)}) collective-permute-start(f32[12,2,16,128]{3,2,1,0:T(8,128)S(1)} %get-tuple-element.127), channel_id=1, source_target_pairs={{0,9},{1,8},{2,11},{3,10},{4,13},{5,12},{6,15},{7,14},{8,1},{9,0},... | collective-permute-start | bytes 589832 | tf_op jit(solution)/shard_map/ppermute | solution.py:286
  244.2 10.5 %collective-permute-start.28 = (f32[12,2,16,128]{3,2,1,0:T(8,128)S(1)}, f32[12,2,16,128]{3,2,1,0:T(8,128)S(1)}, u32[]{:S(2)}, u32[]{:S(2)}) collective-permute-start(f32[12,2,16,128]{3,2,1,0:T(8,128)S(1)} %get-tuple-element.128), channel_id=1, source_target_pairs={{0,10},{1,11},{2,8},{3,9},{4,14},{5,15},{6,12},{7,13},{8,2},{9,3},... | collective-permute-start | bytes 589832 | tf_op jit(solution)/shard_map/ppermute | solution.py:286
  246.5 12.1 %collective-permute-start.29 = (f32[12,2,16,128]{3,2,1,0:T(8,128)}, f32[12,2,16,128]{3,2,1,0:T(8,128)}, u32[]{:S(2)}, u32[]{:S(2)}) collective-permute-start(f32[12,2,16,128]{3,2,1,0:T(8,128)} %get-tuple-element.129), channel_id=1, source_target_pairs={{0,11},{1,10},{2,9},{3,8},{4,15},{5,14},{6,13},{7,12},{8,3},{9,2},... | collective-permute-start | bytes 589832 | tf_op jit(solution)/shard_map/ppermute | solution.py:286
  248.7 14.5 %collective-permute-start.30 = (f32[12,2,16,128]{3,2,1,0:T(8,128)}, f32[12,2,16,128]{3,2,1,0:T(8,128)}, u32[]{:S(2)}, u32[]{:S(2)}) collective-permute-start(f32[12,2,16,128]{3,2,1,0:T(8,128)} %get-tuple-element.130), channel_id=1, source_target_pairs={{0,12},{1,13},{2,14},{3,15},{4,8},{5,9},{6,10},{7,11},{8,4},{9,5},... | collective-permute-start | bytes 589832 | tf_op jit(solution)/shard_map/ppermute | solution.py:286
  251.3 15.9 %collective-permute-start.31 = (f32[12,2,16,128]{3,2,1,0:T(8,128)}, f32[12,2,16,128]{3,2,1,0:T(8,128)}, u32[]{:S(2)}, u32[]{:S(2)}) collective-permute-start(f32[12,2,16,128]{3,2,1,0:T(8,128)} %get-tuple-element.131), channel_id=1, source_target_pairs={{0,13},{1,12},{2,15},{3,14},{4,9},{5,8},{6,11},{7,10},{8,5},{9,4},... | collective-permute-start | bytes 589832 | tf_op jit(solution)/shard_map/ppermute | solution.py:286
  252.2 19.2 %collective-permute-start.32 = (f32[12,2,16,128]{3,2,1,0:T(8,128)}, f32[12,2,16,128]{3,2,1,0:T(8,128)}, u32[]{:S(2)}, u32[]{:S(2)}) collective-permute-start(f32[12,2,16,128]{3,2,1,0:T(8,128)} %get-tuple-element.132), channel_id=1, source_target_pairs={{0,14},{1,15},{2,12},{3,13},{4,10},{5,11},{6,8},{7,9},{8,6},{9,7},... | collective-permute-start | bytes 589832 | tf_op jit(solution)/shard_map/ppermute | solution.py:286
  255.4 20.2 %collective-permute-start.33 = (f32[12,2,16,128]{3,2,1,0:T(8,128)}, f32[12,2,16,128]{3,2,1,0:T(8,128)}, u32[]{:S(2)}, u32[]{:S(2)}) collective-permute-start(f32[12,2,16,128]{3,2,1,0:T(8,128)} %get-tuple-element.133), channel_id=1, source_target_pairs={{0,15},{1,14},{2,13},{3,12},{4,11},{5,10},{6,9},{7,8},{8,7},{9,6},... | collective-permute-start | bytes 589832 | tf_op jit(solution)/shard_map/ppermute | solution.py:286
  (27 other events, 159.4 us)

commit v8 on v7

--- a/solution.py
+++ b/solution.py
@@ -306,15 +306,11 @@
         arrived = lax.ppermute(leaving, "node", swap)
         piece = (count,) + leaving.shape[1:]
         extra = lax.cond(crowded[0] > 0, cross_all, lambda _: jnp.zeros(piece, jnp.float32), spread)
-        if pairwise and c == parts - 1:
+        if pairwise:
             flags = jnp.concatenate([crowded, member])
             sent = scatter(source, flags, spread, arrived, extra, group)
             delivered.append(trade(sent))
             continue
-        if len(spread) > 1:
-            order = [partner(member[0], k, group) for k in range(group)]
-            spread = [jnp.take(jnp.stack(spread), jnp.argsort(jnp.stack(order)), axis=0)]
-            spread = [spread[0].reshape((count,) + spread[0].shape[2:])]
         picked = collect(source, crowded, spread[0], arrived, extra)
         picked = picked.reshape((group, ids.shape[1]) + picked.shape[1:])
         delivered.append(exchange(picked))
@@ -427,42 +423,42 @@
 
 
 def chain_kernel(parts, member, slot, target, sign, node_ref, *refs):
-    part_refs, got_refs, (out_ref, last_ref) = refs[:parts], refs[parts:-2], refs[-2:]
-    for k, ref in enumerate(got_refs):
+    got_refs, (out_ref, right_ref) = refs[:-2], refs[-2:]
+    group = len(got_refs) // parts
+    for i, ref in enumerate(got_refs):
         rows = ref.shape[2]
-        row = pl.multiple_of(partner(member[0], k, len(got_refs)) * rows, rows)
+        row = pl.multiple_of(partner(member[0], i % group, group) * rows, rows)
         for which in range(3):
-            last_ref[which, 0, :, pl.ds(row, rows)] = ref[which]
+            right_ref[i // group, which, 0, :, pl.ds(row, rows)] = ref[which]
     left = wide(node_ref)
     for which in range(3):
-        blocks = [ref[:, which] for ref in part_refs] + [last_ref[which]]
-        left = product(left, blocks)
+        left = product(left, [right_ref[part, which] for part in range(parts)])
     add_result(pl.program_id(0), target, sign, left, out_ref)
 
 
 def chain(member, slot, target, sign, nodes, rights):
     order = nodes.shape[2]
     whole = (RES_COL, 2, order, order)
-    *parts, got = rights
+    parts = len(rights)
+    got = [array for right in rights for array in right]
     _, _, rows, width = got[0].shape
 
     return pl.pallas_call(
-        functools.partial(chain_kernel, len(parts)),
+        functools.partial(chain_kernel, parts),
         grid_spec=pltpu.PrefetchScalarGridSpec(
             num_scalar_prefetch=4,
             grid=(slot.shape[0],),
             in_specs=[
                 pl.BlockSpec((1, 2, order, order), lambda k, m, slot, t, s: (slot[k], 0, 0, 0)),
-                *[triple_spec(part) for part in parts],
                 *[pl.BlockSpec((3, 2, rows, width), lambda k, *scalars: (k, 0, 0, 0))] * len(got),
             ],
             out_specs=pl.BlockSpec(whole, lambda k, *scalars: (0, 0, 0, 0)),
-            scratch_shapes=[pltpu.VMEM((3, 1, 2, order, width), jnp.float32)],
+            scratch_shapes=[pltpu.VMEM((parts, 3, 1, 2, order, width), jnp.float32)],
         ),
         out_shape=jax.ShapeDtypeStruct(whole, jnp.float32),
         compiler_params=CHAIN,
         name="chain",
-    )(member, slot, target, sign, nodes, *parts, *got)
+    )(member, slot, target, sign, nodes, *got)
 
 
 def all_columns(x):

time: 294 us -> 278 us (0.946)
  waiting for transfers between devices: 177 us -> 135 us
  local copies, waits for them, and re-layouts: 23.5 us -> 47 us
  starting transfers between devices: 53.8 us -> 59.9 us
    unnamed x50 -> x154, local copies, waits for them, and re-layouts: 16.4 us -> 40.1 us
    ppermute x2, waiting for transfers between devices: 78.2 us -> 57.9 us  [fetch_items(): arrived = lax.ppermute(leaving, 'node', swap)]
    all_to_all x2 -> x1, waiting for transfers between devices: 18 us -> 0.01 us  [exchange(): return lax.all_to_all(x, 'node', 0, 0, axis_index_groups=halves, tiled=True)]
    ppermute x30 -> x45, starting transfers between devices: 36.7 us -> 50.4 us  [trade(): got.append(array if still else lax.ppermute(array, 'node', pairs))]
    all_to_all x2 -> x1, starting transfers between devices: 11.4 us -> 6.37 us  [exchange(): return lax.all_to_all(x, 'node', 0, 0, axis_index_groups=halves, tiled=True)]
    pallas_call x2 -> x1, Pallas kernels: 14.4 us -> 9.59 us  [chain(): pl.pallas_call(functools.partial(chain_kernel, parts), grid_spec=pltpu.Pr...]
    ppermute x30 -> x45, waiting for transfers between devices: 81.2 us -> 77.1 us  [trade(): got.append(array if still else lax.ppermute(array, 'node', pairs))]
    pallas_call x1 -> x2, Pallas kernels: 4.34 us -> 8.22 us  [scatter(): pl.pallas_call(functools.partial(scatter_kernel, len(spread)), in_specs=[...]
  transfers between devices with their start and end apart: 34 -> 48, of which waited for: 19 -> 24; matrix products, arithmetic and copies ran while one was open for 3% -> 3% of each run, Pallas kernels for 6% -> 7%
where the time goes in v8:
time: 278 us; the launch traced here: 277 us
  waiting for transfers between devices  135 us (49%)
  starting transfers between devices  59.9 us (22%)
  local copies, waits for them, and re-layouts  47 us (17%)
  Pallas kernels  32.6 us (12%)
    ppermute x45, waiting for transfers between devices, trade(): got.append(array if still else lax.ppermute(array, 'node', pairs))  77.1 us
    ppermute x2, waiting for transfers between devices, fetch_items(): arrived = lax.ppermute(leaving, 'node', swap)  57.9 us
    ppermute x45, starting transfers between devices, trade(): got.append(array if still else lax.ppermute(array, 'node', pairs))  50.4 us
    unnamed x154, local copies, waits for them, and re-layouts  40.1 us
    pallas_call x1, Pallas kernels, chain(): pl.pallas_call(functools.partial(chain_kernel, parts), grid_spec=pltpu.Pr...  9.59 us
    pallas_call x2, Pallas kernels, scatter(): pl.pallas_call(functools.partial(scatter_kernel, len(spread)), in_specs=[...  8.22 us
    pallas_call x1, Pallas kernels, make_plan(): pl.pallas_call(functools.partial(plan_kernel, room), in_specs=[SMEM] * 2,...  6.59 us
    all_to_all x1, starting transfers between devices, exchange(): return lax.all_to_all(x, 'node', 0, 0, axis_index_groups=halves, tiled=True)  6.37 us
  transfers between devices with their start and end apart: 48, of which 24 were waited for; matrix products, arithmetic and copies ran while one was open for 3% of the time, Pallas kernels for 7%

profile of v8, /device:TPU:0, one launch (start us, length us, event | category | flops | bytes accessed | tf_op | source)
XLA Modules:
  0.0 277.3 jit_solution(5580331945500461218)
XLA Ops:
  0.0 2.7 cut_rows.1
  2.7 6.4 %all-to-all-start = ((f32[16,8,2,16,128]{4,3,2,1,0:T(8,128)}), f32[16,8,2,16,128]{4,3,2,1,0:T(8,128)}, u32[]{:S(2)}, u32[]{:S(2)}) async-start(f32[16,8,2,16,128]{4,3,2,1,0:T(8,128)} %cut_rows.1), calls=%async_computation | async-start | bytes 4194304 | tf_op jit(solution)/shard_map/all_to_all | solution.py:277
  9.1 3.0 %split_rows.1 = (f32[8,2,16,128]{3,2,1,0:T(8,128)S(1)}, f32[8,2,16,128]{3,2,1,0:T(8,128)}, f32[8,2,16,128]{3,2,1,0:T(8,128)}, f32[8,2,16,128]{3,2,1,0:T(8,128)},...) custom-call(s32[1]{0:T(128)} %bitcast.35.member_ref.member, ...), custom_call_target="tpu_custom_call" | custom-call | tf_op jit(solution)/shard_map/split_rows/pallas_call | solution.py:57
  14.1 1.7 collective-permute-start.21
  16.3 2.6 collective-permute-start.23
  18.9 23.3 %collective-permute-done.19.refs_2_ = f32[8,2,16,128]{3,2,1,0:T(8,128)S(1)} collective-permute-done((f32[8,2,16,128]{3,2,1,0:T(8,128)}, f32[8,2,16,128]{3,2,1,0:T(8,128)S(1)}, u32[]{:S(2)}, u32[]{:S(2)}) %collective-permute-start.19) | collective-permute-done | bytes 131104 | tf_op jit(solution)/shard_map/ppermute | solution.py:286
  46.4 2.3 collective-permute-start.28
  49.0 2.9 %collective-permute-start.29 = (f32[8,2,16,128]{3,2,1,0:T(8,128)}, f32[8,2,16,128]{3,2,1,0:T(8,128)S(1)}, u32[]{:S(2)}, u32[]{:S(2)}) collective-permute-start(f32[8,2,16,128]{3,2,1,0:T(8,128)} %get-tuple-element.146), channel_id=1, source_target_pairs={{0,12},{1,13},{2,14},{3,15},{4,8},{5,9},{6,10},{7,11},{8,4},{9,5},... | collective-permute-start | bytes 393224 | tf_op jit(solution)/shard_map/ppermute | solution.py:286
  53.5 2.5 collective-permute-start.31
  56.5 1.9 gather_fusion.2
  60.4 6.6 %make_plan.1 = (s32[128]{0:T(128)S(1)}, s32[192]{0:T(256)S(1)}, s32[1]{0:T(128)}) custom-call(s32[1]{0:T(128)} %bitcast.36.half_ref, s32[384]{0:T(512)S(1)} %reshape_reshape.3.ids_ref), custom_call_target="tpu_custom_call" | custom-call | tf_op jit(solution)/shard_map/make_plan/pallas_call | solution.py:132
  67.5 3.0 %collective-permute-done.32.refs_15_ = f32[8,2,16,128]{3,2,1,0:T(8,128)S(1)} collective-permute-done((f32[8,2,16,128]{3,2,1,0:T(8,128)}, f32[8,2,16,128]{3,2,1,0:T(8,128)S(1)}, u32[]{:S(2)}, u32[]{:S(2)}) %collective-permute-start.32) | collective-permute-done | bytes 131104 | tf_op jit(solution)/shard_map/ppermute | solution.py:286
  71.3 2.7 collective-permute-start.33
  79.1 57.9 %collective-permute-done.33.arrived_ref = f32[58,2,16,128]{3,2,1,0:T(8,128)} collective-permute-done((f32[58,2,16,128]{3,2,1,0:T(8,128)S(1)}, f32[58,2,16,128]{3,2,1,0:T(8,128)}, u32[]{:S(2)}, u32[]{:S(2)}) %collective-permute-start.33) | collective-permute-done | bytes 950304 | tf_op jit(solution)/shard_map/ppermute | solution.py:306
  137.0 4.3 %scatter.3 = (f32[12,2,16,128]{3,2,1,0:T(8,128)S(1)}, f32[12,2,16,128]{3,2,1,0:T(8,128)S(1)}, f32[12,2,16,128]{3,2,1,0:T(8,128)}, f32[12,2,16,128]{3,2,1,0:T(8,1...) custom-call(s32[192]{0:T(256)S(1)} %get-tuple-element.115.source_ref, ...), custom_call_target="tpu_custom_call" | custom-call | tf_op jit(solution)/shard_map/scatter/pallas_call | solution.py:251
  147.5 1.8 collective-permute-start.36
  152.6 2.9 %collective-permute-done.35.refs_18_ = f32[12,2,16,128]{3,2,1,0:T(8,128)S(1)} collective-permute-done((f32[12,2,16,128]{3,2,1,0:T(8,128)}, f32[12,2,16,128]{3,2,1,0:T(8,128)S(1)}, u32[]{:S(2)}, u32[]{:S(2)}) %collective-permute-start.35) | collective-permute-done | bytes 196640 | tf_op jit(solution)/shard_map/ppermute | solution.py:286
  156.5 2.2 collective-permute-done.36.refs_19_
  160.5 6.9 %collective-permute-done.37.refs_20_ = f32[12,2,16,128]{3,2,1,0:T(8,128)S(1)} collective-permute-done((f32[12,2,16,128]{3,2,1,0:T(8,128)}, f32[12,2,16,128]{3,2,1,0:T(8,128)S(1)}, u32[]{:S(2)}, u32[]{:S(2)}) %collective-permute-start.37) | collective-permute-done | bytes 196640 | tf_op jit(solution)/shard_map/ppermute | solution.py:286
  167.4 2.8 %collective-permute-done.38.refs_21_ = f32[12,2,16,128]{3,2,1,0:T(8,128)S(1)} collective-permute-done((f32[12,2,16,128]{3,2,1,0:T(8,128)}, f32[12,2,16,128]{3,2,1,0:T(8,128)S(1)}, u32[]{:S(2)}, u32[]{:S(2)}) %collective-permute-start.38) | collective-permute-done | bytes 196640 | tf_op jit(solution)/shard_map/ppermute | solution.py:286
  178.3 3.8 %collective-permute-done.43.refs_26_ = f32[12,2,16,128]{3,2,1,0:T(8,128)S(1)} collective-permute-done((f32[12,2,16,128]{3,2,1,0:T(8,128)}, f32[12,2,16,128]{3,2,1,0:T(8,128)S(1)}, u32[]{:S(2)}, u32[]{:S(2)}) %collective-permute-start.43) | collective-permute-done | bytes 196640 | tf_op jit(solution)/shard_map/ppermute | solution.py:286
  184.4 3.9 %scatter.2 = (f32[12,2,16,128]{3,2,1,0:T(8,128)S(1)}, f32[12,2,16,128]{3,2,1,0:T(8,128)S(1)}, f32[12,2,16,128]{3,2,1,0:T(8,128)S(1)}, f32[12,2,16,128]{3,2,1,0:T...) custom-call(s32[192]{0:T(256)S(1)} %get-tuple-element.115.source_ref, ...), custom_call_target="tpu_custom_call" | custom-call | tf_op jit(solution)/shard_map/scatter/pallas_call | solution.py:251
  189.7 2.4 collective-permute-start.3
  192.8 1.9 collective-permute-start.4
  196.3 3.6 %collective-permute-done.47.refs_30_ = f32[12,2,16,128]{3,2,1,0:T(8,128)S(1)} collective-permute-done((f32[12,2,16,128]{3,2,1,0:T(8,128)}, f32[12,2,16,128]{3,2,1,0:T(8,128)S(1)}, u32[]{:S(2)}, u32[]{:S(2)}) %collective-permute-start.47) | collective-permute-done | bytes 196640 | tf_op jit(solution)/shard_map/ppermute | solution.py:286
  213.9 4.8 %collective-permute-done.7.refs_5_ = f32[12,2,16,128]{3,2,1,0:T(8,128)S(1)} collective-permute-done((f32[12,2,16,128]{3,2,1,0:T(8,128)S(1)}, f32[12,2,16,128]{3,2,1,0:T(8,128)S(1)}, u32[]{:S(2)}, u32[]{:S(2)}) %collective-permute-start.7) | collective-permute-done | bytes 196640 | tf_op jit(solution)/shard_map/ppermute | solution.py:286
  220.9 4.5 %collective-permute-start.14 = (f32[12,2,16,128]{3,2,1,0:T(8,128)}, f32[12,2,16,128]{3,2,1,0:T(8,128)S(1)}, u32[]{:S(2)}, u32[]{:S(2)}) collective-permute-start(f32[12,2,16,128]{3,2,1,0:T(8,128)} %get-tuple-element.130), channel_id=1, source_target_pairs={{0,12},{1,13},{2,14},{3,15},{4,8},{5,9},{6,10},{7,11},{8,4},{9,5},... | collective-permute-start | bytes 589832 | tf_op jit(solution)/shard_map/ppermute | solution.py:286
  231.7 5.3 %collective-permute-done.14.refs_12_ = f32[12,2,16,128]{3,2,1,0:T(8,128)S(1)} collective-permute-done((f32[12,2,16,128]{3,2,1,0:T(8,128)}, f32[12,2,16,128]{3,2,1,0:T(8,128)S(1)}, u32[]{:S(2)}, u32[]{:S(2)}) %collective-permute-start.14) | collective-permute-done | bytes 196640 | tf_op jit(solution)/shard_map/ppermute | solution.py:286
  237.7 1.8 collective-permute-done.15.refs_13_
  240.2 4.2 %collective-permute-done.16.refs_14_ = f32[12,2,16,128]{3,2,1,0:T(8,128)S(1)} collective-permute-done((f32[12,2,16,128]{3,2,1,0:T(8,128)}, f32[12,2,16,128]{3,2,1,0:T(8,128)S(1)}, u32[]{:S(2)}, u32[]{:S(2)}) %collective-permute-start.16) | collective-permute-done | bytes 196640 | tf_op jit(solution)/shard_map/ppermute | solution.py:286
  245.0 4.3 %collective-permute-done.17.refs_15_ = f32[12,2,16,128]{3,2,1,0:T(8,128)S(1)} collective-permute-done((f32[12,2,16,128]{3,2,1,0:T(8,128)}, f32[12,2,16,128]{3,2,1,0:T(8,128)S(1)}, u32[]{:S(2)}, u32[]{:S(2)}) %collective-permute-start.17) | collective-permute-done | bytes 196640 | tf_op jit(solution)/shard_map/ppermute | solution.py:286
  267.7 9.6 %chain.1 = f32[2,2,256,256]{3,2,1,0:T(8,128)} custom-call(s32[1]{0:T(128)} %bitcast.35.member_ref.member, s32[4]{0:T(128)S(1)} %subtract_reduce_fusion.slot, s32[4]{0:T(128)S(1)} %dynamic-slice_subtract_fusion.target, s32[4]{0:T(128)S(1)} %dynamic_slice.12.sign, f32[8,2,256,256]{3,2,1,0:T(8,128)} %node_ref.1, f32[12,2,16,128]{3,2,1,0:T(8,128)S(1)} %copy-done.20, ...), custom_call_target="tpu_custom_call" | custom-call | tf_op jit(solution)/shard_map/chain/pallas_call | solution.py:446
  (248 shorter events, 88.7 us)
Async XLA Ops:
  2.7 71.3 %all-to-all-start = ((f32[16,8,2,16,128]{4,3,2,1,0:T(8,128)}), f32[16,8,2,16,128]{4,3,2,1,0:T(8,128)}, u32[]{:S(2)}, u32[]{:S(2)}) async-start(f32[16,8,2,16,128]{4,3,2,1,0:T(8,128)} %cut_rows.1), calls=%async_computation | async-start | bytes 4194304 | tf_op jit(solution)/shard_map/all_to_all | solution.py:277
  12.5 29.6 %collective-permute-start.19 = (f32[8,2,16,128]{3,2,1,0:T(8,128)}, f32[8,2,16,128]{3,2,1,0:T(8,128)S(1)}, u32[]{:S(2)}, u32[]{:S(2)}) collective-permute-start(f32[8,2,16,128]{3,2,1,0:T(8,128)} %get-tuple-element.136), channel_id=1, source_target_pairs={{0,2},{1,3},{2,0},{3,1},{4,6},{5,7},{6,4},{7,5},{8,10},{9,11},{10,... | collective-permute-start | bytes 393224 | tf_op jit(solution)/shard_map/ppermute | solution.py:286
  14.1 29.7 %collective-permute-start.20 = (f32[8,2,16,128]{3,2,1,0:T(8,128)}, f32[8,2,16,128]{3,2,1,0:T(8,128)S(1)}, u32[]{:S(2)}, u32[]{:S(2)}) collective-permute-start(f32[8,2,16,128]{3,2,1,0:T(8,128)} %get-tuple-element.137), channel_id=1, source_target_pairs={{0,3},{1,2},{2,1},{3,0},{4,7},{5,6},{6,5},{7,4},{8,11},{9,10},{10,... | collective-permute-start | bytes 393224 | tf_op jit(solution)/shard_map/ppermute | solution.py:286
  14.1 31.3 %collective-permute-start.21 = (f32[8,2,16,128]{3,2,1,0:T(8,128)}, f32[8,2,16,128]{3,2,1,0:T(8,128)S(1)}, u32[]{:S(2)}, u32[]{:S(2)}) collective-permute-start(f32[8,2,16,128]{3,2,1,0:T(8,128)} %get-tuple-element.138), channel_id=1, source_target_pairs={{0,4},{1,5},{2,6},{3,7},{4,0},{5,1},{6,2},{7,3},{8,12},{9,13},{10,... | collective-permute-start | bytes 393224 | tf_op jit(solution)/shard_map/ppermute | solution.py:286
  15.9 30.5 %collective-permute-start.22 = (f32[8,2,16,128]{3,2,1,0:T(8,128)}, f32[8,2,16,128]{3,2,1,0:T(8,128)S(1)}, u32[]{:S(2)}, u32[]{:S(2)}) collective-permute-start(f32[8,2,16,128]{3,2,1,0:T(8,128)} %get-tuple-element.139), channel_id=1, source_target_pairs={{0,5},{1,4},{2,7},{3,6},{4,1},{5,0},{6,3},{7,2},{8,13},{9,12},{10,... | collective-permute-start | bytes 393224 | tf_op jit(solution)/shard_map/ppermute | solution.py:286
  16.3 30.2 %collective-permute-start.23 = (f32[8,2,16,128]{3,2,1,0:T(8,128)}, f32[8,2,16,128]{3,2,1,0:T(8,128)S(1)}, u32[]{:S(2)}, u32[]{:S(2)}) collective-permute-start(f32[8,2,16,128]{3,2,1,0:T(8,128)} %get-tuple-element.140), channel_id=1, source_target_pairs={{0,6},{1,7},{2,4},{3,5},{4,2},{5,3},{6,0},{7,1},{8,14},{9,15},{10,... | collective-permute-start | bytes 393224 | tf_op jit(solution)/shard_map/ppermute | solution.py:286
  46.4 20.5 %collective-permute-start.28 = (f32[8,2,16,128]{3,2,1,0:T(8,128)}, f32[8,2,16,128]{3,2,1,0:T(8,128)S(1)}, u32[]{:S(2)}, u32[]{:S(2)}) collective-permute-start(f32[8,2,16,128]{3,2,1,0:T(8,128)} %get-tuple-element.145), channel_id=1, source_target_pairs={{0,11},{1,10},{2,9},{3,8},{4,15},{5,14},{6,13},{7,12},{8,3},{9,2},... | collective-permute-start | bytes 393224 | tf_op jit(solution)/shard_map/ppermute | solution.py:286
  49.0 18.0 %collective-permute-start.29 = (f32[8,2,16,128]{3,2,1,0:T(8,128)}, f32[8,2,16,128]{3,2,1,0:T(8,128)S(1)}, u32[]{:S(2)}, u32[]{:S(2)}) collective-permute-start(f32[8,2,16,128]{3,2,1,0:T(8,128)} %get-tuple-element.146), channel_id=1, source_target_pairs={{0,12},{1,13},{2,14},{3,15},{4,8},{5,9},{6,10},{7,11},{8,4},{9,5},... | collective-permute-start | bytes 393224 | tf_op jit(solution)/shard_map/ppermute | solution.py:286
  51.9 15.1 %collective-permute-start.30 = (f32[8,2,16,128]{3,2,1,0:T(8,128)}, f32[8,2,16,128]{3,2,1,0:T(8,128)S(1)}, u32[]{:S(2)}, u32[]{:S(2)}) collective-permute-start(f32[8,2,16,128]{3,2,1,0:T(8,128)} %get-tuple-element.147), channel_id=1, source_target_pairs={{0,13},{1,12},{2,15},{3,14},{4,9},{5,8},{6,11},{7,10},{8,5},{9,4},... | collective-permute-start | bytes 393224 | tf_op jit(solution)/shard_map/ppermute | solution.py:286
  53.5 14.0 %collective-permute-start.31 = (f32[8,2,16,128]{3,2,1,0:T(8,128)}, f32[8,2,16,128]{3,2,1,0:T(8,128)S(1)}, u32[]{:S(2)}, u32[]{:S(2)}) collective-permute-start(f32[8,2,16,128]{3,2,1,0:T(8,128)} %get-tuple-element.148), channel_id=1, source_target_pairs={{0,14},{1,15},{2,12},{3,13},{4,10},{5,11},{6,8},{7,9},{8,6},{9,7},... | collective-permute-start | bytes 393224 | tf_op jit(solution)/shard_map/ppermute | solution.py:286
  56.2 14.3 %collective-permute-start.32 = (f32[8,2,16,128]{3,2,1,0:T(8,128)}, f32[8,2,16,128]{3,2,1,0:T(8,128)S(1)}, u32[]{:S(2)}, u32[]{:S(2)}) collective-permute-start(f32[8,2,16,128]{3,2,1,0:T(8,128)} %get-tuple-element.149), channel_id=1, source_target_pairs={{0,15},{1,14},{2,13},{3,12},{4,11},{5,10},{6,9},{7,8},{8,7},{9,6},... | collective-permute-start | bytes 393224 | tf_op jit(solution)/shard_map/ppermute | solution.py:286
  71.3 65.7 %collective-permute-start.33 = (f32[58,2,16,128]{3,2,1,0:T(8,128)S(1)}, f32[58,2,16,128]{3,2,1,0:T(8,128)}, u32[]{:S(2)}, u32[]{:S(2)}) collective-permute-start(f32[58,2,16,128]{3,2,1,0:T(8,128)S(1)} %pick_leaving.3), channel_id=1, source_target_pairs={{0,16},{1,17},{2,18},{3,19},{4,20},{5,21},{6,22},{7,23},{8,24},{9,... | collective-permute-start | bytes 2850824 | tf_op jit(solution)/shard_map/ppermute | solution.py:306
  75.7 108.3 %collective-permute-start.2 = (f32[58,2,16,128]{3,2,1,0:T(8,128)S(1)}, f32[58,2,16,128]{3,2,1,0:T(8,128)S(1)}, u32[]{:S(2)}, u32[]{:S(2)}) collective-permute-start(f32[58,2,16,128]{3,2,1,0:T(8,128)S(1)} %pick_leaving.2), channel_id=1, source_target_pairs={{0,16},{1,17},{2,18},{3,19},{4,20},{5,21},{6,22},{7,23},{8,24},{9,... | collective-permute-start | bytes 2850824 | tf_op jit(solution)/shard_map/ppermute | solution.py:306
  150.9 16.4 %collective-permute-start.37 = (f32[12,2,16,128]{3,2,1,0:T(8,128)}, f32[12,2,16,128]{3,2,1,0:T(8,128)S(1)}, u32[]{:S(2)}, u32[]{:S(2)}) collective-permute-start(f32[12,2,16,128]{3,2,1,0:T(8,128)} %get-tuple-element.154), channel_id=1, source_target_pairs={{0,4},{1,5},{2,6},{3,7},{4,0},{5,1},{6,2},{7,3},{8,12},{9,13},{10,... | collective-permute-start | bytes 589832 | tf_op jit(solution)/shard_map/ppermute | solution.py:286
  151.0 19.2 %collective-permute-start.38 = (f32[12,2,16,128]{3,2,1,0:T(8,128)}, f32[12,2,16,128]{3,2,1,0:T(8,128)S(1)}, u32[]{:S(2)}, u32[]{:S(2)}) collective-permute-start(f32[12,2,16,128]{3,2,1,0:T(8,128)} %get-tuple-element.155), channel_id=1, source_target_pairs={{0,5},{1,4},{2,7},{3,6},{4,1},{5,0},{6,3},{7,2},{8,13},{9,12},{10,... | collective-permute-start | bytes 589832 | tf_op jit(solution)/shard_map/ppermute | solution.py:286
  155.5 14.7 %collective-permute-start.39 = (f32[12,2,16,128]{3,2,1,0:T(8,128)}, f32[12,2,16,128]{3,2,1,0:T(8,128)S(1)}, u32[]{:S(2)}, u32[]{:S(2)}) collective-permute-start(f32[12,2,16,128]{3,2,1,0:T(8,128)} %copy-done.55), channel_id=1, source_target_pairs={{0,6},{1,7},{2,4},{3,5},{4,2},{5,3},{6,0},{7,1},{8,14},{9,15},{10,... | collective-permute-start | bytes 589832 | tf_op jit(solution)/shard_map/ppermute | solution.py:286
  172.6 16.4 %collective-permute-start.44 = (f32[12,2,16,128]{3,2,1,0:T(8,128)}, f32[12,2,16,128]{3,2,1,0:T(8,128)S(1)}, u32[]{:S(2)}, u32[]{:S(2)}) collective-permute-start(f32[12,2,16,128]{3,2,1,0:T(8,128)} %copy-done.50), channel_id=1, source_target_pairs={{0,11},{1,10},{2,9},{3,8},{4,15},{5,14},{6,13},{7,12},{8,3},{9,2},... | collective-permute-start | bytes 589832 | tf_op jit(solution)/shard_map/ppermute | solution.py:286
  174.3 17.7 %collective-permute-start.45 = (f32[12,2,16,128]{3,2,1,0:T(8,128)}, f32[12,2,16,128]{3,2,1,0:T(8,128)S(1)}, u32[]{:S(2)}, u32[]{:S(2)}) collective-permute-start(f32[12,2,16,128]{3,2,1,0:T(8,128)} %copy-done.49), channel_id=1, source_target_pairs={{0,12},{1,13},{2,14},{3,15},{4,8},{5,9},{6,10},{7,11},{8,4},{9,5},... | collective-permute-start | bytes 589832 | tf_op jit(solution)/shard_map/ppermute | solution.py:286
  177.6 17.1 %collective-permute-start.46 = (f32[12,2,16,128]{3,2,1,0:T(8,128)}, f32[12,2,16,128]{3,2,1,0:T(8,128)S(1)}, u32[]{:S(2)}, u32[]{:S(2)}) collective-permute-start(f32[12,2,16,128]{3,2,1,0:T(8,128)} %copy-done.48), channel_id=1, source_target_pairs={{0,13},{1,12},{2,15},{3,14},{4,9},{5,8},{6,11},{7,10},{8,5},{9,4},... | collective-permute-start | bytes 589832 | tf_op jit(solution)/shard_map/ppermute | solution.py:286
  182.7 17.2 %collective-permute-start.47 = (f32[12,2,16,128]{3,2,1,0:T(8,128)}, f32[12,2,16,128]{3,2,1,0:T(8,128)S(1)}, u32[]{:S(2)}, u32[]{:S(2)}) collective-permute-start(f32[12,2,16,128]{3,2,1,0:T(8,128)} %copy-done.47), channel_id=1, source_target_pairs={{0,14},{1,15},{2,12},{3,13},{4,10},{5,11},{6,8},{7,9},{8,6},{9,7},... | collective-permute-start | bytes 589832 | tf_op jit(solution)/shard_map/ppermute | solution.py:286
  184.0 18.9 %collective-permute-start.48 = (f32[12,2,16,128]{3,2,1,0:T(8,128)S(1)}, f32[12,2,16,128]{3,2,1,0:T(8,128)S(1)}, u32[]{:S(2)}, u32[]{:S(2)}) collective-permute-start(f32[12,2,16,128]{3,2,1,0:T(8,128)S(1)} %get-tuple-element.165), channel_id=1, source_target_pairs={{0,15},{1,14},{2,13},{3,12},{4,11},{5,10},{6,9},{7,8},{8,7},{9,6},... | collective-permute-start | bytes 589832 | tf_op jit(solution)/shard_map/ppermute | solution.py:286
  189.7 14.9 %collective-permute-start.3 = (f32[12,2,16,128]{3,2,1,0:T(8,128)S(1)}, f32[12,2,16,128]{3,2,1,0:T(8,128)S(1)}, u32[]{:S(2)}, u32[]{:S(2)}) collective-permute-start(f32[12,2,16,128]{3,2,1,0:T(8,128)S(1)} %get-tuple-element.119), channel_id=1, source_target_pairs={{0,1},{1,0},{2,3},{3,2},{4,5},{5,4},{6,7},{7,6},{8,9},{9,8},{10,11... | collective-permute-start | bytes 589832 | tf_op jit(solution)/shard_map/ppermute | solution.py:286
  192.8 14.2 %collective-permute-start.4 = (f32[12,2,16,128]{3,2,1,0:T(8,128)S(1)}, f32[12,2,16,128]{3,2,1,0:T(8,128)S(1)}, u32[]{:S(2)}, u32[]{:S(2)}) collective-permute-start(f32[12,2,16,128]{3,2,1,0:T(8,128)S(1)} %get-tuple-element.120), channel_id=1, source_target_pairs={{0,2},{1,3},{2,0},{3,1},{4,6},{5,7},{6,4},{7,5},{8,10},{9,11},{10,... | collective-permute-start | bytes 589832 | tf_op jit(solution)/shard_map/ppermute | solution.py:286
  195.4 15.1 %collective-permute-start.5 = (f32[12,2,16,128]{3,2,1,0:T(8,128)S(1)}, f32[12,2,16,128]{3,2,1,0:T(8,128)S(1)}, u32[]{:S(2)}, u32[]{:S(2)}) collective-permute-start(f32[12,2,16,128]{3,2,1,0:T(8,128)S(1)} %get-tuple-element.121), channel_id=1, source_target_pairs={{0,3},{1,2},{2,1},{3,0},{4,7},{5,6},{6,5},{7,4},{8,11},{9,10},{10,... | collective-permute-start | bytes 589832 | tf_op jit(solution)/shard_map/ppermute | solution.py:286
  203.6 15.2 %collective-permute-start.7 = (f32[12,2,16,128]{3,2,1,0:T(8,128)S(1)}, f32[12,2,16,128]{3,2,1,0:T(8,128)S(1)}, u32[]{:S(2)}, u32[]{:S(2)}) collective-permute-start(f32[12,2,16,128]{3,2,1,0:T(8,128)S(1)} %get-tuple-element.123), channel_id=1, source_target_pairs={{0,5},{1,4},{2,7},{3,6},{4,1},{5,0},{6,3},{7,2},{8,13},{9,12},{10,... | collective-permute-start | bytes 589832 | tf_op jit(solution)/shard_map/ppermute | solution.py:286
  204.6 14.9 %collective-permute-start.8 = (f32[12,2,16,128]{3,2,1,0:T(8,128)S(1)}, f32[12,2,16,128]{3,2,1,0:T(8,128)S(1)}, u32[]{:S(2)}, u32[]{:S(2)}) collective-permute-start(f32[12,2,16,128]{3,2,1,0:T(8,128)S(1)} %get-tuple-element.124), channel_id=1, source_target_pairs={{0,6},{1,7},{2,4},{3,5},{4,2},{5,3},{6,0},{7,1},{8,14},{9,15},{10,... | collective-permute-start | bytes 589832 | tf_op jit(solution)/shard_map/ppermute | solution.py:286
  211.1 14.4 %collective-permute-start.10 = (f32[12,2,16,128]{3,2,1,0:T(8,128)S(1)}, f32[12,2,16,128]{3,2,1,0:T(8,128)S(1)}, u32[]{:S(2)}, u32[]{:S(2)}) collective-permute-start(f32[12,2,16,128]{3,2,1,0:T(8,128)S(1)} %get-tuple-element.126), channel_id=1, source_target_pairs={{0,8},{1,9},{2,10},{3,11},{4,12},{5,13},{6,14},{7,15},{8,0},{9,1},... | collective-permute-start | bytes 589832 | tf_op jit(solution)/shard_map/ppermute | solution.py:286
  212.2 14.6 %collective-permute-start.11 = (f32[12,2,16,128]{3,2,1,0:T(8,128)S(1)}, f32[12,2,16,128]{3,2,1,0:T(8,128)S(1)}, u32[]{:S(2)}, u32[]{:S(2)}) collective-permute-start(f32[12,2,16,128]{3,2,1,0:T(8,128)S(1)} %get-tuple-element.127), channel_id=1, source_target_pairs={{0,9},{1,8},{2,11},{3,10},{4,13},{5,12},{6,15},{7,14},{8,1},{9,0},... | collective-permute-start | bytes 589832 | tf_op jit(solution)/shard_map/ppermute | solution.py:286
  220.9 16.1 %collective-permute-start.14 = (f32[12,2,16,128]{3,2,1,0:T(8,128)}, f32[12,2,16,128]{3,2,1,0:T(8,128)S(1)}, u32[]{:S(2)}, u32[]{:S(2)}) collective-permute-start(f32[12,2,16,128]{3,2,1,0:T(8,128)} %get-tuple-element.130), channel_id=1, source_target_pairs={{0,12},{1,13},{2,14},{3,15},{4,8},{5,9},{6,10},{7,11},{8,4},{9,5},... | collective-permute-start | bytes 589832 | tf_op jit(solution)/shard_map/ppermute | solution.py:286
  226.2 13.4 %collective-permute-start.15 = (f32[12,2,16,128]{3,2,1,0:T(8,128)}, f32[12,2,16,128]{3,2,1,0:T(8,128)S(1)}, u32[]{:S(2)}, u32[]{:S(2)}) collective-permute-start(f32[12,2,16,128]{3,2,1,0:T(8,128)} %get-tuple-element.131), channel_id=1, source_target_pairs={{0,13},{1,12},{2,15},{3,14},{4,9},{5,8},{6,11},{7,10},{8,5},{9,4},... | collective-permute-start | bytes 589832 | tf_op jit(solution)/shard_map/ppermute | solution.py:286
  227.5 16.9 %collective-permute-start.16 = (f32[12,2,16,128]{3,2,1,0:T(8,128)}, f32[12,2,16,128]{3,2,1,0:T(8,128)S(1)}, u32[]{:S(2)}, u32[]{:S(2)}) collective-permute-start(f32[12,2,16,128]{3,2,1,0:T(8,128)} %get-tuple-element.132), channel_id=1, source_target_pairs={{0,14},{1,15},{2,12},{3,13},{4,10},{5,11},{6,8},{7,9},{8,6},{9,7},... | collective-permute-start | bytes 589832 | tf_op jit(solution)/shard_map/ppermute | solution.py:286
  229.8 19.6 %collective-permute-start.17 = (f32[12,2,16,128]{3,2,1,0:T(8,128)}, f32[12,2,16,128]{3,2,1,0:T(8,128)S(1)}, u32[]{:S(2)}, u32[]{:S(2)}) collective-permute-start(f32[12,2,16,128]{3,2,1,0:T(8,128)} %get-tuple-element.133), channel_id=1, source_target_pairs={{0,15},{1,14},{2,13},{3,12},{4,11},{5,10},{6,9},{7,8},{8,7},{9,6},... | collective-permute-start | bytes 589832 | tf_op jit(solution)/shard_map/ppermute | solution.py:286
  (93 other events, 1020.1 us)

commit v9 on v7

--- a/solution.py
+++ b/solution.py
@@ -353,9 +353,9 @@
     return jnp.concatenate([ref[0, 0], ref[0, 1]], axis=1)
 
 
-def triple_spec(array):
+def triple_spec(array, each=1):
     group, _, _, rows, width = array.shape
-    return pl.BlockSpec((group, 3, 2, rows, width), lambda k, *scalars: (0, k, 0, 0, 0))
+    return pl.BlockSpec((group, 3 * each, 2, rows, width), lambda k, *scalars: (0, k, 0, 0, 0))
 
 
 def multiply_kernel(which, index_ref, left_ref, *refs):
@@ -426,18 +426,32 @@
     )(target, sign, lefts, *rights)
 
 
-def chain_kernel(parts, member, slot, target, sign, node_ref, *refs):
+def chain_kernel(parts, each, member, slot, target, sign, *refs):
+    node_refs, refs = refs[:each], refs[each:]
     part_refs, got_refs, (out_ref, last_ref) = refs[:parts], refs[parts:-2], refs[-2:]
+    step = pl.program_id(0)
+    width = out_ref.shape[-1]
     for k, ref in enumerate(got_refs):
         rows = ref.shape[2]
         row = pl.multiple_of(partner(member[0], k, len(got_refs)) * rows, rows)
-        for which in range(3):
+        for which in range(3 * each):
             last_ref[which, 0, :, pl.ds(row, rows)] = ref[which]
-    left = wide(node_ref)
+    lefts = [wide(ref) for ref in node_refs]
     for which in range(3):
-        blocks = [ref[:, which] for ref in part_refs] + [last_ref[which]]
-        left = product(left, blocks)
-    add_result(pl.program_id(0), target, sign, left, out_ref)
+        for n in range(each):
+            item = 3 * n + which
+            blocks = [ref[:, item] for ref in part_refs] + [last_ref[item]]
+            lefts[n] = product(lefts[n], blocks)
+
+    @pl.when(step == 0)
+    def _():
+        out_ref[...] = jnp.zeros_like(out_ref)
+
+    for n, both in enumerate(lefts):
+        both = both * sign[step * each + n].astype(jnp.float32)
+        row = target[step * each + n]
+        out_ref[row, 0] += both[:, :width]
+        out_ref[row, 1] += both[:, width:]
 
 
 def chain(member, slot, target, sign, nodes, rights):
@@ -445,24 +459,30 @@
     whole = (RES_COL, 2, order, order)
     *parts, got = rights
     _, _, rows, width = got[0].shape
-
-    return pl.pallas_call(
-        functools.partial(chain_kernel, len(parts)),
+    each = 2 if slot.shape[0] % 2 == 0 else 1
+
+    def node_spec(n):
+        return pl.BlockSpec(
+            (1, 2, order, order), lambda k, m, slot, t, s: (slot[k * each + n], 0, 0, 0)
+        )
+
+    return pl.pallas_call(
+        functools.partial(chain_kernel, len(parts), each),
         grid_spec=pltpu.PrefetchScalarGridSpec(
             num_scalar_prefetch=4,
-            grid=(slot.shape[0],),
+            grid=(slot.shape[0] // each,),
             in_specs=[
-                pl.BlockSpec((1, 2, order, order), lambda k, m, slot, t, s: (slot[k], 0, 0, 0)),
-                *[triple_spec(part) for part in parts],
-                *[pl.BlockSpec((3, 2, rows, width), lambda k, *scalars: (k, 0, 0, 0))] * len(got),
+                *[node_spec(n) for n in range(each)],
+                *[triple_spec(part, each) for part in parts],
+                *[pl.BlockSpec((3 * each, 2, rows, width), lambda k, *scalars: (k, 0, 0, 0))] * len(got),
             ],
             out_specs=pl.BlockSpec(whole, lambda k, *scalars: (0, 0, 0, 0)),
-            scratch_shapes=[pltpu.VMEM((3, 1, 2, order, width), jnp.float32)],
+            scratch_shapes=[pltpu.VMEM((3 * each, 1, 2, order, width), jnp.float32)],
         ),
         out_shape=jax.ShapeDtypeStruct(whole, jnp.float32),
         compiler_params=CHAIN,
         name="chain",
-    )(member, slot, target, sign, nodes, *parts, *got)
+    )(member, slot, target, sign, *[nodes] * each, *parts, *got)
 
 
 def all_columns(x):

time: 294 us -> 293 us (level)
  no operation moved by 1% of the time
where the time goes in v9:
time: 293 us
  waiting for transfers between devices  177 us (60%)
  starting transfers between devices  53.8 us (18%)
  Pallas kernels  34.8 us (12%)
  local copies, waits for them, and re-layouts  23.5 us (8%)
    ppermute x30, waiting for transfers between devices, trade(): got.append(array if still else lax.ppermute(array, 'node', pairs))  81.2 us
    ppermute x2, waiting for transfers between devices, fetch_items(): arrived = lax.ppermute(leaving, 'node', swap)  78.2 us
    ppermute x30, starting transfers between devices, trade(): got.append(array if still else lax.ppermute(array, 'node', pairs))  36.7 us
    all_to_all x2, waiting for transfers between devices, exchange(): return lax.all_to_all(x, 'node', 0, 0, axis_index_groups=halves, tiled=True)  18 us
    unnamed x50, local copies, waits for them, and re-layouts  16.4 us
    all_to_all x2, starting transfers between devices, exchange(): return lax.all_to_all(x, 'node', 0, 0, axis_index_groups=halves, tiled=True)  11.4 us
    pallas_call x1, Pallas kernels, chain(): pl.pallas_call(functools.partial(chain_kernel, len(parts), each), grid_sp...  8.83 us
    pallas_call x1, Pallas kernels, make_plan(): pl.pallas_call(functools.partial(plan_kernel, room), in_specs=[SMEM] * 2,...  6.59 us
  transfers between devices with their start and end apart: 34, of which 19 were waited for; matrix products, arithmetic and copies ran while one was open for 3% of the time, Pallas kernels for 6%

profile of v9, /device:TPU:0, one launch (start us, length us, event | category | flops | bytes accessed | tf_op | source)
XLA Modules:
  0.0 292.7 jit_solution(286696009397076448)
XLA Ops:
  0.0 2.7 cut_rows.1
  2.7 6.4 %all-to-all-start = ((f32[16,8,2,16,128]{4,3,2,1,0:T(8,128)}), f32[16,8,2,16,128]{4,3,2,1,0:T(8,128)S(1)}, u32[]{:S(2)}, u32[]{:S(2)}) async-start(f32[16,8,2,16,128]{4,3,2,1,0:T(8,128)} %cut_rows.1), calls=%async_computation | async-start | bytes 4194304 | tf_op jit(solution)/shard_map/all_to_all | solution.py:277
  9.8 1.9 gather_fusion.2
  13.7 6.6 %make_plan.1 = (s32[128]{0:T(128)S(1)}, s32[192]{0:T(256)S(1)}, s32[1]{0:T(128)}) custom-call(s32[1]{0:T(128)} %bitcast.36.half_ref, s32[384]{0:T(512)S(1)} %reshape_reshape.3.ids_ref), custom_call_target="tpu_custom_call" | custom-call | tf_op jit(solution)/shard_map/make_plan/pallas_call | solution.py:132
  20.3 18.0 %all-to-all-done = f32[16,8,2,16,128]{4,3,2,1,0:T(8,128)S(1)} async-done(((f32[16,8,2,16,128]{4,3,2,1,0:T(8,128)}), f32[16,8,2,16,128]{4,3,2,1,0:T(8,128)S(1)}, u32[]{:S(2)}, u32[]{:S(2)}) %all-to-all-start) | async-done | bytes 2097184 | tf_op jit(solution)/shard_map/all_to_all | solution.py:277
  41.3 2.7 collective-permute-start.2
  46.3 38.8 %collective-permute-done.2.arrived_ref = f32[58,2,16,128]{3,2,1,0:T(8,128)S(1)} collective-permute-done((f32[58,2,16,128]{3,2,1,0:T(8,128)S(1)}, f32[58,2,16,128]{3,2,1,0:T(8,128)S(1)}, u32[]{:S(2)}, u32[]{:S(2)}) %collective-permute-start.2) | collective-permute-done | bytes 950304 | tf_op jit(solution)/shard_map/ppermute | solution.py:306
  85.1 4.9 %collect.1 = f32[192,2,16,128]{3,2,1,0:T(8,128)} custom-call(s32[192]{0:T(256)S(1)} %get-tuple-element.99.source_ref, s32[1]{0:T(128)} %get-tuple-element.100.crowded_ref, f32[128,2,16,128]{3,2,1,0:T(8,128)} %bitcast.62, f32[58,2,16,128]{3,2,1,0:T(8,128)S(1)} %collective-permute-done.2.arrived_ref, f32[128,2,16,128]{3,2,1,0:T(8,128)} %get-tuple-element.134.extra_ref), custom_call_target="tpu_custom_call" | custom-call | tf_op jit(solution)/shard_map/collect/pallas_call | solution.py:202
  90.0 5.0 %all-to-all-start.1 = ((f32[16,12,2,16,128]{4,3,2,1,0:T(8,128)}), f32[16,12,2,16,128]{4,3,2,1,0:T(8,128)S(1)}, u32[]{:S(2)}, u32[]{:S(2)}) async-start(f32[16,12,2,16,128]{4,3,2,1,0:T(8,128)} %bitcast.39), calls=%async_computation.1 | async-start | bytes 6291456 | tf_op jit(solution)/shard_map/all_to_all | solution.py:277
  95.0 3.0 %split_rows.1 = (f32[8,2,16,128]{3,2,1,0:T(8,128)S(1)}, f32[8,2,16,128]{3,2,1,0:T(8,128)}, f32[8,2,16,128]{3,2,1,0:T(8,128)}, f32[8,2,16,128]{3,2,1,0:T(8,128)},...) custom-call(s32[1]{0:T(128)} %bitcast.35.member_ref.member, ...), custom_call_target="tpu_custom_call" | custom-call | tf_op jit(solution)/shard_map/split_rows/pallas_call | solution.py:57
  102.0 2.5 collective-permute-start.8
  104.5 38.4 %collective-permute-done.4.refs_2_ = f32[8,2,16,128]{3,2,1,0:T(8,128)S(1)} collective-permute-done((f32[8,2,16,128]{3,2,1,0:T(8,128)}, f32[8,2,16,128]{3,2,1,0:T(8,128)S(1)}, u32[]{:S(2)}, u32[]{:S(2)}) %collective-permute-start.4) | collective-permute-done | bytes 131104 | tf_op jit(solution)/shard_map/ppermute | solution.py:286
  149.1 3.8 %collective-permute-start.14 = (f32[8,2,16,128]{3,2,1,0:T(8,128)}, f32[8,2,16,128]{3,2,1,0:T(8,128)}, u32[]{:S(2)}, u32[]{:S(2)}) collective-permute-start(f32[8,2,16,128]{3,2,1,0:T(8,128)} %get-tuple-element.114), channel_id=1, source_target_pairs={{0,12},{1,13},{2,14},{3,15},{4,8},{5,9},{6,10},{7,11},{8,4},{9,5},... | collective-permute-start | bytes 393224 | tf_op jit(solution)/shard_map/ppermute | solution.py:286
  157.2 1.8 collective-permute-done.13.refs_11_
  159.0 2.8 collective-permute-done.14.refs_12_
  161.8 2.9 %collective-permute-done.15.refs_13_ = f32[8,2,16,128]{3,2,1,0:T(8,128)} collective-permute-done((f32[8,2,16,128]{3,2,1,0:T(8,128)}, f32[8,2,16,128]{3,2,1,0:T(8,128)}, u32[]{:S(2)}, u32[]{:S(2)}) %collective-permute-start.15) | collective-permute-done | bytes 131104 | tf_op jit(solution)/shard_map/ppermute | solution.py:286
  164.7 3.0 %collective-permute-done.16.refs_14_ = f32[8,2,16,128]{3,2,1,0:T(8,128)} collective-permute-done((f32[8,2,16,128]{3,2,1,0:T(8,128)}, f32[8,2,16,128]{3,2,1,0:T(8,128)}, u32[]{:S(2)}, u32[]{:S(2)}) %collective-permute-start.16) | collective-permute-done | bytes 131104 | tf_op jit(solution)/shard_map/ppermute | solution.py:286
  167.7 3.0 %collective-permute-done.17.refs_15_ = f32[8,2,16,128]{3,2,1,0:T(8,128)} collective-permute-done((f32[8,2,16,128]{3,2,1,0:T(8,128)}, f32[8,2,16,128]{3,2,1,0:T(8,128)}, u32[]{:S(2)}, u32[]{:S(2)}) %collective-permute-start.17) | collective-permute-done | bytes 131104 | tf_op jit(solution)/shard_map/ppermute | solution.py:286
  170.7 2.7 pick_leaving.3
  173.5 3.0 %collective-permute-start.18 = (f32[58,2,16,128]{3,2,1,0:T(8,128)}, f32[58,2,16,128]{3,2,1,0:T(8,128)}, u32[]{:S(2)}, u32[]{:S(2)}) collective-permute-start(f32[58,2,16,128]{3,2,1,0:T(8,128)} %pick_leaving.3), channel_id=1, source_target_pairs={{0,16},{1,17},{2,18},{3,19},{4,20},{5,21},{6,22},{7,23},{8,24},{9,... | collective-permute-start | bytes 2850824 | tf_op jit(solution)/shard_map/ppermute | solution.py:306
  178.9 39.4 %collective-permute-done.18.arrived_ref = f32[58,2,16,128]{3,2,1,0:T(8,128)} collective-permute-done((f32[58,2,16,128]{3,2,1,0:T(8,128)}, f32[58,2,16,128]{3,2,1,0:T(8,128)}, u32[]{:S(2)}, u32[]{:S(2)}) %collective-permute-start.18) | collective-permute-done | bytes 950304 | tf_op jit(solution)/shard_map/ppermute | solution.py:306
  218.2 4.3 %scatter.1 = (f32[12,2,16,128]{3,2,1,0:T(8,128)S(1)}, f32[12,2,16,128]{3,2,1,0:T(8,128)S(1)}, f32[12,2,16,128]{3,2,1,0:T(8,128)S(1)}, f32[12,2,16,128]{3,2,1,0:T...) custom-call(s32[192]{0:T(256)S(1)} %get-tuple-element.99.source_ref,, ...), custom_call_target="tpu_custom_call" | custom-call | tf_op jit(solution)/shard_map/scatter/pallas_call | solution.py:251
  224.5 1.9 collective-permute-start.22
  226.4 2.9 collective-permute-start.24
  237.6 5.9 %collective-permute-done.23.refs_8_ = f32[12,2,16,128]{3,2,1,0:T(8,128)S(1)} collective-permute-done((f32[12,2,16,128]{3,2,1,0:T(8,128)S(1)}, f32[12,2,16,128]{3,2,1,0:T(8,128)S(1)}, u32[]{:S(2)}, u32[]{:S(2)}) %collective-permute-start.23) | collective-permute-done | bytes 196640 | tf_op jit(solution)/shard_map/ppermute | solution.py:286
  248.7 1.9 collective-permute-start.30
  252.2 2.5 collective-permute-start.32
  258.5 4.6 %collective-permute-done.30.refs_15_ = f32[12,2,16,128]{3,2,1,0:T(8,128)} collective-permute-done((f32[12,2,16,128]{3,2,1,0:T(8,128)}, f32[12,2,16,128]{3,2,1,0:T(8,128)}, u32[]{:S(2)}, u32[]{:S(2)}) %collective-permute-start.30) | collective-permute-done | bytes 196640 | tf_op jit(solution)/shard_map/ppermute | solution.py:286
  263.2 4.0 %collective-permute-done.31.refs_16_ = f32[12,2,16,128]{3,2,1,0:T(8,128)} collective-permute-done((f32[12,2,16,128]{3,2,1,0:T(8,128)}, f32[12,2,16,128]{3,2,1,0:T(8,128)}, u32[]{:S(2)}, u32[]{:S(2)}) %collective-permute-start.31) | collective-permute-done | bytes 196640 | tf_op jit(solution)/shard_map/ppermute | solution.py:286
  267.2 4.2 %collective-permute-done.32.refs_17_ = f32[12,2,16,128]{3,2,1,0:T(8,128)} collective-permute-done((f32[12,2,16,128]{3,2,1,0:T(8,128)}, f32[12,2,16,128]{3,2,1,0:T(8,128)}, u32[]{:S(2)}, u32[]{:S(2)}) %collective-permute-start.32) | collective-permute-done | bytes 196640 | tf_op jit(solution)/shard_map/ppermute | solution.py:286
  271.4 4.1 %collective-permute-done.33.refs_18_ = f32[12,2,16,128]{3,2,1,0:T(8,128)} collective-permute-done((f32[12,2,16,128]{3,2,1,0:T(8,128)}, f32[12,2,16,128]{3,2,1,0:T(8,128)}, u32[]{:S(2)}, u32[]{:S(2)}) %collective-permute-start.33) | collective-permute-done | bytes 196640 | tf_op jit(solution)/shard_map/ppermute | solution.py:286
  283.9 8.8 %chain.1 = f32[2,2,256,256]{3,2,1,0:T(8,128)} custom-call(s32[1]{0:T(128)} %bitcast.35.member_ref.member, s32[4]{0:T(128)S(1)} %subtract_reduce_fusion.slot, s32[4]{0:T(128)S(1)} %dynamic-slice_subtract_fusion.target, s32[4]{0:T(128)S(1)} %dynamic_slice.12.sign, f32[8,2,256,256]{3,2,1,0:T(8,128)} %refs_1_.1, f32[8,2,256,256]{3,2,1,0:T(8,128)} %refs_1_.1, ...), custom_call_target="tpu_custom_call" | custom-call | tf_op jit(solution)/shard_map/chain/pallas_call | solution.py:469
  (116 shorter events, 56.4 us)
Async XLA Ops:
  2.7 35.5 %all-to-all-start = ((f32[16,8,2,16,128]{4,3,2,1,0:T(8,128)}), f32[16,8,2,16,128]{4,3,2,1,0:T(8,128)S(1)}, u32[]{:S(2)}, u32[]{:S(2)}) async-start(f32[16,8,2,16,128]{4,3,2,1,0:T(8,128)} %cut_rows.1), calls=%async_computation | async-start | bytes 4194304 | tf_op jit(solution)/shard_map/all_to_all | solution.py:277
  41.3 43.8 %collective-permute-start.2 = (f32[58,2,16,128]{3,2,1,0:T(8,128)S(1)}, f32[58,2,16,128]{3,2,1,0:T(8,128)S(1)}, u32[]{:S(2)}, u32[]{:S(2)}) collective-permute-start(f32[58,2,16,128]{3,2,1,0:T(8,128)S(1)} %pick_leaving.2), channel_id=1, source_target_pairs={{0,16},{1,17},{2,18},{3,19},{4,20},{5,21},{6,22},{7,23},{8,24},{9,... | collective-permute-start | bytes 2850824 | tf_op jit(solution)/shard_map/ppermute | solution.py:306
  90.0 185.5 %all-to-all-start.1 = ((f32[16,12,2,16,128]{4,3,2,1,0:T(8,128)}), f32[16,12,2,16,128]{4,3,2,1,0:T(8,128)S(1)}, u32[]{:S(2)}, u32[]{:S(2)}) async-start(f32[16,12,2,16,128]{4,3,2,1,0:T(8,128)} %bitcast.39), calls=%async_computation.1 | async-start | bytes 6291456 | tf_op jit(solution)/shard_map/all_to_all | solution.py:277
  98.5 44.5 %collective-permute-start.4 = (f32[8,2,16,128]{3,2,1,0:T(8,128)}, f32[8,2,16,128]{3,2,1,0:T(8,128)S(1)}, u32[]{:S(2)}, u32[]{:S(2)}) collective-permute-start(f32[8,2,16,128]{3,2,1,0:T(8,128)} %get-tuple-element.104), channel_id=1, source_target_pairs={{0,2},{1,3},{2,0},{3,1},{4,6},{5,7},{6,4},{7,5},{8,10},{9,11},{10,... | collective-permute-start | bytes 393224 | tf_op jit(solution)/shard_map/ppermute | solution.py:286
  100.1 44.6 %collective-permute-start.5 = (f32[8,2,16,128]{3,2,1,0:T(8,128)}, f32[8,2,16,128]{3,2,1,0:T(8,128)}, u32[]{:S(2)}, u32[]{:S(2)}) collective-permute-start(f32[8,2,16,128]{3,2,1,0:T(8,128)} %get-tuple-element.105), channel_id=1, source_target_pairs={{0,3},{1,2},{2,1},{3,0},{4,7},{5,6},{6,5},{7,4},{8,11},{9,10},{10,... | collective-permute-start | bytes 393224 | tf_op jit(solution)/shard_map/ppermute | solution.py:286
  100.1 46.3 %collective-permute-start.6 = (f32[8,2,16,128]{3,2,1,0:T(8,128)}, f32[8,2,16,128]{3,2,1,0:T(8,128)}, u32[]{:S(2)}, u32[]{:S(2)}) collective-permute-start(f32[8,2,16,128]{3,2,1,0:T(8,128)} %get-tuple-element.106), channel_id=1, source_target_pairs={{0,4},{1,5},{2,6},{3,7},{4,0},{5,1},{6,2},{7,3},{8,12},{9,13},{10,... | collective-permute-start | bytes 393224 | tf_op jit(solution)/shard_map/ppermute | solution.py:286
  101.8 45.5 %collective-permute-start.7 = (f32[8,2,16,128]{3,2,1,0:T(8,128)}, f32[8,2,16,128]{3,2,1,0:T(8,128)}, u32[]{:S(2)}, u32[]{:S(2)}) collective-permute-start(f32[8,2,16,128]{3,2,1,0:T(8,128)} %get-tuple-element.107), channel_id=1, source_target_pairs={{0,5},{1,4},{2,7},{3,6},{4,1},{5,0},{6,3},{7,2},{8,13},{9,12},{10,... | collective-permute-start | bytes 393224 | tf_op jit(solution)/shard_map/ppermute | solution.py:286
  102.0 45.4 %collective-permute-start.8 = (f32[8,2,16,128]{3,2,1,0:T(8,128)}, f32[8,2,16,128]{3,2,1,0:T(8,128)}, u32[]{:S(2)}, u32[]{:S(2)}) collective-permute-start(f32[8,2,16,128]{3,2,1,0:T(8,128)} %get-tuple-element.108), channel_id=1, source_target_pairs={{0,6},{1,7},{2,4},{3,5},{4,2},{5,3},{6,0},{7,1},{8,14},{9,15},{10,... | collective-permute-start | bytes 393224 | tf_op jit(solution)/shard_map/ppermute | solution.py:286
  142.9 6.2 %collective-permute-start.9 = (f32[8,2,16,128]{3,2,1,0:T(8,128)}, f32[8,2,16,128]{3,2,1,0:T(8,128)}, u32[]{:S(2)}, u32[]{:S(2)}) collective-permute-start(f32[8,2,16,128]{3,2,1,0:T(8,128)} %get-tuple-element.109), channel_id=1, source_target_pairs={{0,7},{1,6},{2,5},{3,4},{4,3},{5,2},{6,1},{7,0},{8,15},{9,14},{10,... | collective-permute-start | bytes 393224 | tf_op jit(solution)/shard_map/ppermute | solution.py:286
  144.7 8.2 %collective-permute-start.10 = (f32[8,2,16,128]{3,2,1,0:T(8,128)}, f32[8,2,16,128]{3,2,1,0:T(8,128)}, u32[]{:S(2)}, u32[]{:S(2)}) collective-permute-start(f32[8,2,16,128]{3,2,1,0:T(8,128)} %get-tuple-element.110), channel_id=1, source_target_pairs={{0,8},{1,9},{2,10},{3,11},{4,12},{5,13},{6,14},{7,15},{8,0},{9,1},... | collective-permute-start | bytes 393224 | tf_op jit(solution)/shard_map/ppermute | solution.py:286
  146.4 8.1 %collective-permute-start.11 = (f32[8,2,16,128]{3,2,1,0:T(8,128)}, f32[8,2,16,128]{3,2,1,0:T(8,128)}, u32[]{:S(2)}, u32[]{:S(2)}) collective-permute-start(f32[8,2,16,128]{3,2,1,0:T(8,128)} %get-tuple-element.111), channel_id=1, source_target_pairs={{0,9},{1,8},{2,11},{3,10},{4,13},{5,12},{6,15},{7,14},{8,1},{9,0},... | collective-permute-start | bytes 393224 | tf_op jit(solution)/shard_map/ppermute | solution.py:286
  147.3 9.7 %collective-permute-start.12 = (f32[8,2,16,128]{3,2,1,0:T(8,128)}, f32[8,2,16,128]{3,2,1,0:T(8,128)}, u32[]{:S(2)}, u32[]{:S(2)}) collective-permute-start(f32[8,2,16,128]{3,2,1,0:T(8,128)} %get-tuple-element.112), channel_id=1, source_target_pairs={{0,10},{1,11},{2,8},{3,9},{4,14},{5,15},{6,12},{7,13},{8,2},{9,3},... | collective-permute-start | bytes 393224 | tf_op jit(solution)/shard_map/ppermute | solution.py:286
  147.3 11.7 %collective-permute-start.13 = (f32[8,2,16,128]{3,2,1,0:T(8,128)}, f32[8,2,16,128]{3,2,1,0:T(8,128)}, u32[]{:S(2)}, u32[]{:S(2)}) collective-permute-start(f32[8,2,16,128]{3,2,1,0:T(8,128)} %get-tuple-element.113), channel_id=1, source_target_pairs={{0,11},{1,10},{2,9},{3,8},{4,15},{5,14},{6,13},{7,12},{8,3},{9,2},... | collective-permute-start | bytes 393224 | tf_op jit(solution)/shard_map/ppermute | solution.py:286
  149.1 12.7 %collective-permute-start.14 = (f32[8,2,16,128]{3,2,1,0:T(8,128)}, f32[8,2,16,128]{3,2,1,0:T(8,128)}, u32[]{:S(2)}, u32[]{:S(2)}) collective-permute-start(f32[8,2,16,128]{3,2,1,0:T(8,128)} %get-tuple-element.114), channel_id=1, source_target_pairs={{0,12},{1,13},{2,14},{3,15},{4,8},{5,9},{6,10},{7,11},{8,4},{9,5},... | collective-permute-start | bytes 393224 | tf_op jit(solution)/shard_map/ppermute | solution.py:286
  152.9 11.9 %collective-permute-start.15 = (f32[8,2,16,128]{3,2,1,0:T(8,128)}, f32[8,2,16,128]{3,2,1,0:T(8,128)}, u32[]{:S(2)}, u32[]{:S(2)}) collective-permute-start(f32[8,2,16,128]{3,2,1,0:T(8,128)} %get-tuple-element.115), channel_id=1, source_target_pairs={{0,13},{1,12},{2,15},{3,14},{4,9},{5,8},{6,11},{7,10},{8,5},{9,4},... | collective-permute-start | bytes 393224 | tf_op jit(solution)/shard_map/ppermute | solution.py:286
  154.5 13.3 %collective-permute-start.16 = (f32[8,2,16,128]{3,2,1,0:T(8,128)}, f32[8,2,16,128]{3,2,1,0:T(8,128)}, u32[]{:S(2)}, u32[]{:S(2)}) collective-permute-start(f32[8,2,16,128]{3,2,1,0:T(8,128)} %get-tuple-element.116), channel_id=1, source_target_pairs={{0,14},{1,15},{2,12},{3,13},{4,10},{5,11},{6,8},{7,9},{8,6},{9,7},... | collective-permute-start | bytes 393224 | tf_op jit(solution)/shard_map/ppermute | solution.py:286
  157.1 13.7 %collective-permute-start.17 = (f32[8,2,16,128]{3,2,1,0:T(8,128)}, f32[8,2,16,128]{3,2,1,0:T(8,128)}, u32[]{:S(2)}, u32[]{:S(2)}) collective-permute-start(f32[8,2,16,128]{3,2,1,0:T(8,128)} %get-tuple-element.117), channel_id=1, source_target_pairs={{0,15},{1,14},{2,13},{3,12},{4,11},{5,10},{6,9},{7,8},{8,7},{9,6},... | collective-permute-start | bytes 393224 | tf_op jit(solution)/shard_map/ppermute | solution.py:286
  173.5 44.8 %collective-permute-start.18 = (f32[58,2,16,128]{3,2,1,0:T(8,128)}, f32[58,2,16,128]{3,2,1,0:T(8,128)}, u32[]{:S(2)}, u32[]{:S(2)}) collective-permute-start(f32[58,2,16,128]{3,2,1,0:T(8,128)} %pick_leaving.3), channel_id=1, source_target_pairs={{0,16},{1,17},{2,18},{3,19},{4,20},{5,21},{6,22},{7,23},{8,24},{9,... | collective-permute-start | bytes 2850824 | tf_op jit(solution)/shard_map/ppermute | solution.py:306
  222.7 7.8 %collective-permute-start.20 = (f32[12,2,16,128]{3,2,1,0:T(8,128)S(1)}, f32[12,2,16,128]{3,2,1,0:T(8,128)S(1)}, u32[]{:S(2)}, u32[]{:S(2)}) collective-permute-start(f32[12,2,16,128]{3,2,1,0:T(8,128)S(1)} %get-tuple-element.120), channel_id=1, source_target_pairs={{0,2},{1,3},{2,0},{3,1},{4,6},{5,7},{6,4},{7,5},{8,10},{9,11},{10,... | collective-permute-start | bytes 589832 | tf_op jit(solution)/shard_map/ppermute | solution.py:286
  223.2 10.4 %collective-permute-start.21 = (f32[12,2,16,128]{3,2,1,0:T(8,128)S(1)}, f32[12,2,16,128]{3,2,1,0:T(8,128)S(1)}, u32[]{:S(2)}, u32[]{:S(2)}) collective-permute-start(f32[12,2,16,128]{3,2,1,0:T(8,128)S(1)} %get-tuple-element.121), channel_id=1, source_target_pairs={{0,3},{1,2},{2,1},{3,0},{4,7},{5,6},{6,5},{7,4},{8,11},{9,10},{10,... | collective-permute-start | bytes 589832 | tf_op jit(solution)/shard_map/ppermute | solution.py:286
  224.5 10.5 %collective-permute-start.22 = (f32[12,2,16,128]{3,2,1,0:T(8,128)S(1)}, f32[12,2,16,128]{3,2,1,0:T(8,128)S(1)}, u32[]{:S(2)}, u32[]{:S(2)}) collective-permute-start(f32[12,2,16,128]{3,2,1,0:T(8,128)S(1)} %get-tuple-element.122), channel_id=1, source_target_pairs={{0,4},{1,5},{2,6},{3,7},{4,0},{5,1},{6,2},{7,3},{8,12},{9,13},{10,... | collective-permute-start | bytes 589832 | tf_op jit(solution)/shard_map/ppermute | solution.py:286
  226.4 17.1 %collective-permute-start.23 = (f32[12,2,16,128]{3,2,1,0:T(8,128)S(1)}, f32[12,2,16,128]{3,2,1,0:T(8,128)S(1)}, u32[]{:S(2)}, u32[]{:S(2)}) collective-permute-start(f32[12,2,16,128]{3,2,1,0:T(8,128)S(1)} %get-tuple-element.123), channel_id=1, source_target_pairs={{0,5},{1,4},{2,7},{3,6},{4,1},{5,0},{6,3},{7,2},{8,13},{9,12},{10,... | collective-permute-start | bytes 589832 | tf_op jit(solution)/shard_map/ppermute | solution.py:286
  226.4 19.4 %collective-permute-start.24 = (f32[12,2,16,128]{3,2,1,0:T(8,128)S(1)}, f32[12,2,16,128]{3,2,1,0:T(8,128)S(1)}, u32[]{:S(2)}, u32[]{:S(2)}) collective-permute-start(f32[12,2,16,128]{3,2,1,0:T(8,128)S(1)} %get-tuple-element.124), channel_id=1, source_target_pairs={{0,6},{1,7},{2,4},{3,5},{4,2},{5,3},{6,0},{7,1},{8,14},{9,15},{10,... | collective-permute-start | bytes 589832 | tf_op jit(solution)/shard_map/ppermute | solution.py:286
  231.2 16.9 %collective-permute-start.25 = (f32[12,2,16,128]{3,2,1,0:T(8,128)S(1)}, f32[12,2,16,128]{3,2,1,0:T(8,128)S(1)}, u32[]{:S(2)}, u32[]{:S(2)}) collective-permute-start(f32[12,2,16,128]{3,2,1,0:T(8,128)S(1)} %get-tuple-element.125), channel_id=1, source_target_pairs={{0,7},{1,6},{2,5},{3,4},{4,3},{5,2},{6,1},{7,0},{8,15},{9,14},{10,... | collective-permute-start | bytes 589832 | tf_op jit(solution)/shard_map/ppermute | solution.py:286
  234.3 16.3 %collective-permute-start.26 = (f32[12,2,16,128]{3,2,1,0:T(8,128)S(1)}, f32[12,2,16,128]{3,2,1,0:T(8,128)S(1)}, u32[]{:S(2)}, u32[]{:S(2)}) collective-permute-start(f32[12,2,16,128]{3,2,1,0:T(8,128)S(1)} %get-tuple-element.126), channel_id=1, source_target_pairs={{0,8},{1,9},{2,10},{3,11},{4,12},{5,13},{6,14},{7,15},{8,0},{9,1},... | collective-permute-start | bytes 589832 | tf_op jit(solution)/shard_map/ppermute | solution.py:286
  235.7 15.8 %collective-permute-start.27 = (f32[12,2,16,128]{3,2,1,0:T(8,128)S(1)}, f32[12,2,16,128]{3,2,1,0:T(8,128)S(1)}, u32[]{:S(2)}, u32[]{:S(2)}) collective-permute-start(f32[12,2,16,128]{3,2,1,0:T(8,128)S(1)} %get-tuple-element.127), channel_id=1, source_target_pairs={{0,9},{1,8},{2,11},{3,10},{4,13},{5,12},{6,15},{7,14},{8,1},{9,0},... | collective-permute-start | bytes 589832 | tf_op jit(solution)/shard_map/ppermute | solution.py:286
  244.2 10.5 %collective-permute-start.28 = (f32[12,2,16,128]{3,2,1,0:T(8,128)S(1)}, f32[12,2,16,128]{3,2,1,0:T(8,128)S(1)}, u32[]{:S(2)}, u32[]{:S(2)}) collective-permute-start(f32[12,2,16,128]{3,2,1,0:T(8,128)S(1)} %get-tuple-element.128), channel_id=1, source_target_pairs={{0,10},{1,11},{2,8},{3,9},{4,14},{5,15},{6,12},{7,13},{8,2},{9,3},... | collective-permute-start | bytes 589832 | tf_op jit(solution)/shard_map/ppermute | solution.py:286
  246.5 12.1 %collective-permute-start.29 = (f32[12,2,16,128]{3,2,1,0:T(8,128)}, f32[12,2,16,128]{3,2,1,0:T(8,128)}, u32[]{:S(2)}, u32[]{:S(2)}) collective-permute-start(f32[12,2,16,128]{3,2,1,0:T(8,128)} %get-tuple-element.129), channel_id=1, source_target_pairs={{0,11},{1,10},{2,9},{3,8},{4,15},{5,14},{6,13},{7,12},{8,3},{9,2},... | collective-permute-start | bytes 589832 | tf_op jit(solution)/shard_map/ppermute | solution.py:286
  248.7 14.5 %collective-permute-start.30 = (f32[12,2,16,128]{3,2,1,0:T(8,128)}, f32[12,2,16,128]{3,2,1,0:T(8,128)}, u32[]{:S(2)}, u32[]{:S(2)}) collective-permute-start(f32[12,2,16,128]{3,2,1,0:T(8,128)} %get-tuple-element.130), channel_id=1, source_target_pairs={{0,12},{1,13},{2,14},{3,15},{4,8},{5,9},{6,10},{7,11},{8,4},{9,5},... | collective-permute-start | bytes 589832 | tf_op jit(solution)/shard_map/ppermute | solution.py:286
  251.3 15.9 %collective-permute-start.31 = (f32[12,2,16,128]{3,2,1,0:T(8,128)}, f32[12,2,16,128]{3,2,1,0:T(8,128)}, u32[]{:S(2)}, u32[]{:S(2)}) collective-permute-start(f32[12,2,16,128]{3,2,1,0:T(8,128)} %get-tuple-element.131), channel_id=1, source_target_pairs={{0,13},{1,12},{2,15},{3,14},{4,9},{5,8},{6,11},{7,10},{8,5},{9,4},... | collective-permute-start | bytes 589832 | tf_op jit(solution)/shard_map/ppermute | solution.py:286
  252.2 19.2 %collective-permute-start.32 = (f32[12,2,16,128]{3,2,1,0:T(8,128)}, f32[12,2,16,128]{3,2,1,0:T(8,128)}, u32[]{:S(2)}, u32[]{:S(2)}) collective-permute-start(f32[12,2,16,128]{3,2,1,0:T(8,128)} %get-tuple-element.132), channel_id=1, source_target_pairs={{0,14},{1,15},{2,12},{3,13},{4,10},{5,11},{6,8},{7,9},{8,6},{9,7},... | collective-permute-start | bytes 589832 | tf_op jit(solution)/shard_map/ppermute | solution.py:286
  255.4 20.2 %collective-permute-start.33 = (f32[12,2,16,128]{3,2,1,0:T(8,128)}, f32[12,2,16,128]{3,2,1,0:T(8,128)}, u32[]{:S(2)}, u32[]{:S(2)}) collective-permute-start(f32[12,2,16,128]{3,2,1,0:T(8,128)} %get-tuple-element.133), channel_id=1, source_target_pairs={{0,15},{1,14},{2,13},{3,12},{4,11},{5,10},{6,9},{7,8},{8,7},{9,6},... | collective-permute-start | bytes 589832 | tf_op jit(solution)/shard_map/ppermute | solution.py:286
  (27 other events, 159.4 us)
